TPU v7x, 256 devices: a whole 4x4x8 slice. The times are simulated.
256 devices in a mesh: ta: 4 (over x), sa: 64 (over y, z, core).
Axes of the slice: x: 4, y: 4, z: 8, core: 2. Of those that a mesh axis runs over, the one named last changes fastest.
Arguments:
- snapshots: float32 [256, 2, 262144], P('ta', None, 'sa'), may hold values from -6 to 6
- bins: int32 [16], replicated, may hold values from 0 to 127, as said below
- eigenvalues: float32 [16, 32], P('ta'), may hold values from 100 to 1000
- old_basis: bfloat16 [16, 2, 32, 2, 262144], P('ta', None, None, None, 'sa'), may hold values from -0.0055242717 to 0.0055242717, as said below
- block_count: int32 [1], replicated, may hold values from 1 to 8
Outputs:
- new_basis: bfloat16 [16, 2, 32, 2, 262144], P('ta', None, None, None, 'sa')
- coherence: float32 [16, 2, 32, 32], P('ta')
Inputs may be any that keep to these rules, and one draw needn't show every extreme that they name: The 16 bins are distinct; 0 and 127 are always among them. `old_basis`: every entry lies within 4 / sqrt(524288) in magnitude.
All inputs are finite; a program needn't handle non-finite values.
Results may differ from a plain program's by a relative error of at most 0.001.
Values sent between devices are 32-bit elements; how exact they have to be, the bound alone decides.
No kernel may reach another device: no remote copies, remote signals or barrier semaphores. Data moves between devices by JAX's collectives and lax.ppermute only.
A program may use at most 128 MiB of HBM per device.

v0:
```python
import math

import jax
import jax.numpy as jnp
from jax import lax
from jax.sharding import PartitionSpec as P


def tables(bins, times, total):
    phase = bins[:, None] * times[None, :] % total
    angle = 2.0 * math.pi / total * phase.astype(jnp.float32)
    window = 0.5 - 0.5 * jnp.cos(2.0 * math.pi / total * times.astype(jnp.float32))
    scale = math.sqrt(8.0 / (3.0 * total))
    return (jnp.cos(angle) * window[None, :] * scale, -jnp.sin(angle) * window[None, :] * scale)


def pair_dot(left, right, form):
    return jnp.einsum(form, left, right, precision=lax.Precision.HIGHEST)


def local(snapshots, bins, eigenvalues, old_basis, block_count):
    hi = lax.Precision.HIGHEST
    slice_len = snapshots.shape[0]
    points = snapshots.shape[2]
    groups = lax.axis_size("ta")
    total = slice_len * groups
    times = lax.axis_index("ta") * slice_len + jnp.arange(slice_len, dtype=jnp.int32)
    c_tab, s_tab = tables(bins, times, total)
    flat = snapshots.reshape(slice_len, 2 * points)
    terms = jnp.stack(
        [jnp.dot(c_tab, flat, precision=hi), jnp.dot(s_tab, flat, precision=hi)], axis=1
    )
    spec = lax.psum_scatter(terms, "ta", scatter_dimension=0, tiled=True)
    local_bins = spec.shape[0]
    rank = old_basis.shape[2]
    basis = old_basis.reshape(local_bins, 2, rank, 2 * points).astype(jnp.float32)
    u_re = basis[:, 0]
    u_im = basis[:, 1]
    s_re = spec[:, 0]
    s_im = spec[:, 1]
    c_re = pair_dot(u_re, s_re, "bjm,bm->bj") + pair_dot(u_im, s_im, "bjm,bm->bj")
    c_im = pair_dot(u_re, s_im, "bjm,bm->bj") - pair_dot(u_im, s_re, "bjm,bm->bj")
    count = block_count[0].astype(jnp.float32)
    w_old = count / (count + 1.0)
    w_new = 1.0 / (count + 1.0)
    scaled = w_old * eigenvalues
    c_re, c_im = lax.psum((c_re, c_im), "sa")
    g_re = scaled[:, :, None] * u_re + w_new * (
        c_re[:, :, None] * s_re[:, None, :] + c_im[:, :, None] * s_im[:, None, :]
    )
    g_im = scaled[:, :, None] * u_im + w_new * (
        c_re[:, :, None] * s_im[:, None, :] - c_im[:, :, None] * s_re[:, None, :]
    )
    part_re = pair_dot(g_re, g_re, "bjm,bkm->bjk") + pair_dot(g_im, g_im, "bjm,bkm->bjk")
    part_im = pair_dot(g_re, g_im, "bjm,bkm->bjk") - pair_dot(g_im, g_re, "bjm,bkm->bjk")
    gram_re, gram_im = lax.psum((part_re, part_im), "sa")
    inv = 1.0 / jnp.sqrt(jnp.diagonal(gram_re, axis1=1, axis2=2) + 1e-06)
    fresh = jnp.stack([g_re * inv[:, :, None], g_im * inv[:, :, None]], axis=1).astype(jnp.bfloat16)
    outer = inv[:, :, None] * inv[:, None, :]
    coherence = jnp.stack([gram_re * outer, gram_im * outer], axis=1)
    return (fresh.reshape(old_basis.shape), coherence)


def solution(mesh):
    return jax.shard_map(
        local,
        mesh=mesh,
        in_specs=(P("ta", None, "sa"), P(), P("ta", None), P("ta", None, None, None, "sa"), P()),
        out_specs=(P("ta", None, None, None, "sa"), P("ta", None, None, None)),
        check_vma=False,
    )
```

profile of v0, /device:TPU:1, one launch (start us, length us, event | category | flops | bytes accessed | tf_op | source)
XLA Modules:
  0.0 522.2 jit_solution(14996345941327891724)
XLA Ops:
  7.2 0.0 copy-start.2
  7.2 0.0 all-reduce.5.cloned.1.call-start
  7.3 2.8 copy.27
  10.1 0.0 copy-done.2
  10.1 1.2 convolution_bitcast_fusion
  11.3 1.2 convolution_bitcast_fusion.1
  12.5 1.0 pad_maximum_fusion.1
  13.5 0.0 all-reduce.5.cloned.1.call-update
  13.5 7.8 %reshape.63 = bf16[4,2,32,8192]{3,2,1,0:T(8,128)(2,1)} reshape(bf16[4,2,32,2,4096]{4,3,2,1,0:T(2,128)(2,1)} %param.8) | data formatting | bytes 8388608 | tf_op jit(solution)/shard_map/reshape | solution.py:36
  21.3 0.0 copy-start.3
  21.3 0.0 copy-start.1
  21.3 6.4 %copy_convert_fusion = f32[4,2,32,8192]{3,2,0,1:T(8,128)} fusion(bf16[4,2,32,8192]{3,2,1,0:T(8,128)(2,1)} %reshape.63), kind=kLoop, calls=%fused_computation.8 | loop fusion | flops 2097152 | bytes 12582912 | tf_op jit(solution)/shard_map/convert_element_type | solution.py:36
  28.5 0.0 copy-done.3
  28.5 0.6 dynamic-slice
  29.8 0.0 copy-done.1
  29.8 37.2 %all-reduce.5.cloned.1.call-done = f32[16,2,8192]{2,0,1:T(8,128)} async-done(((f32[16,2,8192]{2,0,1:T(8,128)}), f32[16,2,8192]{2,0,1:T(8,128)}) %all-reduce.5.cloned.1.call-update) | async-done | bytes 1048592
  67.0 0.0 copy-start
  67.0 1.3 dynamic-slice_bitcast_fusion.1
  68.2 3.5 fusion.4
  71.7 3.3 fusion.3
  75.0 0.0 copy-done
  75.1 1.7 fusion.2
  76.8 1.7 fusion.5
  78.5 126.3 %all-reduce.2 = (f32[4,32]{1,0:T(4,128)S(1)}, f32[4,32]{1,0:T(4,128)S(1)}) all-reduce(f32[4,32]{1,0:T(4,128)S(1)} %sub.26, f32[4,32]{1,0:T(4,128)S(1)} %add.85), channel_id=1, replica_groups=mesh['ta'=4,'sa'=64] {'sa'}, use_global_device_ids=true, to_apply=%region_2.3 | all-reduce | flops 256 | bytes 2048 | tf_op jit(solution)/shard_map/psum | solution.py:47
  204.8 0.0 slice-start
  204.8 9.2 %fusion.9 = f32[4,32,32]{2,1,0:T(8,128)S(1)} fusion(f32[4,2,32,8192]{3,2,0,1:T(8,128)} %copy_convert_fusion, f32[4,8192]{1,0:T(4,128)S(1)} %get-tuple-element.15, f32[4,32]{1,0:T(4,128)S(1)} %get-tuple-element.8, f32[4,8192]{1,0:T(4,128)S(1)} %get-tuple-element.12, f32[4,32]{1,0:T(4,128)S(1)} %get-tuple-element.9, f32[]{:T(128)S(6)} %div.9, ...), kind=kOutput, calls=%fused_computation.21 | convolution fusion | flops 408944640 | bytes 4474372 | tf_op jit(solution)/shard_map/bjm,bkm->bjk/dot_general | solution.py:18
  214.0 0.0 slice-start.1
  214.0 9.2 %fusion.7 = f32[4,32,32]{2,1,0:T(8,128)S(1)} fusion(f32[4,2,32,8192]{3,2,0,1:T(8,128)} %copy_convert_fusion, f32[4,8192]{1,0:T(4,128)S(1)} %get-tuple-element.15, f32[4,32]{1,0:T(4,128)S(1)} %get-tuple-element.8, f32[4,8192]{1,0:T(4,128)S(1)} %get-tuple-element.12, f32[4,32]{1,0:T(4,128)S(1)} %get-tuple-element.9, f32[]{:T(128)S(6)} %div.9, ...), kind=kOutput, calls=%fused_computation.20 | convolution fusion | flops 415236096 | bytes 8942592 | tf_op jit(solution)/shard_map/bjm,bkm->bjk/dot_general | solution.py:18
  223.3 0.0 slice-done
  223.3 0.0 slice-done.1
  223.3 16.7 %convolution_add_fusion = f32[4,32,32]{2,1,0:T(8,128)S(1)} fusion(f32[4,32,32]{2,1,0:T(8,128)S(1)} %fusion.9, f32[4,2,32,8192]{3,2,0,1:T(8,128)S(1)} %bitcast.65, f32[4,8192]{1,0:T(4,128)S(1)} %get-tuple-element.15, f32[4,32]{1,0:T(4,128)S(1)} %get-tuple-element.8, f32[4,8192]{1,0:T(4,128)S(1)} %get-tuple-element.12, f32[4,32]{1,0:T(4,128)S(1)} %get-tuple-element.9, ...), kind=kOutput, calls=%fused_computation.18 | convolution fusion | flops 408948736 | bytes 4544516 | tf_op jit(solution)/shard_map/bjm,bkm->bjk/dot_general | solution.py:18
  240.0 6.0 %convolution_subtract_fusion = f32[4,32,32]{2,1,0:T(8,128)S(1)} fusion(f32[4,32,32]{2,1,0:T(8,128)S(1)} %fusion.7, f32[4,2,32,8192]{3,2,0,1:T(8,128)S(1)} %bitcast.65, f32[4,8192]{1,0:T(4,128)S(1)} %get-tuple-element.15, f32[4,32]{1,0:T(4,128)S(1)} %get-tuple-element.8, f32[4,8192]{1,0:T(4,128)S(1)} %get-tuple-element.12, ...), kind=kOutput, calls=%fused_computation.17 | convolution fusion | flops 415240192 | bytes 9008128 | tf_op jit(solution)/shard_map/bjm,bkm->bjk/dot_general | solution.py:18
  246.0 244.2 %all-reduce.1 = (f32[4,32,32]{2,1,0:T(8,128)S(1)}, f32[4,32,32]{2,1,0:T(8,128)S(1)}) all-reduce(f32[4,32,32]{2,1,0:T(8,128)S(1)} %convolution_add_fusion, f32[4,32,32]{2,1,0:T(8,128)S(1)} %convolution_subtract_fusion), channel_id=1, replica_groups=mesh['ta'=4,'sa'=64] {'sa'}, use_global_device_ids=true, to_apply=%region_3.4 | all-reduce | flops 8192 | bytes 65536 | tf_op jit(solution)/shard_map/psum | solution.py:56
  490.2 0.3 copy.14
  490.5 0.7 gather_fusion
  491.2 0.1 copy.15
  491.3 5.5 %multiply_convert_fusion.1 = (bf16[4,1,32,8192]{3,2,0,1:T(8,128)(2,1)}, bf16[4,1,32,8192]{3,2,0,1:T(8,128)(2,1)S(1)}) fusion(f32[4,2,32,8192]{3,2,0,1:T(8,128)} %copy_convert_fusion, f32[4,32]{1,0:T(4,128)S(1)} %copy.15, f32[4,8192]{1,0:T(4,128)S(1)} %get-tuple-element.15, f32[4,32]{1,0:T(4,128)S(1)} %get-tuple-element.8, ...), kind=kLoop, calls=%fused_computation.10 | loop fusion | flops 16777216 | bytes 12847108 | tf_op jit(solution)/shard_map/convert.3
  496.8 0.1 fusion.18
  496.9 0.7 copy.18
  497.6 4.5 stack.30
  502.0 2.7 stack.31
  504.8 10.4 %pad_maximum_fusion = bf16[4,2,32,2,4096]{4,3,2,1,0:T(2,128)(2,1)} fusion(bf16[4,1,32,2,4096]{4,3,2,1,0:T(2,128)(2,1)} %stack.31, bf16[4,1,32,2,4096]{4,3,2,1,0:T(2,128)(2,1)} %stack.30), kind=kLoop, calls=%fused_computation.3 | loop fusion | flops 2097152 | bytes 8388608 | tf_op jit(solution)/shard_map/stack | solution.py:58
  (9 shorter events, 0.1 us)
Async XLA Ops:
  7.2 2.9 copy-start.2
  7.2 59.8 %all-reduce.5.cloned.1.call-start = ((), (), s32[]{:S(2)}) async-start(), calls=%async_computation | async-start | bytes 2097152
  21.3 7.2 %copy-start.3 = (u32[256]{0:T(256)S(1)}, u32[256]{0:T(256)}, u32[]{:S(2)}) copy-start(u32[256]{0:T(256)} %constant.55) | copy-start | bytes 3076
  21.3 8.5 %copy-start.1 = (f32[4,32]{1,0:T(4,128)S(1)}, f32[4,32]{1,0:T(4,128)}, u32[]{:S(2)}) copy-start(f32[4,32]{1,0:T(4,128)} %param.7) | copy-start | bytes 1540
  67.0 8.1 %copy-start = (bf16[4,2,32,8192]{3,2,1,0:T(8,128)(2,1)S(1)}, bf16[4,2,32,8192]{3,2,1,0:T(8,128)(2,1)}, u32[]{:S(2)}) copy-start(bf16[4,2,32,8192]{3,2,1,0:T(8,128)(2,1)} %reshape.63) | copy-start | bytes 12582916
  204.8 18.5 %slice-start = ((s8[8388608]{0:T(1024)(128)(4,1)}), s8[4194304]{0:T(1024)(128)(4,1)S(1)}, s32[]{:S(2)}) async-start(s8[8388608]{0:T(1024)(128)(4,1)} %bitcast.64), calls=%async_computation.1 | async-start | bytes 8388608
  214.0 9.3 %slice-start.1 = ((s8[8388608]{0:T(1024)(128)(4,1)}), s8[4194304]{0:T(1024)(128)(4,1)S(1)}, s32[]{:S(2)}) async-start(s8[8388608]{0:T(1024)(128)(4,1)} %bitcast.64), calls=%async_computation.2 | async-start | bytes 8388608
Sparse Core Ops, SparseCore 0:
  13.6 53.2 all-reduce.4
where the time goes:
time: 528 us; the launch traced here: 522 us
  blocking collectives  370 us (70%)
  matrix products  53.8 us (10%)
  waiting for transfers between devices  37.2 us (7%)
  other arithmetic  23.6 us (4%)
  local copies, waits for them, and re-layouts  21.4 us (4%)
  between operations  15.8 us (3%)
    psum x1, blocking collectives, local(): gram_re, gram_im = lax.psum((part_re, part_im), 'sa')  244 us
    psum x1, blocking collectives, local(): c_re, c_im = lax.psum((c_re, c_im), 'sa')  126 us
    dot_general x8, matrix products, pair_dot(): return jnp.einsum(form, left, right, precision=lax.Precision.HIGHEST)  51.4 us
    unnamed x2, waiting for transfers between devices  37.2 us
  transfers between devices with their start and end apart: 1, of which 1 were waited for; matrix products, arithmetic and copies ran while one was open for 3% of the time, Pallas kernels for 0%

commit v1 on v0

v1 whole, which is shorter than its diff:
```python
import math

import jax
import jax.numpy as jnp
from jax import lax
from jax.experimental import pallas as pl
from jax.experimental.pallas import tpu as pltpu
from jax.sharding import Mesh, PartitionSpec as P

SPACE = ("y", "z", "core")
HI = lax.Precision.HIGHEST
LANES = 128


def fold(v, axis):
    shape = v.shape
    lead, tiles = shape[:-2], shape[-1] // LANES
    v = v.reshape(*lead, 2, tiles, LANES)
    return jnp.swapaxes(v, axis, axis + 1).reshape(*lead, 2 * tiles, LANES)


def unfold(v, axis):
    lead, rows = v.shape[:-2], v.shape[-2]
    v = v.reshape(*lead, rows // 2, 2, LANES)
    return jnp.swapaxes(v, axis, axis + 1).reshape(*lead, 2, rows // 2 * LANES)


def transform_kernel(total, slice_len, rows, bins_ref, place_ref, x_ref, out_ref):
    n = 2 * bins_ref.shape[0]
    row = lax.broadcasted_iota(jnp.int32, (n, slice_len), 0)
    t = lax.broadcasted_iota(jnp.int32, (n, slice_len), 1) + place_ref[0] * slice_len
    which = jnp.zeros((n, slice_len), jnp.int32)
    for b in range(n // 2):
        which = jnp.where(row // 2 == b, bins_ref[b], which)
    phase = (which * t + (row % 2) * (total // 4)) % total
    step = 2.0 * math.pi / total
    window = 0.5 - 0.5 * jnp.cos(step * t.astype(jnp.float32))
    table = jnp.cos(step * phase.astype(jnp.float32)) * window * math.sqrt(8.0 / (3.0 * total))
    t_hi = table.astype(jnp.bfloat16)
    t_lo = (table - t_hi.astype(jnp.float32)).astype(jnp.bfloat16)
    left = jnp.concatenate([t_hi, t_lo], axis=0)
    left = jnp.concatenate([left, left], axis=1)
    for r in range(0, rows, 2):
        x = jnp.concatenate(
            [x_ref[pl.ds(r, slice_len, stride=rows), :], x_ref[pl.ds(r + 1, slice_len, stride=rows), :]],
            axis=1,
        )
        hi = x.astype(jnp.bfloat16)
        lo = (x - hi.astype(jnp.float32)).astype(jnp.bfloat16)
        res = jnp.dot(left, jnp.concatenate([hi, lo], axis=0), preferred_element_type=jnp.float32)
        res = res[:n] + res[n:]
        out_ref[pl.ds(r, n, stride=rows), :] = res[:, :LANES]
        out_ref[pl.ds(r + 1, n, stride=rows), :] = res[:, LANES:]


def project_kernel(nb, rank, parts_ref, u_ref, h_ref, s_ref, blk_ref, acc_ref):
    b = pl.program_id(0)
    rows = u_ref.shape[-2]

    @pl.when(b == 0)
    def _():
        acc_ref[...] = jnp.zeros_like(acc_ref)

    s = parts_ref[0, 0]
    for k in range(1, parts_ref.shape[0]):
        s = s + parts_ref[k, 0]
    s_ref[0] = s
    s_re, s_im = s[0], s[1]

    def eight(v):
        return v.reshape(rows // 8, 8, LANES).sum(axis=0)

    acc_ref[pl.ds((2 * nb * rank + b) * 8, 8), :] = eight(s_re * s_re + s_im * s_im)

    def body(j, carry):
        u_re = u_ref[0, 0, j].astype(jnp.float32)
        u_im = u_ref[0, 1, j].astype(jnp.float32)
        at = (b * 2 * rank + j) * 8
        acc_ref[pl.ds(pl.multiple_of(at, 8), 8), :] = eight(u_re * s_re + u_im * s_im)
        acc_ref[pl.ds(pl.multiple_of(at + rank * 8, 8), 8), :] = eight(u_re * s_im - u_im * s_re)
        return carry

    lax.fori_loop(0, rank, body, 0, unroll=4)

    @pl.when(b == nb - 1)
    def _():
        n = acc_ref.shape[0] // 8
        x = acc_ref[pl.ds(0, n, stride=8), :]
        for k in range(1, 8):
            x = x + acc_ref[pl.ds(k, n, stride=8), :]
        sums = lax.dot_general(
            jnp.ones((8, LANES), jnp.float32), x, (((1,), (1,)), ((), ())),
            precision=HI, preferred_element_type=jnp.float32,
        )
        blk = jnp.concatenate(
            [sums[0:1, k * LANES:(k + 1) * LANES] for k in range(3)] + [h_ref[...]], axis=0
        )
        blk_ref[...] = jnp.broadcast_to(blk[None], blk_ref.shape)


def update_kernel(nb, rank, count_ref, g_ref, eig_ref, s_ref, u_ref, out_ref, coh_ref, coef_ref):
    b, half = pl.program_id(0), pl.program_id(1)
    rows = u_ref.shape[-2]
    n_from = g_ref.shape[0] // 4

    @pl.when((b == 0) & (half == 0))
    def _():
        count = jnp.full((1, 1), count_ref[0], jnp.int32).astype(jnp.float32)
        w_old = count / (count + 1.0)
        w_new = 1.0 / (count + 1.0)
        sums = [g_ref[pl.ds(k, n_from, stride=4), :].sum(axis=0, keepdims=True) for k in range(3)]
        h = g_ref[pl.ds(3, n_from, stride=4), :]
        eye = lax.broadcasted_iota(jnp.int32, (rank, rank), 0) == lax.broadcasted_iota(jnp.int32, (rank, rank), 1)

        def col(v):
            return jnp.where(eye, v, 0.0).sum(axis=1, keepdims=True)

        for i in range(nb):
            at = (i % 2) * 2 * rank
            cr = sums[i // 2][:, at:at + rank]
            ci = sums[i // 2][:, at + rank:at + 2 * rank]
            power = sums[2][:, i:i + 1]
            a = w_old * eig_ref[i:i + 1, :]
            cr_c, ci_c, a_c = col(cr), col(ci), col(a)
            h_re = h[:rank, i * rank:(i + 1) * rank]
            h_im = h[rank:2 * rank, i * rank:(i + 1) * rank]
            both = w_new * (a_c + a + w_new * power)
            gram_re = a_c * a * h_re + (cr_c * cr + ci_c * ci) * both
            gram_im = a_c * a * h_im + (ci_c * cr - cr_c * ci) * both
            diag = jnp.where(eye, gram_re, 0.0)
            inv_c = 1.0 / jnp.sqrt(diag.sum(axis=1, keepdims=True) + 1e-06)
            inv_r = 1.0 / jnp.sqrt(diag.sum(axis=0, keepdims=True) + 1e-06)
            coh_ref[i, 0] = gram_re * inv_c * inv_r
            coh_ref[i, 1] = gram_im * inv_c * inv_r
            for k, v in enumerate((a_c * inv_c, w_new * cr_c * inv_c, w_new * ci_c * inv_c)):
                coef_ref[pl.ds((k * nb + i) * rank, rank), :] = jnp.broadcast_to(v, (rank, LANES))

    s_re, s_im = s_ref[0, 0], s_ref[0, 1]
    block = u_ref.shape[2]

    def body(j, carry):
        at = b * rank + half * block + j

        def coef(k):
            one = coef_ref[pl.ds(k * nb * rank + at, 1), :]
            return jnp.broadcast_to(one, (rows, LANES))

        alpha, beta, gamma = coef(0), coef(1), coef(2)
        u_re = u_ref[0, 0, j].astype(jnp.float32)
        u_im = u_ref[0, 1, j].astype(jnp.float32)
        out_ref[0, 0, j] = (alpha * u_re + (beta * s_re + gamma * s_im)).astype(out_ref.dtype)
        out_ref[0, 1, j] = (alpha * u_im + (beta * s_im - gamma * s_re)).astype(out_ref.dtype)
        return carry

    lax.fori_loop(0, block, body, 0, unroll=4)


def local(snapshots, bins, eigenvalues, old_basis, block_count):
    slice_len, _, points = snapshots.shape
    groups = lax.axis_size("ta")
    total = slice_len * groups
    rows = 2 * points // LANES
    nb, _, rank = old_basis.shape[:3]
    n_space = lax.axis_size(SPACE)
    place = lax.axis_index("ta").astype(jnp.int32).reshape(1)
    smem = pl.BlockSpec(memory_space=pltpu.SMEM)
    vmem = pl.BlockSpec(memory_space=pltpu.VMEM)

    x = fold(snapshots, 1).reshape(slice_len * rows, LANES)
    n = 2 * bins.shape[0]
    terms = pl.pallas_call(
        lambda *refs: transform_kernel(total, slice_len, rows, *refs),
        out_shape=jax.ShapeDtypeStruct((n * rows, LANES), jnp.float32),
        in_specs=[smem, smem, vmem],
        out_specs=vmem,
        name="transform",
    )(bins, place, x)
    parts = lax.all_to_all(terms.reshape(groups, n // groups * rows, LANES), "ta", 0, 0, tiled=True)
    parts = parts.reshape(groups, nb, 2, rows, LANES)

    u = fold(old_basis, 3)
    v = old_basis.reshape(nb, 2 * rank, 2 * points)
    vv = jnp.einsum("bjm,bkm->bjk", v, v, preferred_element_type=jnp.float32)
    h_re = vv[:, :rank, :rank] + vv[:, rank:, rank:]
    h_im = vv[:, :rank, rank:] - vv[:, rank:, :rank]
    h = jnp.concatenate([h_re, h_im], axis=1).transpose(1, 0, 2).reshape(2 * rank, 1, nb * rank)
    h = lax.all_to_all(h, SPACE, 0, 0, tiled=True).sum(axis=0)

    spec, blk = pl.pallas_call(
        lambda *refs: project_kernel(nb, rank, *refs),
        grid=(nb,),
        out_shape=(
            jax.ShapeDtypeStruct((nb, 2, rows, LANES), jnp.float32),
            jax.ShapeDtypeStruct((n_space, 4, LANES), jnp.float32),
        ),
        in_specs=[
            pl.BlockSpec((groups, 1, 2, rows, LANES), lambda b: (0, b, 0, 0, 0)),
            pl.BlockSpec((1, 2, rank, rows, LANES), lambda b: (b, 0, 0, 0, 0)),
            pl.BlockSpec((1, LANES), lambda b: (0, 0)),
        ],
        out_specs=(
            pl.BlockSpec((1, 2, rows, LANES), lambda b: (b, 0, 0, 0)),
            pl.BlockSpec((n_space, 4, LANES), lambda b: (0, 0, 0)),
        ),
        scratch_shapes=[pltpu.VMEM((3 * LANES * 8, LANES), jnp.float32)],
        name="project",
    )(parts, u, h)
    g = lax.all_to_all(blk, SPACE, 0, 0, tiled=True).reshape(n_space * 4, LANES)

    block = rank // 2
    fresh, coherence = pl.pallas_call(
        lambda *refs: update_kernel(nb, rank, *refs),
        grid=(nb, rank // block),
        out_shape=(
            jax.ShapeDtypeStruct(u.shape, jnp.bfloat16),
            jax.ShapeDtypeStruct((nb, 2, rank, rank), jnp.float32),
        ),
        in_specs=[
            smem,
            pl.BlockSpec((n_space * 4, LANES), lambda b, i: (0, 0)),
            pl.BlockSpec((nb, rank), lambda b, i: (0, 0)),
            pl.BlockSpec((1, 2, rows, LANES), lambda b, i: (b, 0, 0, 0)),
            pl.BlockSpec((1, 2, block, rows, LANES), lambda b, i: (b, 0, i, 0, 0)),
        ],
        out_specs=(
            pl.BlockSpec((1, 2, block, rows, LANES), lambda b, i: (b, 0, i, 0, 0)),
            pl.BlockSpec((nb, 2, rank, rank), lambda b, i: (0, 0, 0, 0)),
        ),
        scratch_shapes=[pltpu.VMEM((3 * nb * rank, LANES), jnp.float32)],
        name="update",
    )(block_count, g, eigenvalues, spec, u)
    return unfold(fresh, 3), coherence


def solution(mesh):
    inner = Mesh(mesh.devices.reshape(4, 4, 8, 2), ("ta",) + SPACE)
    return jax.shard_map(
        local,
        mesh=inner,
        in_specs=(P("ta", None, SPACE), P(), P("ta", None), P("ta", None, None, None, SPACE), P()),
        out_specs=(P("ta", None, None, None, SPACE), P("ta", None, None, None)),
        check_vma=False,
    )
```

time: 528 us -> 88.1 us (0.17)
  blocking collectives: 370 us -> 0 us
  matrix products: 53.8 us -> 4.69 us
  starting transfers between devices: 0.04 us -> 24.3 us
  other arithmetic: 23.6 us -> 0.78 us
  Pallas kernels: 0 us -> 18.2 us
  between operations: 15.8 us -> 1.33 us
  local copies, waits for them, and re-layouts: 21.4 us -> 10.1 us
  waiting for transfers between devices: 37.2 us -> 28 us
    psum x2 -> x0, blocking collectives: 370 us -> none  [the longest x1 244 us: local(): gram_re, gram_im = lax.psum((part_re, part_im), 'sa')]
    dot_general x10 -> x1, matrix products: 53.8 us -> 4.69 us  [local(): vv = jnp.einsum('bjm,bkm->bjk', v, v, preferred_element_type=jnp.float32)]
    unnamed x2 -> x0, waiting for transfers between devices: 37.2 us -> none
    all_to_all x0 -> x3, waiting for transfers between devices: none -> 28 us  [the longest x1 13.6 us: local(): lax.all_to_all(terms.reshape(groups, n // groups * rows, LANES), 'ta', 0,...]
    all_to_all x0 -> x3, starting transfers between devices: none -> 24.3 us  [the longest x1 13.2 us: local(): h = lax.all_to_all(h, SPACE, 0, 0, tiled=True).sum(axis=0)]
    pallas_call x0 -> x3, Pallas kernels: none -> 18.2 us  [the longest x1 8.2 us: local(): pl.pallas_call(lambda *refs: update_kernel(nb, rank, *refs), grid=(nb, ra...]
    another operation x5 -> x0, other arithmetic: 17 us -> none  [the longest x1 10.4 us: local(): jnp.stack([g_re * inv[:, :, None], g_im * inv[:, :, None]], axis=1)]
    another operation x2 -> x0, local copies, waits for them, and re-layouts: 7.2 us -> none  [local(): jnp.stack([g_re * inv[:, :, None], g_im * inv[:, :, None]], axis=1)]
  transfers between devices with their start and end apart: 1 -> 3, of which waited for: 1 -> 3; matrix products, arithmetic and copies ran while one was open for 3% -> 1% of each run, Pallas kernels for 0% -> 5%
where the time goes in v1:
time: 88.1 us; the launch traced here: 87.4 us
  waiting for transfers between devices  28 us (32%)
  starting transfers between devices  24.3 us (28%)
  Pallas kernels  18.2 us (21%)
  local copies, waits for them, and re-layouts  10.1 us (11%)
  matrix products  4.69 us (5%)
  between operations  1.33 us (2%)
    all_to_all x1, waiting for transfers between devices, local(): lax.all_to_all(terms.reshape(groups, n // groups * rows, LANES), 'ta', 0,...  13.6 us
    all_to_all x1, starting transfers between devices, local(): h = lax.all_to_all(h, SPACE, 0, 0, tiled=True).sum(axis=0)  13.2 us
    all_to_all x1, waiting for transfers between devices, local(): g = lax.all_to_all(blk, SPACE, 0, 0, tiled=True).reshape(n_space * 4, LANES)  9.72 us
    pallas_call x1, Pallas kernels, local(): pl.pallas_call(lambda *refs: update_kernel(nb, rank, *refs), grid=(nb, ra...  8.2 us
    reshape x1, local copies, waits for them, and re-layouts, local(): v = old_basis.reshape(nb, 2 * rank, 2 * points)  7.8 us
    all_to_all x1, starting transfers between devices, local(): g = lax.all_to_all(blk, SPACE, 0, 0, tiled=True).reshape(n_space * 4, LANES)  7.14 us
    pallas_call x1, Pallas kernels, local(): pl.pallas_call(lambda *refs: project_kernel(nb, rank, *refs), grid=(nb,),...  5.48 us
    dot_general x1, matrix products, local(): vv = jnp.einsum('bjm,bkm->bjk', v, v, preferred_element_type=jnp.float32)  4.69 us
  transfers between devices with their start and end apart: 3, of which 3 were waited for; matrix products, arithmetic and copies ran while one was open for 1% of the time, Pallas kernels for 5%

profile of v1, /device:TPU:1, one launch (start us, length us, event | category | flops | bytes accessed | tf_op | source)
XLA Modules:
  0.0 87.4 jit_solution(6388040370062539841)
XLA Ops:
  0.6 7.8 %reshape.44 = bf16[4,64,8192]{2,1,0:T(8,128)(2,1)} reshape(bf16[4,2,32,2,4096]{4,3,2,1,0:T(2,128)(2,1)} %param.8) | data formatting | bytes 8388608 | tf_op jit(solution)/shard_map/reshape | solution.py:182
  8.4 4.7 %fusion = f32[4,64,64]{1,2,0:T(8,128)S(1)} fusion(bf16[4,64,8192]{2,1,0:T(8,128)(2,1)} %reshape.44), kind=kOutput, calls=%fused_computation.3 | convolution fusion | flops 268435456 | bytes 4259840 | tf_op jit(solution)/shard_map/bjm,bkm->bjk/dot_general | solution.py:183
  13.1 0.1 slice_add_fusion
  13.2 0.1 pad_maximum_fusion
  13.3 0.7 copy.12
  14.0 13.2 %all-to-all-start.1 = ((f32[64,1,128]{2,1,0:T(1,128)}), f32[64,1,128]{2,1,0:T(1,128)S(1)}, u32[]{:S(2)}, u32[]{:S(2)}) async-start(f32[64,1,128]{2,1,0:T(1,128)} %copy.12), calls=%async_computation.1 | async-start | bytes 65536 | tf_op jit(solution)/shard_map/all_to_all | solution.py:187
  27.2 4.5 %transform.1 = f32[2048,128]{1,0:T(8,128)} custom-call(s32[16]{0:T(128)} %refs_0_.2, s32[1]{0:T(128)} %bitcast.refs_1_, f32[4096,128]{1,0:T(8,128)} %bitcast.29), custom_call_target="tpu_custom_call" | custom-call | tf_op jit(solution)/shard_map/transform/pallas_call | solution.py:171
  31.7 4.7 %all-to-all-done.1 = f32[64,1,128]{2,1,0:T(1,128)S(1)} async-done(((f32[64,1,128]{2,1,0:T(1,128)}), f32[64,1,128]{2,1,0:T(1,128)S(1)}, u32[]{:S(2)}, u32[]{:S(2)}) %all-to-all-start.1) | async-done | bytes 32800 | tf_op jit(solution)/shard_map/all_to_all | solution.py:187
  36.4 4.0 %all-to-all-start = ((f32[4,512,128]{2,1,0:T(8,128)}), f32[4,512,128]{2,1,0:T(8,128)S(1)}, u32[]{:S(2)}, u32[]{:S(2)}) async-start(f32[4,512,128]{2,1,0:T(8,128)} %bitcast.27), calls=%async_computation | async-start | bytes 2097152 | tf_op jit(solution)/shard_map/all_to_all | solution.py:178
  40.4 0.6 reduce_sum.11
  41.0 13.6 %all-to-all-done = f32[4,512,128]{2,1,0:T(8,128)S(1)} async-done(((f32[4,512,128]{2,1,0:T(8,128)}), f32[4,512,128]{2,1,0:T(8,128)S(1)}, u32[]{:S(2)}, u32[]{:S(2)}) %all-to-all-start) | async-done | bytes 1048608 | tf_op jit(solution)/shard_map/all_to_all | solution.py:178
  54.6 0.0 copy-start
  54.6 1.0 %copy-done = f32[4,512,128]{2,1,0:T(8,128)} copy-done((f32[4,512,128]{2,1,0:T(8,128)}, f32[4,512,128]{2,1,0:T(8,128)S(1)}, u32[]{:S(2)}) %copy-start) | copy-done | bytes 1048600
  55.6 5.5 %project.1 = (f32[4,2,64,128]{3,2,1,0:T(8,128)}, f32[64,4,128]{2,1,0:T(4,128)}) custom-call(f32[4,4,2,64,128]{4,3,2,1,0:T(8,128)} %bitcast.28, bf16[4,2,32,64,128]{4,3,2,1,0:T(8,128)(2,1)} %bitcast.25, f32[1,128]{1,0:T(1,128)} %bitcast.32), custom_call_target="tpu_custom_call" | custom-call | tf_op jit(solution)/shard_map/project/pallas_call | solution.py:189
  61.0 7.1 %all-to-all-start.2 = ((f32[64,4,128]{2,1,0:T(4,128)}), f32[64,4,128]{2,1,0:T(4,128)S(1)}, u32[]{:S(2)}, u32[]{:S(2)}) async-start(f32[64,4,128]{2,1,0:T(4,128)} %get-tuple-element.6), calls=%async_computation.2 | async-start | bytes 262144 | tf_op jit(solution)/shard_map/all_to_all | solution.py:208
  68.8 9.7 %all-to-all-done.2 = f32[64,4,128]{2,1,0:T(4,128)S(1)} async-done(((f32[64,4,128]{2,1,0:T(4,128)}), f32[64,4,128]{2,1,0:T(4,128)S(1)}, u32[]{:S(2)}, u32[]{:S(2)}) %all-to-all-start.2) | async-done | bytes 131104 | tf_op jit(solution)/shard_map/all_to_all | solution.py:208
  78.6 0.0 copy-start.1
  78.6 0.6 copy-done.1
  79.2 8.2 %update.1 = (bf16[4,2,32,64,128]{4,3,2,1,0:T(8,128)(2,1)}, f32[4,2,32,32]{3,2,1,0:T(8,128)}) custom-call(s32[1]{0:T(128)S(6)} %copy.14.refs_0_, f32[256,128]{1,0:T(8,128)} %bitcast.30, f32[4,32]{1,0:T(4,128)} %refs_2_.1, f32[4,2,64,128]{3,2,1,0:T(8,128)} %get-tuple-element.7.refs_3_, bf16[4,2,32,64,128]{4,3,2,1,0:T(8,128)(2,1)} %bitcast.26), custom_call_target="tpu_custom_call" | custom-call | tf_op jit(solution)/shard_map/update/pallas_call | solution.py:211
Async XLA Ops:
  14.0 22.4 %all-to-all-start.1 = ((f32[64,1,128]{2,1,0:T(1,128)}), f32[64,1,128]{2,1,0:T(1,128)S(1)}, u32[]{:S(2)}, u32[]{:S(2)}) async-start(f32[64,1,128]{2,1,0:T(1,128)} %copy.12), calls=%async_computation.1 | async-start | bytes 65536 | tf_op jit(solution)/shard_map/all_to_all | solution.py:187
  36.4 18.2 %all-to-all-start = ((f32[4,512,128]{2,1,0:T(8,128)}), f32[4,512,128]{2,1,0:T(8,128)S(1)}, u32[]{:S(2)}, u32[]{:S(2)}) async-start(f32[4,512,128]{2,1,0:T(8,128)} %bitcast.27), calls=%async_computation | async-start | bytes 2097152 | tf_op jit(solution)/shard_map/all_to_all | solution.py:178
  54.6 1.0 %copy-start = (f32[4,512,128]{2,1,0:T(8,128)}, f32[4,512,128]{2,1,0:T(8,128)S(1)}, u32[]{:S(2)}) copy-start(f32[4,512,128]{2,1,0:T(8,128)S(1)} %all-to-all-done) | copy-start | bytes 3145732
  61.0 17.5 %all-to-all-start.2 = ((f32[64,4,128]{2,1,0:T(4,128)}), f32[64,4,128]{2,1,0:T(4,128)S(1)}, u32[]{:S(2)}, u32[]{:S(2)}) async-start(f32[64,4,128]{2,1,0:T(4,128)} %get-tuple-element.6), calls=%async_computation.2 | async-start | bytes 262144 | tf_op jit(solution)/shard_map/all_to_all | solution.py:208
  78.6 0.6 copy-start.1

commit v2 on v1

v2 whole, which is shorter than its diff:
```python
import math

import jax
import jax.numpy as jnp
import numpy as np
from jax import lax
from jax.experimental import pallas as pl
from jax.experimental.pallas import tpu as pltpu
from jax.sharding import Mesh, PartitionSpec as P

SPACE = ("y", "z", "core")
LANES = 128
BLK = 8
UP = ((2, 0), (2, 1), (1, 2), (1, 3))
DOWN = ((2, 2), (2, 3), (3, 0), (3, 1))
KEEP = ((1, 0), (1, 1), (3, 2), (3, 3))
OWN = ((0, 0), (0, 1), (0, 2), (0, 3))
ORDER = UP + DOWN + KEEP + OWN


def fold(v, axis):
    shape = v.shape
    lead, tiles = shape[:-2], shape[-1] // LANES
    v = v.reshape(*lead, 2, tiles, LANES)
    return jnp.swapaxes(v, axis, axis + 1).reshape(*lead, 2 * tiles, LANES)


def unfold(v, axis):
    lead, rows = v.shape[:-2], v.shape[-2]
    v = v.reshape(*lead, rows // 2, 2, LANES)
    return jnp.swapaxes(v, axis, axis + 1).reshape(*lead, 2, rows // 2 * LANES)


def split3(v):
    hi = v.astype(jnp.bfloat16)
    rest = v - hi.astype(jnp.float32)
    mid = rest.astype(jnp.bfloat16)
    low = (rest - mid.astype(jnp.float32)).astype(jnp.bfloat16)
    return hi, mid, low


def transform_kernel(total, slice_len, rows, bins_ref, place_ref, x_ref, *out_refs):
    n = 2 * len(ORDER)
    place = place_ref[0]
    row = lax.broadcasted_iota(jnp.int32, (n, slice_len), 0)
    t = lax.broadcasted_iota(jnp.int32, (n, slice_len), 1) + place * slice_len
    which = jnp.zeros((n, slice_len), jnp.int32)
    for i, (ahead, b) in enumerate(ORDER):
        which = jnp.where(row // 2 == i, bins_ref[((place + ahead) % 4) * 4 + b], which)
    phase = (which * t + (row % 2) * (total // 4)) % total
    step = 2.0 * math.pi / total
    window = 0.5 - 0.5 * jnp.cos(step * t.astype(jnp.float32))
    table = jnp.cos(step * phase.astype(jnp.float32)) * window * math.sqrt(8.0 / (3.0 * total))
    t_hi = table.astype(jnp.bfloat16)
    t_lo = (table - t_hi.astype(jnp.float32)).astype(jnp.bfloat16)
    left = jnp.concatenate([t_hi, t_lo], axis=0)
    left = jnp.concatenate([left, left], axis=1)
    each = n // len(out_refs)
    for r in range(0, rows, 2):
        x = jnp.concatenate(
            [x_ref[pl.ds(r, slice_len, stride=rows), :], x_ref[pl.ds(r + 1, slice_len, stride=rows), :]],
            axis=1,
        )
        hi = x.astype(jnp.bfloat16)
        lo = (x - hi.astype(jnp.float32)).astype(jnp.bfloat16)
        res = jnp.dot(left, jnp.concatenate([hi, lo], axis=0), preferred_element_type=jnp.float32)
        res = res[:n] + res[n:]
        for i, out_ref in enumerate(out_refs):
            part = res[i * each:(i + 1) * each]
            out_ref[pl.ds(r, each, stride=rows), :] = part[:, :LANES]
            out_ref[pl.ds(r + 1, each, stride=rows), :] = part[:, LANES:]


def gram_kernel(nb, rank, core_ref, u_ref, send_ref, keep_ref, wide_ref, all_ref):
    b = pl.program_id(0)
    rows = u_ref.shape[-2]
    for c in range(2):
        def widen(j, carry, c=c):
            at = pl.multiple_of((c * rank + j) * rows, rows)
            wide_ref[pl.ds(at, rows), :] = u_ref[0, c, j].astype(jnp.float32)
            return carry

        lax.fori_loop(0, rank, widen, 0, unroll=4)
    some = 8
    n = 2 * rank

    def body(i, acc):
        part = [wide_ref[pl.ds(i * some + k, n, stride=rows), :].astype(jnp.bfloat16) for k in range(some)]
        v = jnp.concatenate(part, axis=1)
        return acc + lax.dot_general(v, v, (((1,), (1,)), ((), ())), preferred_element_type=jnp.float32)

    vv = lax.fori_loop(0, rows // some, body, jnp.zeros((n, n), jnp.float32))
    h_re = vv[:rank, :rank] + vv[rank:, rank:]
    h_im = vv[:rank, rank:] - vv[rank:, :rank]
    j = lax.broadcasted_iota(jnp.int32, (rank, rank), 0)
    k = lax.broadcasted_iota(jnp.int32, (rank, rank), 1)
    all_ref[b] = jnp.where(j <= k, h_re, h_im)

    @pl.when(b == nb - 1)
    def _():
        h = jnp.concatenate([all_ref[i] for i in range(nb)], axis=1)
        low, high = h[:rank // 2], h[rank // 2:]
        first = core_ref[0] == 0
        send_ref[...] = jnp.where(first, high, low)
        keep_ref[...] = jnp.where(first, low, high)


def project_kernel(nb, rank, own_ref, a_ref, b_ref, c_ref, d_ref, u_ref, h_ref, s_ref, blk_ref, acc_ref):
    b = pl.program_id(0)
    rows = u_ref.shape[-2]

    @pl.when(b == 0)
    def _():
        acc_ref[...] = jnp.zeros_like(acc_ref)

    low = b < nb // 2
    s = own_ref[0] + jnp.where(low, b_ref[0, 0], a_ref[0, 0]) + jnp.where(low, c_ref[0], d_ref[0])
    s_ref[0] = s
    s_re, s_im = s[0], s[1]

    def eight(v):
        return v.reshape(rows // 8, 8, LANES).sum(axis=0)

    acc_ref[pl.ds((2 * nb * rank + b) * 8, 8), :] = eight(s_re * s_re + s_im * s_im)

    def body(j, carry):
        u_re = u_ref[0, 0, j].astype(jnp.float32)
        u_im = u_ref[0, 1, j].astype(jnp.float32)
        at = (b * 2 * rank + j) * 8
        acc_ref[pl.ds(pl.multiple_of(at, 8), 8), :] = eight(u_re * s_re + u_im * s_im)
        acc_ref[pl.ds(pl.multiple_of(at + rank * 8, 8), 8), :] = eight(u_re * s_im - u_im * s_re)
        return carry

    lax.fori_loop(0, rank, body, 0, unroll=4)

    @pl.when(b == nb - 1)
    def _():
        n = acc_ref.shape[0] // 8
        x = acc_ref[pl.ds(0, n, stride=8), :]
        for k in range(1, 8):
            x = x + acc_ref[pl.ds(k, n, stride=8), :]
        ones = jnp.ones((8, LANES), jnp.bfloat16)
        sums = sum(
            lax.dot_general(ones, v, (((1,), (1,)), ((), ())), preferred_element_type=jnp.float32)
            for v in split3(x)
        )
        blk = jnp.concatenate(
            [sums[0:1, k * LANES:(k + 1) * LANES] for k in range(3)]
            + [h_ref[...], jnp.zeros((1, LANES), jnp.float32)],
            axis=0,
        )
        blk_ref[...] = jnp.broadcast_to(blk[None], blk_ref.shape)


def update_kernel(nb, rank, count_ref, g_ref, pick_ref, eig_ref, s_ref, u_ref, out_ref, coh_ref, coef_ref):
    b, half = pl.program_id(0), pl.program_id(1)
    rows = u_ref.shape[-2]

    @pl.when((b == 0) & (half == 0))
    def _():
        count = jnp.full((1, 1), count_ref[0], jnp.int32).astype(jnp.float32)
        w_old = count / (count + 1.0)
        w_new = 1.0 / (count + 1.0)
        pick = pick_ref[...]
        sums = sum(jnp.dot(pick, v, preferred_element_type=jnp.float32) for v in split3(g_ref[...]))
        g = sums[BLK:]
        g_t = g.T
        j = lax.broadcasted_iota(jnp.int32, (rank, rank), 0)
        k = lax.broadcasted_iota(jnp.int32, (rank, rank), 1)
        eye = j == k

        def col(v):
            return jnp.where(eye, v, 0.0).sum(axis=1, keepdims=True)

        for i in range(nb):
            at = (i % 2) * 2 * rank
            cr = sums[i // 2:i // 2 + 1, at:at + rank]
            ci = sums[i // 2:i // 2 + 1, at + rank:at + 2 * rank]
            power = sums[2:3, i:i + 1]
            a = w_old * eig_ref[i:i + 1, :]
            cr_c, ci_c, a_c = col(cr), col(ci), col(a)
            p = g[:, i * rank:(i + 1) * rank]
            p_t = g_t[i * rank:(i + 1) * rank, :]
            h_re = jnp.where(j <= k, p, p_t)
            h_im = jnp.where(j > k, p, jnp.where(eye, 0.0, -p_t))
            both = w_new * (a_c + a + w_new * power)
            gram_re = a_c * a * h_re + (cr_c * cr + ci_c * ci) * both
            gram_im = a_c * a * h_im + (ci_c * cr - cr_c * ci) * both
            diag = jnp.where(eye, gram_re, 0.0)
            inv_c = 1.0 / jnp.sqrt(diag.sum(axis=1, keepdims=True) + 1e-06)
            inv_r = 1.0 / jnp.sqrt(diag.sum(axis=0, keepdims=True) + 1e-06)
            coh_ref[i, 0] = gram_re * inv_c * inv_r
            coh_ref[i, 1] = gram_im * inv_c * inv_r
            for m, v in enumerate((a_c * inv_c, w_new * cr_c * inv_c, w_new * ci_c * inv_c)):
                coef_ref[pl.ds((m * nb + i) * rank, rank), :] = jnp.broadcast_to(v, (rank, LANES))

    s_re, s_im = s_ref[0, 0], s_ref[0, 1]
    block = u_ref.shape[2]

    def body(j, carry):
        at = b * rank + half * block + j

        def coef(m):
            one = coef_ref[pl.ds(m * nb * rank + at, 1), :]
            return jnp.broadcast_to(one, (rows, LANES))

        alpha, beta, gamma = coef(0), coef(1), coef(2)
        u_re = u_ref[0, 0, j].astype(jnp.float32)
        u_im = u_ref[0, 1, j].astype(jnp.float32)
        out_ref[0, 0, j] = (alpha * u_re + (beta * s_re + gamma * s_im)).astype(out_ref.dtype)
        out_ref[0, 1, j] = (alpha * u_im + (beta * s_im - gamma * s_re)).astype(out_ref.dtype)
        return carry

    lax.fori_loop(0, block, body, 0, unroll=4)


def pick_table(rank):
    m = np.zeros((BLK + rank, 64 * BLK), np.float32)
    for s in range(64):
        y, core = s // 16, s % 2
        for k in range(3):
            m[k, s * BLK + k] = 1.0
        for i in range(4):
            m[BLK + core * 16 + (y & 1) * 8 + (y >> 1) * 4 + i, s * BLK + 3 + i] = 1.0
    return jnp.asarray(m, jnp.bfloat16)


def trade(v, axis, mask):
    n = lax.axis_size(axis)
    return lax.ppermute(v, axis, [(i, i ^ mask) for i in range(n)])


SMEM = pl.BlockSpec(memory_space=pltpu.SMEM)
VMEM = pl.BlockSpec(memory_space=pltpu.VMEM)


def call_transform(bins, place, x, total, slice_len, rows):
    n = 2 * len(ORDER)
    return pl.pallas_call(
        lambda *refs: transform_kernel(total, slice_len, rows, *refs),
        out_shape=[jax.ShapeDtypeStruct((n // 4 * rows, LANES), jnp.float32)] * 4,
        in_specs=[SMEM, SMEM, VMEM],
        out_specs=[VMEM] * 4,
        name="transform",
    )(bins, place, x)


def call_gram(core, u):
    nb, _, rank, rows, _ = u.shape
    return pl.pallas_call(
        lambda *refs: gram_kernel(nb, rank, *refs),
        grid=(nb,),
        out_shape=[jax.ShapeDtypeStruct((rank // 2, nb * rank), jnp.float32)] * 2,
        in_specs=[SMEM, pl.BlockSpec((1, 2, rank, rows, LANES), lambda b: (b, 0, 0, 0, 0))],
        out_specs=[pl.BlockSpec((rank // 2, nb * rank), lambda b: (0, 0))] * 2,
        scratch_shapes=[
            pltpu.VMEM((2 * rank * rows, LANES), jnp.float32),
            pltpu.VMEM((nb, rank, rank), jnp.float32),
        ],
        cost_estimate=pl.CostEstimate(flops=2 * nb * (2 * rank) ** 2 * rows * LANES * 8, bytes_accessed=u.size * 4, transcendentals=0),
        name="gram",
    )(core, u)


def call_project(own, a, b_, c, d, u, h, n_space):
    nb, _, rank, rows, _ = u.shape
    half = nb // 2
    return pl.pallas_call(
        lambda *refs: project_kernel(nb, rank, *refs),
        grid=(nb,),
        out_shape=(
            jax.ShapeDtypeStruct((nb, 2, rows, LANES), jnp.float32),
            jax.ShapeDtypeStruct((n_space, BLK, LANES), jnp.float32),
        ),
        in_specs=[
            pl.BlockSpec((1, 2, rows, LANES), lambda b: (b, 0, 0, 0)),
            pl.BlockSpec((1, 1, 2, rows, LANES), lambda b: (1, jnp.maximum(b - half, 0), 0, 0, 0)),
            pl.BlockSpec((1, 1, 2, rows, LANES), lambda b: (1, jnp.minimum(b, half - 1), 0, 0, 0)),
            pl.BlockSpec((1, 2, rows, LANES), lambda b: (jnp.minimum(b, half - 1), 0, 0, 0)),
            pl.BlockSpec((1, 2, rows, LANES), lambda b: (jnp.maximum(b - half, 0), 0, 0, 0)),
            pl.BlockSpec((1, 2, rank, rows, LANES), lambda b: (b, 0, 0, 0, 0)),
            pl.BlockSpec((4, LANES), lambda b: (0, 0)),
        ],
        out_specs=(
            pl.BlockSpec((1, 2, rows, LANES), lambda b: (b, 0, 0, 0)),
            pl.BlockSpec((n_space, BLK, LANES), lambda b: (0, 0, 0)),
        ),
        scratch_shapes=[pltpu.VMEM((3 * LANES * 8, LANES), jnp.float32)],
        cost_estimate=pl.CostEstimate(flops=16 * u.size, bytes_accessed=u.size * 2, transcendentals=0),
        name="project",
    )(own, a, b_, c, d, u, h)


def call_update(block_count, g, eigenvalues, spec, u):
    nb, _, rank, rows, _ = u.shape
    block = rank // 2
    n = g.shape[0]
    return pl.pallas_call(
        lambda *refs: update_kernel(nb, rank, *refs),
        grid=(nb, rank // block),
        out_shape=(
            jax.ShapeDtypeStruct(u.shape, jnp.bfloat16),
            jax.ShapeDtypeStruct((nb, 2, rank, rank), jnp.float32),
        ),
        in_specs=[
            SMEM,
            pl.BlockSpec((n, LANES), lambda b, i: (0, 0)),
            pl.BlockSpec((BLK + rank, n), lambda b, i: (0, 0)),
            pl.BlockSpec((nb, rank), lambda b, i: (0, 0)),
            pl.BlockSpec((1, 2, rows, LANES), lambda b, i: (b, 0, 0, 0)),
            pl.BlockSpec((1, 2, block, rows, LANES), lambda b, i: (b, 0, i, 0, 0)),
        ],
        out_specs=(
            pl.BlockSpec((1, 2, block, rows, LANES), lambda b, i: (b, 0, i, 0, 0)),
            pl.BlockSpec((nb, 2, rank, rank), lambda b, i: (0, 0, 0, 0)),
        ),
        scratch_shapes=[pltpu.VMEM((3 * nb * rank, LANES), jnp.float32)],
        name="update",
    )(block_count, g, pick_table(rank), eigenvalues, spec, u)


def local(snapshots, bins, eigenvalues, old_basis, block_count):
    slice_len, _, points = snapshots.shape
    groups = lax.axis_size("ta")
    total = slice_len * groups
    rows = 2 * points // LANES
    nb, _, rank = old_basis.shape[:3]
    n_space = lax.axis_size(SPACE)
    place = lax.axis_index("ta").astype(jnp.int32).reshape(1)
    core = lax.axis_index("core").astype(jnp.int32).reshape(1)
    y = lax.axis_index("y")

    x = fold(snapshots, 1).reshape(slice_len * rows, LANES)
    up, down, keep, own = call_transform(bins, place, x, total, slice_len, rows)
    ring_up = [(i, (i + 1) % groups) for i in range(groups)]
    ring_down = [(i, (i - 1) % groups) for i in range(groups)]
    a = lax.ppermute(up, "ta", ring_up)
    b = lax.ppermute(down, "ta", ring_down)

    u = fold(old_basis, 3)
    send, kept = call_gram(core, u)
    h = kept + trade(send, "core", 1)

    half = up.shape[0] // 2
    c = lax.ppermute(keep[:half] + a[:half], "ta", ring_up)
    d = lax.ppermute(keep[half:] + b[:half], "ta", ring_down)

    for bit in (0, 1):
        n = h.shape[0] // 2
        first = (y >> bit) & 1 == 0
        h = jnp.where(first, h[:n], h[n:]) + trade(jnp.where(first, h[n:], h[:n]), "y", 1 << bit)

    spec, blk = call_project(
        own.reshape(nb, 2, rows, LANES),
        a.reshape(2, nb // 2, 2, rows, LANES),
        b.reshape(2, nb // 2, 2, rows, LANES),
        c.reshape(nb // 2, 2, rows, LANES),
        d.reshape(nb // 2, 2, rows, LANES),
        u, h, n_space,
    )
    g = lax.all_to_all(blk, SPACE, 0, 0, tiled=True).reshape(n_space * BLK, LANES)
    fresh, coherence = call_update(block_count, g, eigenvalues, spec, u)
    return unfold(fresh, 3), coherence


def solution(mesh):
    inner = Mesh(mesh.devices.reshape(4, 4, 8, 2), ("ta",) + SPACE)
    return jax.shard_map(
        local,
        mesh=inner,
        in_specs=(P("ta", None, SPACE), P(), P("ta", None), P("ta", None, None, None, SPACE), P()),
        out_specs=(P("ta", None, None, None, SPACE), P("ta", None, None, None)),
        check_vma=False,
    )
```

time: 88.1 us -> 81.6 us (0.926)
  Pallas kernels: 18.2 us -> 30.7 us
  local copies, waits for them, and re-layouts: 10.1 us -> 1.36 us
  waiting for transfers between devices: 28 us -> 20.9 us
  matrix products: 4.69 us -> 0 us
  other arithmetic: 0.78 us -> 2.48 us
    all_to_all x3 -> x1, waiting for transfers between devices: 28 us -> 11.4 us  [local(): lax.all_to_all(blk, SPACE, 0, 0, tiled=True).reshape(n_space * BLK, LANES)]
    pallas_call x3 -> x4, Pallas kernels: 18.2 us -> 30.7 us  [the longest x1 12.4 us: call_gram(): pl.pallas_call(lambda *refs: gram_kernel(nb, rank, *refs), grid=(nb,), ou...]
    ppermute x0 -> x7, starting transfers between devices: none -> 10.5 us  [the longest x3 5.5 us: trade(): return lax.ppermute(v, axis, [(i, i ^ mask) for i in range(n)])]
    all_to_all x3 -> x1, starting transfers between devices: 24.3 us -> 13.8 us  [local(): lax.all_to_all(blk, SPACE, 0, 0, tiled=True).reshape(n_space * BLK, LANES)]
    ppermute x0 -> x7, waiting for transfers between devices: none -> 9.51 us  [the longest x1 4.02 us: local(): a = lax.ppermute(up, 'ta', ring_up)]
    reshape x2 -> x0, local copies, waits for them, and re-layouts: 8.5 us -> none  [the longest x1 7.8 us: local(): v = old_basis.reshape(nb, 2 * rank, 2 * points)]
    dot_general x1 -> x0, matrix products: 4.69 us -> none  [local(): vv = jnp.einsum('bjm,bkm->bjk', v, v, preferred_element_type=jnp.float32)]
    add x1 -> x4, other arithmetic: 0.1 us -> 2.47 us  [the longest x1 1.19 us: local(): d = lax.ppermute(keep[half:] + b[:half], 'ta', ring_down)]
  transfers between devices with their start and end apart: 3 -> 8, of which waited for: 3 -> 5; matrix products, arithmetic and copies ran while one was open for 1% -> 2% of each run, Pallas kernels for 5% -> 6%
where the time goes in v2:
time: 81.6 us; the launch traced here: 81.1 us
  Pallas kernels  30.7 us (38%)
  starting transfers between devices  24.3 us (30%)
  waiting for transfers between devices  20.9 us (26%)
  other arithmetic  2.48 us (3%)
  local copies, waits for them, and re-layouts  1.36 us (2%)
  between operations  1.31 us (2%)
    all_to_all x1, starting transfers between devices, local(): lax.all_to_all(blk, SPACE, 0, 0, tiled=True).reshape(n_space * BLK, LANES)  13.8 us
    pallas_call x1, Pallas kernels, call_gram(): pl.pallas_call(lambda *refs: gram_kernel(nb, rank, *refs), grid=(nb,), ou...  12.4 us
    all_to_all x1, waiting for transfers between devices, local(): lax.all_to_all(blk, SPACE, 0, 0, tiled=True).reshape(n_space * BLK, LANES)  11.4 us
    pallas_call x1, Pallas kernels, call_update(): pl.pallas_call(lambda *refs: update_kernel(nb, rank, *refs), grid=(nb, ra...  8.32 us
    pallas_call x1, Pallas kernels, call_project(): pl.pallas_call(lambda *refs: project_kernel(nb, rank, *refs), grid=(nb,),...  5.5 us
    ppermute x3, starting transfers between devices, trade(): return lax.ppermute(v, axis, [(i, i ^ mask) for i in range(n)])  5.5 us
    pallas_call x1, Pallas kernels, call_transform(): pl.pallas_call(lambda *refs: transform_kernel(total, slice_len, rows, *re...  4.5 us
    ppermute x1, waiting for transfers between devices, local(): a = lax.ppermute(up, 'ta', ring_up)  4.02 us
  transfers between devices with their start and end apart: 8, of which 5 were waited for; matrix products, arithmetic and copies ran while one was open for 2% of the time, Pallas kernels for 6%

profile of v2, /device:TPU:1, one launch (start us, length us, event | category | flops | bytes accessed | tf_op | source)
XLA Modules:
  0.0 81.1 jit_solution(13777054179352416562)
XLA Ops:
  0.6 12.4 %gram.1 = (f32[16,128]{1,0:T(8,128)}, f32[16,128]{1,0:T(8,128)}) custom-call(s32[1]{0:T(128)} %bitcast.12.refs_0_, bf16[4,2,32,64,128]{4,3,2,1,0:T(8,128)(2,1)} %bitcast.23), custom_call_target="tpu_custom_call" | custom-call | flops 2147483648 | bytes 8388608 | tf_op jit(solution)/shard_map/gram/pallas_call | solution.py:250
  13.0 3.2 %collective-permute-start.4 = (f32[16,128]{1,0:T(8,128)}, f32[16,128]{1,0:T(8,128)S(1)}, u32[]{:S(2)}, u32[]{:S(2)}) collective-permute-start(f32[16,128]{1,0:T(8,128)} %get-tuple-element.17), channel_id=1, source_target_pairs={{0,1},{1,0},{2,3},{3,2},{4,5},{5,4},{6,7},{7,6},{8,9},{9,8},{10,11... | collective-permute-start | bytes 24584 | tf_op jit(solution)/shard_map/ppermute | solution.py:230
  16.3 1.0 %collective-permute-done.4 = f32[16,128]{1,0:T(8,128)S(1)} collective-permute-done((f32[16,128]{1,0:T(8,128)}, f32[16,128]{1,0:T(8,128)S(1)}, u32[]{:S(2)}, u32[]{:S(2)}) %collective-permute-start.4) | collective-permute-done | bytes 8224 | tf_op jit(solution)/shard_map/ppermute | solution.py:230
  17.3 0.7 add.17
  18.0 0.0 collective-permute-start.5
  18.0 4.5 %transform.1 = (f32[512,128]{1,0:T(8,128)}, f32[512,128]{1,0:T(8,128)}, f32[512,128]{1,0:T(8,128)}, f32[512,128]{1,0:T(8,128)}) custom-call(s32[16]{0:T(128)} %refs_0_.2, s32[1]{0:T(128)} %bitcast.refs_1_, f32[4096,128]{1,0:T(8,128)} %bitcast.26), custom_call_target="tpu_custom_call" | custom-call | tf_op jit(solution)/shard_map/transform/pallas_call | solution.py:239
  22.5 0.8 collective-permute-start
  23.3 1.9 %collective-permute-start.1 = (f32[512,128]{1,0:T(8,128)}, f32[512,128]{1,0:T(8,128)S(1)}, u32[]{:S(2)}, u32[]{:S(2)}) collective-permute-start(f32[512,128]{1,0:T(8,128)} %get-tuple-element.14), channel_id=1, source_target_pairs={{0,192},{64,0},{128,64},{192,128},{1,193},{65,1},{129,65},{193,129... | collective-permute-start | bytes 786440 | tf_op jit(solution)/shard_map/ppermute | solution.py:338
  25.2 0.0 collective-permute-done.5
  25.2 2.3 %collective-permute-start.6 = (f32[4,128]{1,0:T(4,128)S(1)}, f32[4,128]{1,0:T(4,128)S(1)}, u32[]{:S(2)}, u32[]{:S(2)}) collective-permute-start(f32[4,128]{1,0:T(4,128)S(1)} %slice_select_fusion.1), channel_id=1, source_target_pairs={{0,32},{16,48},{32,0},{48,16},{1,33},{17,49},{33,1},{49,17},{2,34}... | collective-permute-start | bytes 6152 | tf_op jit(solution)/shard_map/ppermute | solution.py:230
  27.5 4.0 %collective-permute-done = f32[512,128]{1,0:T(8,128)S(1)} collective-permute-done((f32[512,128]{1,0:T(8,128)}, f32[512,128]{1,0:T(8,128)S(1)}, u32[]{:S(2)}, u32[]{:S(2)}) %collective-permute-start) | collective-permute-done | bytes 262176 | tf_op jit(solution)/shard_map/ppermute | solution.py:337
  31.5 0.0 copy-start.1
  31.5 0.0 collective-permute-done.1
  31.5 0.0 copy-start.2
  31.5 1.2 %slice_add_fusion = (f32[256,128]{1,0:T(8,128)S(1)}, f32[256,128]{1,0:T(8,128)S(1)}) fusion(f32[512,128]{1,0:T(8,128)S(1)} %collective-permute-done.1, f32[512,128]{1,0:T(8,128)} %get-tuple-element.15, f32[512,128]{1,0:T(8,128)S(1)} %collective-permute-done), kind=kLoop, calls=%fused_computation | loop fusion | flops 65536 | bytes 786432 | tf_op jit(solution)/shard_map/add | solution.py:346
  32.7 2.3 %collective-permute-start.3 = (f32[256,128]{1,0:T(8,128)S(1)}, f32[256,128]{1,0:T(8,128)S(1)}, u32[]{:S(2)}, u32[]{:S(2)}) collective-permute-start(f32[256,128]{1,0:T(8,128)S(1)} %get-tuple-element.22), channel_id=1, source_target_pairs={{0,192},{64,0},{128,64},{192,128},{1,193},{65,1},{129,65},{193,129... | collective-permute-start | bytes 393224 | tf_op jit(solution)/shard_map/ppermute | solution.py:346
  35.0 0.0 collective-permute-start.2
  35.0 0.0 collective-permute-done.6
  35.0 0.6 select_add_fusion.1.refs_6_
  35.6 1.4 %collective-permute-done.3 = f32[256,128]{1,0:T(8,128)S(1)} collective-permute-done((f32[256,128]{1,0:T(8,128)S(1)}, f32[256,128]{1,0:T(8,128)S(1)}, u32[]{:S(2)}, u32[]{:S(2)}) %collective-permute-start.3) | collective-permute-done | bytes 131104 | tf_op jit(solution)/shard_map/ppermute | solution.py:346
  37.0 0.0 copy-start.3
  37.0 3.1 %collective-permute-done.2 = f32[256,128]{1,0:T(8,128)S(1)} collective-permute-done((f32[256,128]{1,0:T(8,128)S(1)}, f32[256,128]{1,0:T(8,128)S(1)}, u32[]{:S(2)}, u32[]{:S(2)}) %collective-permute-start.2) | collective-permute-done | bytes 131104 | tf_op jit(solution)/shard_map/ppermute | solution.py:345
  40.0 0.0 copy-start.4
  40.1 0.0 copy-done.1
  40.1 0.0 copy-done.2
  40.1 0.0 copy-done.3
  40.1 0.6 copy-done.4
  40.7 5.5 %project.1 = (f32[4,2,64,128]{3,2,1,0:T(8,128)}, f32[64,8,128]{2,1,0:T(8,128)}) custom-call(f32[4,2,64,128]{3,2,1,0:T(8,128)} %bitcast.30, f32[2,2,2,64,128]{4,3,2,1,0:T(8,128)} %bitcast.28, f32[2,2,2,64,128]{4,3,2,1,0:T(8,128)} %bitcast.29, f32[2,2,64,128]{3,2,1,0:T(8,128)} %bitcast.32, f32[2,2,64,128]{3,2,1,0:T(8,128)} %bitcast.31, ...), custom_call_target="tpu_custom_call" | custom-call | flops 33554432 | bytes 4194304 | tf_op jit(solution)/shard_map/project/pallas_call | solution.py:268
  46.2 13.8 %all-to-all-start = ((f32[64,8,128]{2,1,0:T(8,128)}), f32[64,8,128]{2,1,0:T(8,128)S(1)}, u32[]{:S(2)}, u32[]{:S(2)}) async-start(f32[64,8,128]{2,1,0:T(8,128)} %get-tuple-element.18), calls=%async_computation | async-start | bytes 524288 | tf_op jit(solution)/shard_map/all_to_all | solution.py:361
  60.7 11.4 %all-to-all-done = f32[64,8,128]{2,1,0:T(8,128)S(1)} async-done(((f32[64,8,128]{2,1,0:T(8,128)}), f32[64,8,128]{2,1,0:T(8,128)S(1)}, u32[]{:S(2)}, u32[]{:S(2)}) %all-to-all-start) | async-done | bytes 262176 | tf_op jit(solution)/shard_map/all_to_all | solution.py:361
  72.0 0.0 copy-start
  72.1 0.7 copy-done
  72.8 8.3 %update.1 = (bf16[4,2,32,64,128]{4,3,2,1,0:T(8,128)(2,1)}, f32[4,2,32,32]{3,2,1,0:T(8,128)}) custom-call(s32[1]{0:T(128)S(6)} %copy.11.refs_0_, f32[512,128]{1,0:T(8,128)} %bitcast.27, bf16[40,512]{1,0:T(8,128)(2,1)} %constant.20.clone.refs_2_, f32[4,32]{1,0:T(4,128)} %refs_3_.1, f32[4,2,64,128]{3,2,1,0:T(8,128)} %get-tuple-element.19.refs_4_, ...), custom_call_target="tpu_custom_call" | custom-call | tf_op jit(solution)/shard_map/update/pallas_call | solution.py:298
  (3 shorter events, 0.0 us)
Async XLA Ops:
  13.0 4.3 %collective-permute-start.4 = (f32[16,128]{1,0:T(8,128)}, f32[16,128]{1,0:T(8,128)S(1)}, u32[]{:S(2)}, u32[]{:S(2)}) collective-permute-start(f32[16,128]{1,0:T(8,128)} %get-tuple-element.17), channel_id=1, source_target_pairs={{0,1},{1,0},{2,3},{3,2},{4,5},{5,4},{6,7},{7,6},{8,9},{9,8},{10,11... | collective-permute-start | bytes 24584 | tf_op jit(solution)/shard_map/ppermute | solution.py:230
  18.0 7.2 %collective-permute-start.5 = (f32[8,128]{1,0:T(8,128)S(1)}, f32[8,128]{1,0:T(8,128)S(1)}, u32[]{:S(2)}, u32[]{:S(2)}) collective-permute-start(f32[8,128]{1,0:T(8,128)S(1)} %slice_select_fusion), channel_id=1, source_target_pairs={{0,16},{16,0},{32,48},{48,32},{1,17},{17,1},{33,49},{49,33},{2,18}... | collective-permute-start | bytes 12296 | tf_op jit(solution)/shard_map/ppermute | solution.py:230
  22.5 9.0 %collective-permute-start = (f32[512,128]{1,0:T(8,128)}, f32[512,128]{1,0:T(8,128)S(1)}, u32[]{:S(2)}, u32[]{:S(2)}) collective-permute-start(f32[512,128]{1,0:T(8,128)} %get-tuple-element.13), channel_id=1, source_target_pairs={{0,64},{64,128},{128,192},{192,0},{1,65},{65,129},{129,193},{193,1... | collective-permute-start | bytes 786440 | tf_op jit(solution)/shard_map/ppermute | solution.py:337
  23.3 8.2 %collective-permute-start.1 = (f32[512,128]{1,0:T(8,128)}, f32[512,128]{1,0:T(8,128)S(1)}, u32[]{:S(2)}, u32[]{:S(2)}) collective-permute-start(f32[512,128]{1,0:T(8,128)} %get-tuple-element.14), channel_id=1, source_target_pairs={{0,192},{64,0},{128,64},{192,128},{1,193},{65,1},{129,65},{193,129... | collective-permute-start | bytes 786440 | tf_op jit(solution)/shard_map/ppermute | solution.py:338
  25.2 9.8 %collective-permute-start.6 = (f32[4,128]{1,0:T(4,128)S(1)}, f32[4,128]{1,0:T(4,128)S(1)}, u32[]{:S(2)}, u32[]{:S(2)}) collective-permute-start(f32[4,128]{1,0:T(4,128)S(1)} %slice_select_fusion.1), channel_id=1, source_target_pairs={{0,32},{16,48},{32,0},{48,16},{1,33},{17,49},{33,1},{49,17},{2,34}... | collective-permute-start | bytes 6152 | tf_op jit(solution)/shard_map/ppermute | solution.py:230
  31.5 8.6 %copy-start.1 = (f32[512,128]{1,0:T(8,128)}, f32[512,128]{1,0:T(8,128)S(1)}, u32[]{:S(2)}) copy-start(f32[512,128]{1,0:T(8,128)S(1)} %collective-permute-done) | copy-start | bytes 786436
  31.5 8.6 %copy-start.2 = (f32[512,128]{1,0:T(8,128)}, f32[512,128]{1,0:T(8,128)S(1)}, u32[]{:S(2)}) copy-start(f32[512,128]{1,0:T(8,128)S(1)} %collective-permute-done.1) | copy-start | bytes 786436
  32.7 4.3 %collective-permute-start.3 = (f32[256,128]{1,0:T(8,128)S(1)}, f32[256,128]{1,0:T(8,128)S(1)}, u32[]{:S(2)}, u32[]{:S(2)}) collective-permute-start(f32[256,128]{1,0:T(8,128)S(1)} %get-tuple-element.22), channel_id=1, source_target_pairs={{0,192},{64,0},{128,64},{192,128},{1,193},{65,1},{129,65},{193,129... | collective-permute-start | bytes 393224 | tf_op jit(solution)/shard_map/ppermute | solution.py:346
  35.0 5.0 %collective-permute-start.2 = (f32[256,128]{1,0:T(8,128)S(1)}, f32[256,128]{1,0:T(8,128)S(1)}, u32[]{:S(2)}, u32[]{:S(2)}) collective-permute-start(f32[256,128]{1,0:T(8,128)S(1)} %get-tuple-element.23), channel_id=1, source_target_pairs={{0,64},{64,128},{128,192},{192,0},{1,65},{65,129},{129,193},{193,1... | collective-permute-start | bytes 393224 | tf_op jit(solution)/shard_map/ppermute | solution.py:345
  37.0 3.1 %copy-start.3 = (f32[256,128]{1,0:T(8,128)}, f32[256,128]{1,0:T(8,128)S(1)}, u32[]{:S(2)}) copy-start(f32[256,128]{1,0:T(8,128)S(1)} %collective-permute-done.3) | copy-start | bytes 393220
  40.0 0.7 copy-start.4
  46.2 25.8 %all-to-all-start = ((f32[64,8,128]{2,1,0:T(8,128)}), f32[64,8,128]{2,1,0:T(8,128)S(1)}, u32[]{:S(2)}, u32[]{:S(2)}) async-start(f32[64,8,128]{2,1,0:T(8,128)} %get-tuple-element.18), calls=%async_computation | async-start | bytes 524288 | tf_op jit(solution)/shard_map/all_to_all | solution.py:361
  72.0 0.7 copy-start

commit v3 on v2

v3 whole, which is shorter than its diff:
```python
import math

import jax
import jax.numpy as jnp
import numpy as np
from jax import lax
from jax.experimental import pallas as pl
from jax.experimental.pallas import tpu as pltpu
from jax.sharding import Mesh, PartitionSpec as P

SPACE = ("y", "z", "core")
LANES = 128
BLK = 8
UP = ((2, 0), (2, 1), (1, 2), (1, 3))
DOWN = ((2, 2), (2, 3), (3, 0), (3, 1))
KEEP = ((1, 0), (1, 1), (3, 2), (3, 3))
OWN = ((0, 0), (0, 1), (0, 2), (0, 3))
ORDER = UP + DOWN + KEEP + OWN


def fold(v, axis):
    shape = v.shape
    lead, tiles = shape[:-2], shape[-1] // LANES
    v = v.reshape(*lead, 2, tiles, LANES)
    return jnp.swapaxes(v, axis, axis + 1).reshape(*lead, 2 * tiles, LANES)


def unfold(v, axis):
    lead, rows = v.shape[:-2], v.shape[-2]
    v = v.reshape(*lead, rows // 2, 2, LANES)
    return jnp.swapaxes(v, axis, axis + 1).reshape(*lead, 2, rows // 2 * LANES)


def split3(v):
    hi = v.astype(jnp.bfloat16)
    rest = v - hi.astype(jnp.float32)
    mid = rest.astype(jnp.bfloat16)
    low = (rest - mid.astype(jnp.float32)).astype(jnp.bfloat16)
    return hi, mid, low


def transform_kernel(total, chunks, bins_ref, place_ref, x_hbm, *refs):
    *out_refs, x_ref, sems = refs
    slice_len, rows, _ = x_ref.shape
    piece = rows // chunks
    copies = [
        pltpu.make_async_copy(x_hbm.at[:, pl.ds(c * piece, piece)], x_ref.at[:, pl.ds(c * piece, piece)], sems.at[c])
        for c in range(chunks)
    ]
    for copy in copies:
        copy.start()
    n = 2 * len(ORDER)
    place = place_ref[0]
    row = lax.broadcasted_iota(jnp.int32, (n, slice_len), 0)
    t = lax.broadcasted_iota(jnp.int32, (n, slice_len), 1) + place * slice_len
    which = jnp.zeros((n, slice_len), jnp.int32)
    for i, (ahead, b) in enumerate(ORDER):
        which = jnp.where(row // 2 == i, bins_ref[((place + ahead) % 4) * 4 + b], which)
    phase = (which * t + (row % 2) * (total // 4)) % total
    step = 2.0 * math.pi / total
    window = 0.5 - 0.5 * jnp.cos(step * t.astype(jnp.float32))
    table = jnp.cos(step * phase.astype(jnp.float32)) * window * math.sqrt(8.0 / (3.0 * total))
    t_hi = table.astype(jnp.bfloat16)
    t_lo = (table - t_hi.astype(jnp.float32)).astype(jnp.bfloat16)
    left = jnp.concatenate([t_hi, t_lo], axis=0)
    left = jnp.concatenate([left, left], axis=1)
    each = n // len(out_refs)
    for at in range(0, rows, 8):
        if at % piece == 0:
            copies[at // piece].wait()
        x8 = jnp.swapaxes(x_ref[:, at:at + 8, :], 0, 1)
        got = []
        for r in range(0, 8, 2):
            x = jnp.concatenate([x8[r], x8[r + 1]], axis=1)
            hi = x.astype(jnp.bfloat16)
            lo = (x - hi.astype(jnp.float32)).astype(jnp.bfloat16)
            res = jnp.dot(left, jnp.concatenate([hi, lo], axis=0), preferred_element_type=jnp.float32)
            res = res[:n] + res[n:]
            got += [res[:, :LANES], res[:, LANES:]]
        got = jnp.swapaxes(jnp.stack(got, axis=0), 0, 1)
        for i, out_ref in enumerate(out_refs):
            out_ref[:, at:at + 8, :] = got[i * each:(i + 1) * each]


def gram_kernel(core_ref, u_hbm, send_ref, keep_ref, all_ref, u_ref, sems):
    nb, _, rank, rows, _ = u_ref.shape
    n = 2 * rank

    def load(b):
        return pltpu.make_async_copy(u_hbm.at[b], u_ref.at[b], sems.at[b])

    for b in range(nb):
        load(b).start()

    def one(b, carry):
        load(b).wait()
        vv = jnp.zeros((n, n), jnp.float32)
        for at in range(0, rows, 16):
            u = u_ref[b, :, :, at:at + 16, :].reshape(n, 16, LANES)
            u = jnp.swapaxes(u, 0, 1)
            for r in range(0, 16, 4):
                v = jnp.concatenate([u[r + k] for k in range(4)], axis=1)
                vv = vv + lax.dot_general(v, v, (((1,), (1,)), ((), ())), preferred_element_type=jnp.float32)
        h_re = vv[:rank, :rank] + vv[rank:, rank:]
        h_im = vv[:rank, rank:] - vv[rank:, :rank]
        j = lax.broadcasted_iota(jnp.int32, (rank, rank), 0)
        k = lax.broadcasted_iota(jnp.int32, (rank, rank), 1)
        all_ref[b] = jnp.where(j <= k, h_re, h_im)
        return carry

    lax.fori_loop(0, nb, one, 0)
    h = jnp.concatenate([all_ref[i] for i in range(nb)], axis=1)
    low, high = h[:rank // 2], h[rank // 2:]
    first = core_ref[0] == 0
    send_ref[...] = jnp.where(first, high, low)
    keep_ref[...] = jnp.where(first, low, high)


def project_kernel(own_ref, a_ref, b_ref, c_ref, d_ref, u_hbm, h_ref, s_ref, blk_ref, acc_ref, u_ref, sems):
    nb, _, rank, rows, _ = u_ref.shape
    loads = [pltpu.make_async_copy(u_hbm.at[b], u_ref.at[b], sems.at[b]) for b in range(nb)]
    for load in loads:
        load.start()
    half = nb // 2
    used = nb * (2 * rank + 1) * 8
    acc_ref[pl.ds(used, acc_ref.shape[0] - used), :] = jnp.zeros((acc_ref.shape[0] - used, LANES), jnp.float32)

    def eight(v):
        return v.reshape(rows // 8, 8, LANES).sum(axis=0)

    for b in range(nb):
        at = 2 * b
        s = []
        for k in (at, at + 1):
            if b < half:
                s.append(own_ref[k] + b_ref[k + nb] + c_ref[k])
            else:
                s.append(own_ref[k] + a_ref[k] + d_ref[k - nb])
        s_re, s_im = s
        s_ref[b, 0] = s_re
        s_ref[b, 1] = s_im
        acc_ref[pl.ds((2 * nb * rank + b) * 8, 8), :] = eight(s_re * s_re + s_im * s_im)
        loads[b].wait()

        def body(j, carry, b=b, s_re=s_re, s_im=s_im):
            u_re = u_ref[b, 0, j].astype(jnp.float32)
            u_im = u_ref[b, 1, j].astype(jnp.float32)
            at = (b * 2 * rank + j) * 8
            acc_ref[pl.ds(pl.multiple_of(at, 8), 8), :] = eight(u_re * s_re + u_im * s_im)
            acc_ref[pl.ds(pl.multiple_of(at + rank * 8, 8), 8), :] = eight(u_re * s_im - u_im * s_re)
            return carry

        lax.fori_loop(0, rank, body, 0, unroll=4)

    n = acc_ref.shape[0] // 8
    x = acc_ref[pl.ds(0, n, stride=8), :]
    for k in range(1, 8):
        x = x + acc_ref[pl.ds(k, n, stride=8), :]
    ones = jnp.ones((8, LANES), jnp.bfloat16)
    sums = sum(
        lax.dot_general(ones, v, (((1,), (1,)), ((), ())), preferred_element_type=jnp.float32)
        for v in split3(x)
    )
    blk = jnp.concatenate(
        [sums[0:1, k * LANES:(k + 1) * LANES] for k in range(3)]
        + [h_ref[...], jnp.zeros((1, LANES), jnp.float32)],
        axis=0,
    )
    blk_ref[...] = jnp.broadcast_to(blk[None], blk_ref.shape)


def update_kernel(parts, count_ref, g_ref, pick_ref, eig_ref, s_ref, u_hbm, out_hbm, coh_ref, coef_ref, u_ref, out_ref, in_sems, sems):
    nb, _, rank, rows, _ = u_ref.shape
    loads = [pltpu.make_async_copy(u_hbm.at[b], u_ref.at[b], in_sems.at[b]) for b in range(nb)]
    for load in loads:
        load.start()

    def coefficients():
        count = jnp.full((1, 1), count_ref[0], jnp.int32).astype(jnp.float32)
        w_old = count / (count + 1.0)
        w_new = 1.0 / (count + 1.0)
        pick = pick_ref[...]
        sums = sum(jnp.dot(pick, v, preferred_element_type=jnp.float32) for v in split3(g_ref[...]))
        g = sums[BLK:]
        g_t = g.T
        j = lax.broadcasted_iota(jnp.int32, (rank, rank), 0)
        k = lax.broadcasted_iota(jnp.int32, (rank, rank), 1)
        eye = j == k

        def col(v):
            return jnp.where(eye, v, 0.0).sum(axis=1, keepdims=True)

        for i in range(nb):
            at = (i % 2) * 2 * rank
            cr = sums[i // 2:i // 2 + 1, at:at + rank]
            ci = sums[i // 2:i // 2 + 1, at + rank:at + 2 * rank]
            power = sums[2:3, i:i + 1]
            a = w_old * eig_ref[i:i + 1, :]
            cr_c, ci_c, a_c = col(cr), col(ci), col(a)
            p = g[:, i * rank:(i + 1) * rank]
            p_t = g_t[i * rank:(i + 1) * rank, :]
            h_re = jnp.where(j <= k, p, p_t)
            h_im = jnp.where(j > k, p, jnp.where(eye, 0.0, -p_t))
            both = w_new * (a_c + a + w_new * power)
            gram_re = a_c * a * h_re + (cr_c * cr + ci_c * ci) * both
            gram_im = a_c * a * h_im + (ci_c * cr - cr_c * ci) * both
            diag = jnp.where(eye, gram_re, 0.0)
            inv_c = 1.0 / jnp.sqrt(diag.sum(axis=1, keepdims=True) + 1e-06)
            inv_r = 1.0 / jnp.sqrt(diag.sum(axis=0, keepdims=True) + 1e-06)
            coh_ref[i, 0] = gram_re * inv_c * inv_r
            coh_ref[i, 1] = gram_im * inv_c * inv_r
            for m, v in enumerate((a_c * inv_c, w_new * cr_c * inv_c, w_new * ci_c * inv_c)):
                coef_ref[pl.ds((m * nb + i) * rank, rank), :] = jnp.broadcast_to(v, (rank, LANES))

    coefficients()
    block = rank // parts
    copies = []
    for b in range(nb):
        loads[b].wait()
        s_re, s_im = s_ref[b, 0], s_ref[b, 1]

        def body(j, carry, b=b, s_re=s_re, s_im=s_im):
            def coef(m):
                one = coef_ref[pl.ds((m * nb + b) * rank + j, 1), :]
                return jnp.broadcast_to(one, (rows, LANES))

            alpha, beta, gamma = coef(0), coef(1), coef(2)
            u_re = u_ref[b, 0, j].astype(jnp.float32)
            u_im = u_ref[b, 1, j].astype(jnp.float32)
            out_ref[b, 0, j] = (alpha * u_re + (beta * s_re + gamma * s_im)).astype(out_ref.dtype)
            out_ref[b, 1, j] = (alpha * u_im + (beta * s_im - gamma * s_re)).astype(out_ref.dtype)
            return carry

        for part in range(parts):
            lax.fori_loop(part * block, (part + 1) * block, body, 0, unroll=4)
            at = pl.ds(part * block, block)
            copy = pltpu.make_async_copy(out_ref.at[b, :, at], out_hbm.at[b, :, at], sems.at[b * parts + part])
            copy.start()
            copies.append(copy)
    for copy in copies:
        copy.wait()


def pick_table(rank):
    m = np.zeros((BLK + rank, 64 * BLK), np.float32)
    for s in range(64):
        y, core = s // 16, s % 2
        for k in range(3):
            m[k, s * BLK + k] = 1.0
        for i in range(4):
            m[BLK + core * 16 + y * 4 + i, s * BLK + 3 + i] = 1.0
    return jnp.asarray(m, jnp.bfloat16)


def trade(v, axis, mask):
    n = lax.axis_size(axis)
    return lax.ppermute(v, axis, [(i, i ^ mask) for i in range(n)])


SMEM = pl.BlockSpec(memory_space=pltpu.SMEM)
VMEM = pl.BlockSpec(memory_space=pltpu.VMEM)
HBM = pl.BlockSpec(memory_space=pltpu.HBM)


def room(kib):
    return pltpu.CompilerParams(vmem_limit_bytes=kib * 1024)


def call_transform(bins, place, x, total, chunks=4):
    slice_len, rows, _ = x.shape
    n = 2 * len(ORDER)
    return pl.pallas_call(
        lambda *refs: transform_kernel(total, chunks, *refs),
        out_shape=[jax.ShapeDtypeStruct((n // 4, rows, LANES), jnp.float32)] * 4,
        in_specs=[SMEM, SMEM, HBM],
        out_specs=[VMEM] * 4,
        scratch_shapes=[pltpu.VMEM(x.shape, jnp.float32), pltpu.SemaphoreType.DMA((chunks,))],
        compiler_params=room(53500),
        name="transform",
    )(bins, place, x)


def call_gram(core, u):
    nb, _, rank, rows, _ = u.shape
    return pl.pallas_call(
        gram_kernel,
        out_shape=[jax.ShapeDtypeStruct((rank // 2, nb * rank), jnp.float32)] * 2,
        in_specs=[SMEM, HBM],
        out_specs=[VMEM] * 2,
        scratch_shapes=[
            pltpu.VMEM((nb, rank, rank), jnp.float32),
            pltpu.VMEM(u.shape, u.dtype),
            pltpu.SemaphoreType.DMA((nb,)),
        ],
        compiler_params=room(52000),
        cost_estimate=pl.CostEstimate(flops=4 * 10**9, bytes_accessed=u.size * 2, transcendentals=0),
        name="gram",
    )(core, u)


def call_project(own, a, b, c, d, u, h, n_space):
    nb, _, rank, rows, _ = u.shape
    return pl.pallas_call(
        project_kernel,
        out_shape=(
            jax.ShapeDtypeStruct((nb, 2, rows, LANES), jnp.float32),
            jax.ShapeDtypeStruct((n_space, BLK, LANES), jnp.float32),
        ),
        in_specs=[VMEM] * 5 + [HBM, VMEM],
        out_specs=(VMEM, VMEM),
        scratch_shapes=[
            pltpu.VMEM((3 * LANES * 8, LANES), jnp.float32),
            pltpu.VMEM(u.shape, u.dtype),
            pltpu.SemaphoreType.DMA((nb,)),
        ],
        compiler_params=room(52000),
        cost_estimate=pl.CostEstimate(flops=16 * u.size, bytes_accessed=u.size * 2, transcendentals=0),
        name="project",
    )(own, a, b, c, d, u, h)


def call_update(block_count, g, eigenvalues, spec, u, parts=2):
    nb, _, rank, rows, _ = u.shape
    return pl.pallas_call(
        lambda *refs: update_kernel(parts, *refs),
        out_shape=(
            jax.ShapeDtypeStruct(u.shape, jnp.bfloat16),
            jax.ShapeDtypeStruct((nb, 2, rank, rank), jnp.float32),
        ),
        in_specs=[SMEM] + [VMEM] * 4 + [HBM],
        out_specs=(HBM, VMEM),
        scratch_shapes=[
            pltpu.VMEM((3 * nb * rank, LANES), jnp.float32),
            pltpu.VMEM(u.shape, u.dtype),
            pltpu.VMEM(u.shape, u.dtype),
            pltpu.SemaphoreType.DMA((nb,)),
            pltpu.SemaphoreType.DMA((nb * parts,)),
        ],
        compiler_params=room(52000),
        name="update",
    )(block_count, g, pick_table(rank), eigenvalues, spec, u)


def local(snapshots, bins, eigenvalues, old_basis, block_count):
    slice_len = snapshots.shape[0]
    groups = lax.axis_size("ta")
    total = slice_len * groups
    nb = old_basis.shape[0]
    n_space = lax.axis_size(SPACE)
    place = lax.axis_index("ta").astype(jnp.int32).reshape(1)
    core = lax.axis_index("core").astype(jnp.int32).reshape(1)
    y = lax.axis_index("y")

    up, down, keep, own = call_transform(bins, place, fold(snapshots, 1), total)
    ring_up = [(i, (i + 1) % groups) for i in range(groups)]
    ring_down = [(i, (i - 1) % groups) for i in range(groups)]
    a = lax.ppermute(up, "ta", ring_up)
    b = lax.ppermute(down, "ta", ring_down)

    u = fold(old_basis, 3)
    u, _ = lax.optimization_barrier((u, up))
    send, kept = call_gram(core, u)

    h = kept + trade(send, "core", 1)

    c, d = keep[:nb] + a[:nb], keep[nb:] + b[:nb]
    c, d, h = lax.optimization_barrier((c, d, h))
    c = lax.ppermute(c, "ta", ring_up)
    d = lax.ppermute(d, "ta", ring_down)

    n = h.shape[0] // 4
    h = h.reshape(4, n, h.shape[1])
    quarter = [lax.dynamic_index_in_dim(h, y ^ k, 0, keepdims=False) for k in range(4)]
    h = quarter[0] + trade(quarter[1], "y", 1) + trade(quarter[2], "y", 2) + trade(quarter[3], "y", 3)

    spec, blk = call_project(own, a, b, c, d, u, h, n_space)
    g = lax.all_to_all(blk, SPACE, 0, 0, tiled=True).reshape(n_space * BLK, LANES)
    fresh, coherence = call_update(block_count, g, eigenvalues, spec, u)
    return unfold(fresh, 3), coherence


def solution(mesh):
    inner = Mesh(mesh.devices.reshape(4, 4, 8, 2), ("ta",) + SPACE)
    return jax.shard_map(
        local,
        mesh=inner,
        in_specs=(P("ta", None, SPACE), P(), P("ta", None), P("ta", None, None, None, SPACE), P()),
        out_specs=(P("ta", None, None, None, SPACE), P("ta", None, None, None)),
        check_vma=False,
    )
```

time: 81.6 us -> 60.6 us (0.74)
  Pallas kernels: 30.7 us -> 16 us
  waiting for transfers between devices: 20.9 us -> 15.4 us
  starting transfers between devices: 24.3 us -> 27 us
  other arithmetic: 2.48 us -> 0.04 us
    pallas_call x4, Pallas kernels: 30.7 us -> 16 us  [the longest x1 4.73 us: call_update(): pl.pallas_call(lambda *refs: update_kernel(parts, *refs), out_shape=(jax....]
    ppermute x1, waiting for transfers between devices: 4.02 us -> 0.88 us  [local(): a = lax.ppermute(up, 'ta', ring_up)]
    ppermute x2, waiting for transfers between devices: 4.44 us -> 1.81 us  [the longest x1 1.8 us: local(): c = lax.ppermute(c, 'ta', ring_up)]
    add x3 -> x2, other arithmetic: 1.77 us -> 0.04 us  [the longest x1 0.03 us: local(): c, d = (keep[:nb] + a[:nb], keep[nb:] + b[:nb])]
    ppermute x1, starting transfers between devices: 1.91 us -> 3.39 us  [local(): b = lax.ppermute(down, 'ta', ring_down)]
    all_to_all x1, starting transfers between devices: 13.8 us -> 14.9 us  [local(): lax.all_to_all(blk, SPACE, 0, 0, tiled=True).reshape(n_space * BLK, LANES)]
    ppermute x3 -> x4, starting transfers between devices: 5.5 us -> 6.04 us  [trade(): return lax.ppermute(v, axis, [(i, i ^ mask) for i in range(n)])]
  transfers between devices with their start and end apart: 8 -> 9, of which waited for: 5 -> 5; matrix products, arithmetic and copies ran while one was open for 2% -> 0% of each run, Pallas kernels for 6% -> 7%
where the time goes in v3:
time: 60.6 us; the launch traced here: 60.4 us
  starting transfers between devices  27 us (45%)
  Pallas kernels  16 us (26%)
  waiting for transfers between devices  15.4 us (25%)
  between operations  1.36 us (2%)
  local copies, waits for them, and re-layouts  0.67 us (1%)
    all_to_all x1, starting transfers between devices, local(): lax.all_to_all(blk, SPACE, 0, 0, tiled=True).reshape(n_space * BLK, LANES)  14.9 us
    all_to_all x1, waiting for transfers between devices, local(): lax.all_to_all(blk, SPACE, 0, 0, tiled=True).reshape(n_space * BLK, LANES)  11.4 us
    ppermute x4, starting transfers between devices, trade(): return lax.ppermute(v, axis, [(i, i ^ mask) for i in range(n)])  6.04 us
    pallas_call x1, Pallas kernels, call_update(): pl.pallas_call(lambda *refs: update_kernel(parts, *refs), out_shape=(jax....  4.73 us
    pallas_call x1, Pallas kernels, call_gram(): pl.pallas_call(gram_kernel, out_shape=[jax.ShapeDtypeStruct((rank // 2, n...  4.27 us
    pallas_call x1, Pallas kernels, call_project(): pl.pallas_call(project_kernel, out_shape=(jax.ShapeDtypeStruct((nb, 2, ro...  3.94 us
    ppermute x1, starting transfers between devices, local(): b = lax.ppermute(down, 'ta', ring_down)  3.39 us
    pallas_call x1, Pallas kernels, call_transform(): pl.pallas_call(lambda *refs: transform_kernel(total, chunks, *refs), out_...  3.02 us
  transfers between devices with their start and end apart: 9, of which 5 were waited for; matrix products, arithmetic and copies ran while one was open for 0% of the time, Pallas kernels for 7%

profile of v3, /device:TPU:1, one launch (start us, length us, event | category | flops | bytes accessed | tf_op | source)
XLA Modules:
  0.0 60.4 jit_solution(2321700186608698730)
XLA Ops:
  0.6 0.0 copy-start.2
  0.6 0.6 %copy-done.2 = s32[16]{0:T(128)S(1)} copy-done((s32[16]{0:T(128)S(1)}, s32[16]{0:T(128)}, u32[]{:S(2)}) %copy-start.2) | copy-done | bytes 88
  1.3 3.0 %transform.1 = (f32[8,64,128]{2,1,0:T(8,128)S(1)}, f32[8,64,128]{2,1,0:T(8,128)S(1)}, f32[8,64,128]{2,1,0:T(8,128)S(1)}, f32[8,64,128]{2,1,0:T(8,128)S(1)}) custom-call(s32[16]{0:T(128)S(1)} %copy-done.2, s32[1]{0:T(128)} %bitcast.refs_1_, f32[64,64,128]{2,1,0:T(8,128)} %bitcast.35), custom_call_target="tpu_custom_call" | custom-call | tf_op jit(solution)/shard_map/transform/pallas_call | solution.py:272
  4.3 3.4 %collective-permute-start.1 = (f32[8,64,128]{2,1,0:T(8,128)S(1)}, f32[8,64,128]{2,1,0:T(8,128)S(1)}, u32[]{:S(2)}, u32[]{:S(2)}) collective-permute-start(f32[8,64,128]{2,1,0:T(8,128)S(1)} %get-tuple-element.18), channel_id=1, source_target_pairs={{0,192},{64,0},{128,64},{192,128},{1,193},{65,1},{129,65},{193,129... | collective-permute-start | bytes 786440 | tf_op jit(solution)/shard_map/ppermute | solution.py:358
  7.7 0.0 collective-permute-start
  7.7 4.3 %gram.1 = (f32[16,128]{1,0:T(8,128)S(1)}, f32[16,128]{1,0:T(8,128)S(1)}) custom-call(s32[1]{0:T(128)} %bitcast.4.core_ref, bf16[4,2,32,64,128]{4,3,2,1,0:T(8,128)(2,1)} %bitcast.32), custom_call_target="tpu_custom_call" | custom-call | flops 4000000000 | bytes 4194304 | tf_op jit(solution)/shard_map/gram/pallas_call | solution.py:285
  12.0 0.0 copy-start
  12.0 0.0 copy-start.1
  12.0 2.0 %collective-permute-start.2 = (f32[16,128]{1,0:T(8,128)S(1)}, f32[16,128]{1,0:T(8,128)S(1)}, u32[]{:S(2)}, u32[]{:S(2)}) collective-permute-start(f32[16,128]{1,0:T(8,128)S(1)} %get-tuple-element.22), channel_id=1, source_target_pairs={{0,1},{1,0},{2,3},{3,2},{4,5},{5,4},{6,7},{7,6},{8,9},{9,8},{10,11... | collective-permute-start | bytes 24584 | tf_op jit(solution)/shard_map/ppermute | solution.py:257
  14.1 0.8 %collective-permute-done.2 = f32[16,128]{1,0:T(8,128)S(1)} collective-permute-done((f32[16,128]{1,0:T(8,128)S(1)}, f32[16,128]{1,0:T(8,128)S(1)}, u32[]{:S(2)}, u32[]{:S(2)}) %collective-permute-start.2) | collective-permute-done | bytes 8224 | tf_op jit(solution)/shard_map/ppermute | solution.py:257
  14.9 0.0 collective-permute-done.1.b_ref
  14.9 0.9 %collective-permute-done.a_ref = f32[8,64,128]{2,1,0:T(8,128)S(1)} collective-permute-done((f32[8,64,128]{2,1,0:T(8,128)S(1)}, f32[8,64,128]{2,1,0:T(8,128)S(1)}, u32[]{:S(2)}, u32[]{:S(2)}) %collective-permute-start) | collective-permute-done | bytes 262176 | tf_op jit(solution)/shard_map/ppermute | solution.py:357
  15.8 1.4 %collective-permute-start.5 = (f32[4,128]{1,0:T(4,128)S(1)}, f32[4,128]{1,0:T(4,128)S(1)}, u32[]{:S(2)}, u32[]{:S(2)}) collective-permute-start(f32[4,128]{1,0:T(4,128)S(1)} %get-tuple-element.32), channel_id=1, source_target_pairs={{0,16},{16,0},{32,48},{48,32},{1,17},{17,1},{33,49},{49,33},{2,18}... | collective-permute-start | bytes 6152 | tf_op jit(solution)/shard_map/ppermute | solution.py:257
  17.2 1.9 %collective-permute-start.7 = (f32[4,128]{1,0:T(4,128)S(1)}, f32[4,128]{1,0:T(4,128)S(1)}, u32[]{:S(2)}, u32[]{:S(2)}) collective-permute-start(f32[4,128]{1,0:T(4,128)S(1)} %get-tuple-element.33), channel_id=1, source_target_pairs={{0,48},{16,32},{32,16},{48,0},{1,49},{17,33},{33,17},{49,1},{2,50}... | collective-permute-start | bytes 6152 | tf_op jit(solution)/shard_map/ppermute | solution.py:257
  19.1 0.7 %collective-permute-start.6 = (f32[4,128]{1,0:T(4,128)S(1)}, f32[4,128]{1,0:T(4,128)S(1)}, u32[]{:S(2)}, u32[]{:S(2)}) collective-permute-start(f32[4,128]{1,0:T(4,128)S(1)} %get-tuple-element.34), channel_id=1, source_target_pairs={{0,32},{16,48},{32,0},{48,16},{1,33},{17,49},{33,1},{49,17},{2,34}... | collective-permute-start | bytes 6152 | tf_op jit(solution)/shard_map/ppermute | solution.py:257
  19.8 0.0 collective-permute-start.3
  19.8 2.7 %collective-permute-start.4 = (f32[4,64,128]{2,1,0:T(8,128)S(1)}, f32[4,64,128]{2,1,0:T(8,128)S(1)}, u32[]{:S(2)}, u32[]{:S(2)}) collective-permute-start(f32[4,64,128]{2,1,0:T(8,128)S(1)} %get-tuple-element.24), channel_id=1, source_target_pairs={{0,192},{64,0},{128,64},{192,128},{1,193},{65,1},{129,65},{193,129... | collective-permute-start | bytes 393224 | tf_op jit(solution)/shard_map/ppermute | solution.py:369
  22.5 0.0 collective-permute-done.5
  22.5 0.0 collective-permute-done.7
  22.5 0.5 collective-permute-done.6
  23.1 1.8 %collective-permute-done.3.c_ref = f32[4,64,128]{2,1,0:T(8,128)S(1)} collective-permute-done((f32[4,64,128]{2,1,0:T(8,128)S(1)}, f32[4,64,128]{2,1,0:T(8,128)S(1)}, u32[]{:S(2)}, u32[]{:S(2)}) %collective-permute-start.3) | collective-permute-done | bytes 131104 | tf_op jit(solution)/shard_map/ppermute | solution.py:368
  24.9 0.0 collective-permute-done.4.d_ref
  24.9 3.9 %project.1 = (f32[4,2,64,128]{3,2,1,0:T(8,128)S(1)}, f32[64,8,128]{2,1,0:T(8,128)}) custom-call(f32[8,64,128]{2,1,0:T(8,128)S(1)} %get-tuple-element.16.own_ref, f32[8,64,128]{2,1,0:T(8,128)S(1)} %collective-permute-done.a_ref, f32[8,64,128]{2,1,0:T(8,128)S(1)} %collective-permute-done.1.b_ref, f32[4,64,128]{2,1,0:T(8,128)S(1)} %collective-permute-done.3.c_ref, ...), custom_call_target="tpu_custom_call" | custom-call | flops 33554432 | bytes 4194304 | tf_op jit(solution)/shard_map/project/pallas_call | solution.py:303
  28.8 14.9 %all-to-all-start = ((f32[64,8,128]{2,1,0:T(8,128)}), f32[64,8,128]{2,1,0:T(8,128)S(1)}, u32[]{:S(2)}, u32[]{:S(2)}) async-start(f32[64,8,128]{2,1,0:T(8,128)} %get-tuple-element.26), calls=%async_computation | async-start | bytes 524288 | tf_op jit(solution)/shard_map/all_to_all | solution.py:377
  44.3 11.4 %all-to-all-done = f32[64,8,128]{2,1,0:T(8,128)S(1)} async-done(((f32[64,8,128]{2,1,0:T(8,128)}), f32[64,8,128]{2,1,0:T(8,128)S(1)}, u32[]{:S(2)}, u32[]{:S(2)}) %all-to-all-start) | async-done | bytes 262176 | tf_op jit(solution)/shard_map/all_to_all | solution.py:377
  55.7 0.0 copy-done
  55.7 0.0 copy-done.1
  55.7 4.7 %update.1 = (bf16[4,2,32,64,128]{4,3,2,1,0:T(8,128)(2,1)}, f32[4,2,32,32]{3,2,1,0:T(8,128)}) custom-call(s32[1]{0:T(128)S(6)} %copy.11.refs_0_, f32[512,128]{1,0:T(8,128)S(1)} %bitcast.31, bf16[40,512]{1,0:T(8,128)(2,1)S(1)} %copy-done, f32[4,32]{1,0:T(4,128)S(1)} %copy-done.1, f32[4,2,64,128]{3,2,1,0:T(8,128)S(1)} %get-tuple-element.27.refs_4_, ...), custom_call_target="tpu_custom_call" | custom-call | tf_op jit(solution)/shard_map/update/pallas_call | solution.py:324
  (4 shorter events, 0.1 us)
Async XLA Ops:
  0.6 0.7 %copy-start.2 = (s32[16]{0:T(128)S(1)}, s32[16]{0:T(128)}, u32[]{:S(2)}) copy-start(s32[16]{0:T(128)} %refs_0_.2) | copy-start | bytes 196
  4.3 10.6 %collective-permute-start.1 = (f32[8,64,128]{2,1,0:T(8,128)S(1)}, f32[8,64,128]{2,1,0:T(8,128)S(1)}, u32[]{:S(2)}, u32[]{:S(2)}) collective-permute-start(f32[8,64,128]{2,1,0:T(8,128)S(1)} %get-tuple-element.18), channel_id=1, source_target_pairs={{0,192},{64,0},{128,64},{192,128},{1,193},{65,1},{129,65},{193,129... | collective-permute-start | bytes 786440 | tf_op jit(solution)/shard_map/ppermute | solution.py:358
  7.7 8.1 %collective-permute-start = (f32[8,64,128]{2,1,0:T(8,128)S(1)}, f32[8,64,128]{2,1,0:T(8,128)S(1)}, u32[]{:S(2)}, u32[]{:S(2)}) collective-permute-start(f32[8,64,128]{2,1,0:T(8,128)S(1)} %get-tuple-element.17), channel_id=1, source_target_pairs={{0,64},{64,128},{128,192},{192,0},{1,65},{65,129},{129,193},{193,1... | collective-permute-start | bytes 786440 | tf_op jit(solution)/shard_map/ppermute | solution.py:357
  12.0 43.7 %copy-start = (bf16[40,512]{1,0:T(8,128)(2,1)S(1)}, bf16[40,512]{1,0:T(8,128)(2,1)}, u32[]{:S(2)}) copy-start(bf16[40,512]{1,0:T(8,128)(2,1)} %constant.34.clone.refs_2_) | copy-start | bytes 122884
  12.0 43.7 %copy-start.1 = (f32[4,32]{1,0:T(4,128)S(1)}, f32[4,32]{1,0:T(4,128)}, u32[]{:S(2)}) copy-start(f32[4,32]{1,0:T(4,128)} %refs_3_.1) | copy-start | bytes 1540
  12.0 2.9 %collective-permute-start.2 = (f32[16,128]{1,0:T(8,128)S(1)}, f32[16,128]{1,0:T(8,128)S(1)}, u32[]{:S(2)}, u32[]{:S(2)}) collective-permute-start(f32[16,128]{1,0:T(8,128)S(1)} %get-tuple-element.22), channel_id=1, source_target_pairs={{0,1},{1,0},{2,3},{3,2},{4,5},{5,4},{6,7},{7,6},{8,9},{9,8},{10,11... | collective-permute-start | bytes 24584 | tf_op jit(solution)/shard_map/ppermute | solution.py:257
  15.8 6.7 %collective-permute-start.5 = (f32[4,128]{1,0:T(4,128)S(1)}, f32[4,128]{1,0:T(4,128)S(1)}, u32[]{:S(2)}, u32[]{:S(2)}) collective-permute-start(f32[4,128]{1,0:T(4,128)S(1)} %get-tuple-element.32), channel_id=1, source_target_pairs={{0,16},{16,0},{32,48},{48,32},{1,17},{17,1},{33,49},{49,33},{2,18}... | collective-permute-start | bytes 6152 | tf_op jit(solution)/shard_map/ppermute | solution.py:257
  17.2 5.3 %collective-permute-start.7 = (f32[4,128]{1,0:T(4,128)S(1)}, f32[4,128]{1,0:T(4,128)S(1)}, u32[]{:S(2)}, u32[]{:S(2)}) collective-permute-start(f32[4,128]{1,0:T(4,128)S(1)} %get-tuple-element.33), channel_id=1, source_target_pairs={{0,48},{16,32},{32,16},{48,0},{1,49},{17,33},{33,17},{49,1},{2,50}... | collective-permute-start | bytes 6152 | tf_op jit(solution)/shard_map/ppermute | solution.py:257
  19.1 3.9 %collective-permute-start.6 = (f32[4,128]{1,0:T(4,128)S(1)}, f32[4,128]{1,0:T(4,128)S(1)}, u32[]{:S(2)}, u32[]{:S(2)}) collective-permute-start(f32[4,128]{1,0:T(4,128)S(1)} %get-tuple-element.34), channel_id=1, source_target_pairs={{0,32},{16,48},{32,0},{48,16},{1,33},{17,49},{33,1},{49,17},{2,34}... | collective-permute-start | bytes 6152 | tf_op jit(solution)/shard_map/ppermute | solution.py:257
  19.8 5.0 %collective-permute-start.3 = (f32[4,64,128]{2,1,0:T(8,128)S(1)}, f32[4,64,128]{2,1,0:T(8,128)S(1)}, u32[]{:S(2)}, u32[]{:S(2)}) collective-permute-start(f32[4,64,128]{2,1,0:T(8,128)S(1)} %get-tuple-element.23), channel_id=1, source_target_pairs={{0,64},{64,128},{128,192},{192,0},{1,65},{65,129},{129,193},{193,1... | collective-permute-start | bytes 393224 | tf_op jit(solution)/shard_map/ppermute | solution.py:368
  19.8 5.0 %collective-permute-start.4 = (f32[4,64,128]{2,1,0:T(8,128)S(1)}, f32[4,64,128]{2,1,0:T(8,128)S(1)}, u32[]{:S(2)}, u32[]{:S(2)}) collective-permute-start(f32[4,64,128]{2,1,0:T(8,128)S(1)} %get-tuple-element.24), channel_id=1, source_target_pairs={{0,192},{64,0},{128,64},{192,128},{1,193},{65,1},{129,65},{193,129... | collective-permute-start | bytes 393224 | tf_op jit(solution)/shard_map/ppermute | solution.py:369
  28.8 26.9 %all-to-all-start = ((f32[64,8,128]{2,1,0:T(8,128)}), f32[64,8,128]{2,1,0:T(8,128)S(1)}, u32[]{:S(2)}, u32[]{:S(2)}) async-start(f32[64,8,128]{2,1,0:T(8,128)} %get-tuple-element.26), calls=%async_computation | async-start | bytes 524288 | tf_op jit(solution)/shard_map/all_to_all | solution.py:377

commit v4 on v3

--- a/solution.py
+++ b/solution.py
@@ -10,7 +10,7 @@
 
 SPACE = ("y", "z", "core")
 LANES = 128
-BLK = 8
+BLK = 4
 UP = ((2, 0), (2, 1), (1, 2), (1, 3))
 DOWN = ((2, 2), (2, 3), (3, 0), (3, 1))
 KEEP = ((1, 0), (1, 1), (3, 2), (3, 3))
@@ -82,7 +82,7 @@
             out_ref[:, at:at + 8, :] = got[i * each:(i + 1) * each]
 
 
-def gram_kernel(core_ref, u_hbm, send_ref, keep_ref, all_ref, u_ref, sems):
+def gram_kernel(u_hbm, h_ref, all_ref, u_ref, sems):
     nb, _, rank, rows, _ = u_ref.shape
     n = 2 * rank
 
@@ -109,11 +109,7 @@
         return carry
 
     lax.fori_loop(0, nb, one, 0)
-    h = jnp.concatenate([all_ref[i] for i in range(nb)], axis=1)
-    low, high = h[:rank // 2], h[rank // 2:]
-    first = core_ref[0] == 0
-    send_ref[...] = jnp.where(first, high, low)
-    keep_ref[...] = jnp.where(first, low, high)
+    h_ref[...] = jnp.concatenate([all_ref[i] for i in range(nb)], axis=1)
 
 
 def project_kernel(own_ref, a_ref, b_ref, c_ref, d_ref, u_hbm, h_ref, s_ref, blk_ref, acc_ref, u_ref, sems):
@@ -163,7 +159,7 @@
     )
     blk = jnp.concatenate(
         [sums[0:1, k * LANES:(k + 1) * LANES] for k in range(3)]
-        + [h_ref[...], jnp.zeros((1, LANES), jnp.float32)],
+        + [h_ref[...].sum(axis=0, keepdims=True)],
         axis=0,
     )
     blk_ref[...] = jnp.broadcast_to(blk[None], blk_ref.shape)
@@ -181,7 +177,7 @@
         w_new = 1.0 / (count + 1.0)
         pick = pick_ref[...]
         sums = sum(jnp.dot(pick, v, preferred_element_type=jnp.float32) for v in split3(g_ref[...]))
-        g = sums[BLK:]
+        g = sums[8:]
         g_t = g.T
         j = lax.broadcasted_iota(jnp.int32, (rank, rank), 0)
         k = lax.broadcasted_iota(jnp.int32, (rank, rank), 1)
@@ -241,20 +237,13 @@
         copy.wait()
 
 
-def pick_table(rank):
-    m = np.zeros((BLK + rank, 64 * BLK), np.float32)
-    for s in range(64):
-        y, core = s // 16, s % 2
+def pick_table(rank, n_space):
+    m = np.zeros((8 + rank, n_space * BLK), np.float32)
+    for s in range(n_space):
         for k in range(3):
             m[k, s * BLK + k] = 1.0
-        for i in range(4):
-            m[BLK + core * 16 + y * 4 + i, s * BLK + 3 + i] = 1.0
+        m[8 + s * rank // n_space, s * BLK + 3] = 1.0
     return jnp.asarray(m, jnp.bfloat16)
-
-
-def trade(v, axis, mask):
-    n = lax.axis_size(axis)
-    return lax.ppermute(v, axis, [(i, i ^ mask) for i in range(n)])
 
 
 SMEM = pl.BlockSpec(memory_space=pltpu.SMEM)
@@ -280,13 +269,13 @@
     )(bins, place, x)
 
 
-def call_gram(core, u):
+def call_gram(u):
     nb, _, rank, rows, _ = u.shape
     return pl.pallas_call(
         gram_kernel,
-        out_shape=[jax.ShapeDtypeStruct((rank // 2, nb * rank), jnp.float32)] * 2,
-        in_specs=[SMEM, HBM],
-        out_specs=[VMEM] * 2,
+        out_shape=jax.ShapeDtypeStruct((rank, nb * rank), jnp.float32),
+        in_specs=[HBM],
+        out_specs=VMEM,
         scratch_shapes=[
             pltpu.VMEM((nb, rank, rank), jnp.float32),
             pltpu.VMEM(u.shape, u.dtype),
@@ -295,7 +284,7 @@
         compiler_params=room(52000),
         cost_estimate=pl.CostEstimate(flops=4 * 10**9, bytes_accessed=u.size * 2, transcendentals=0),
         name="gram",
-    )(core, u)
+    )(u)
 
 
 def call_project(own, a, b, c, d, u, h, n_space):
@@ -338,7 +327,7 @@
         ],
         compiler_params=room(52000),
         name="update",
-    )(block_count, g, pick_table(rank), eigenvalues, spec, u)
+    )(block_count, g, pick_table(rank, g.shape[0] // BLK), eigenvalues, spec, u)
 
 
 def local(snapshots, bins, eigenvalues, old_basis, block_count):
@@ -348,8 +337,6 @@
     nb = old_basis.shape[0]
     n_space = lax.axis_size(SPACE)
     place = lax.axis_index("ta").astype(jnp.int32).reshape(1)
-    core = lax.axis_index("core").astype(jnp.int32).reshape(1)
-    y = lax.axis_index("y")
 
     up, down, keep, own = call_transform(bins, place, fold(snapshots, 1), total)
     ring_up = [(i, (i + 1) % groups) for i in range(groups)]
@@ -359,19 +346,12 @@
 
     u = fold(old_basis, 3)
     u, _ = lax.optimization_barrier((u, up))
-    send, kept = call_gram(core, u)
-
-    h = kept + trade(send, "core", 1)
-
+    h = call_gram(u)
     c, d = keep[:nb] + a[:nb], keep[nb:] + b[:nb]
     c, d, h = lax.optimization_barrier((c, d, h))
     c = lax.ppermute(c, "ta", ring_up)
     d = lax.ppermute(d, "ta", ring_down)
-
-    n = h.shape[0] // 4
-    h = h.reshape(4, n, h.shape[1])
-    quarter = [lax.dynamic_index_in_dim(h, y ^ k, 0, keepdims=False) for k in range(4)]
-    h = quarter[0] + trade(quarter[1], "y", 1) + trade(quarter[2], "y", 2) + trade(quarter[3], "y", 3)
+    h = lax.all_to_all(h[:, None], ("y", "z"), 0, 0, tiled=True)[:, 0]
 
     spec, blk = call_project(own, a, b, c, d, u, h, n_space)
     g = lax.all_to_all(blk, SPACE, 0, 0, tiled=True).reshape(n_space * BLK, LANES)

time: 60.6 us -> 65.5 us (1.081)
  blocking collectives: 0 us -> 19.6 us
  starting transfers between devices: 27 us -> 14 us
  waiting for transfers between devices: 15.4 us -> 13.6 us
    all_to_all x0 -> x1, blocking collectives: none -> 19.6 us  [local(): h = lax.all_to_all(h[:, None], ('y', 'z'), 0, 0, tiled=True)[:, 0]]
    all_to_all x1, starting transfers between devices: 14.9 us -> 7.92 us  [local(): lax.all_to_all(blk, SPACE, 0, 0, tiled=True).reshape(n_space * BLK, LANES)]
    ppermute x4 -> x0, starting transfers between devices: 6.04 us -> none  [trade(): return lax.ppermute(v, axis, [(i, i ^ mask) for i in range(n)])]
    ppermute x1, waiting for transfers between devices: 0.88 us -> 3.09 us  [local(): a = lax.ppermute(up, 'ta', ring_up)]
    ppermute x1, waiting for transfers between devices: 1.8 us -> 0.01 us  [local(): c = lax.ppermute(c, 'ta', ring_up)]
    all_to_all x1, waiting for transfers between devices: 11.4 us -> 9.83 us  [local(): lax.all_to_all(blk, SPACE, 0, 0, tiled=True).reshape(n_space * BLK, LANES)]
    ppermute x4 -> x0, waiting for transfers between devices: 1.37 us -> none  [trade(): return lax.ppermute(v, axis, [(i, i ^ mask) for i in range(n)])]
    ppermute x1, waiting for transfers between devices: 0.01 us -> 0.66 us  [local(): b = lax.ppermute(down, 'ta', ring_down)]
  transfers between devices with their start and end apart: 9 -> 5, of which waited for: 5 -> 3; matrix products, arithmetic and copies ran while one was open for 0% -> 0% of each run, Pallas kernels for 7% -> 7%
where the time goes in v4:
time: 65.5 us; the launch traced here: 65.2 us
  blocking collectives  19.6 us (30%)
  Pallas kernels  15.9 us (24%)
  starting transfers between devices  14 us (21%)
  waiting for transfers between devices  13.6 us (21%)
  between operations  1.35 us (2%)
  local copies, waits for them, and re-layouts  0.66 us (1%)
    all_to_all x1, blocking collectives, local(): h = lax.all_to_all(h[:, None], ('y', 'z'), 0, 0, tiled=True)[:, 0]  19.6 us
    all_to_all x1, waiting for transfers between devices, local(): lax.all_to_all(blk, SPACE, 0, 0, tiled=True).reshape(n_space * BLK, LANES)  9.83 us
    all_to_all x1, starting transfers between devices, local(): lax.all_to_all(blk, SPACE, 0, 0, tiled=True).reshape(n_space * BLK, LANES)  7.92 us
    pallas_call x1, Pallas kernels, call_update(): pl.pallas_call(lambda *refs: update_kernel(parts, *refs), out_shape=(jax....  4.72 us
    pallas_call x1, Pallas kernels, call_gram(): pl.pallas_call(gram_kernel, out_shape=jax.ShapeDtypeStruct((rank, nb * ra...  4.27 us
    pallas_call x1, Pallas kernels, call_project(): pl.pallas_call(project_kernel, out_shape=(jax.ShapeDtypeStruct((nb, 2, ro...  3.9 us
    ppermute x1, starting transfers between devices, local(): b = lax.ppermute(down, 'ta', ring_down)  3.38 us
    ppermute x1, waiting for transfers between devices, local(): a = lax.ppermute(up, 'ta', ring_up)  3.09 us
  transfers between devices with their start and end apart: 5, of which 3 were waited for; matrix products, arithmetic and copies ran while one was open for 0% of the time, Pallas kernels for 7%

profile of v4, /device:TPU:1, one launch (start us, length us, event | category | flops | bytes accessed | tf_op | source)
XLA Modules:
  0.0 65.2 jit_solution(10003576239478114365)
XLA Ops:
  0.6 0.0 copy-start.2
  0.6 0.6 copy-done.2
  1.3 3.0 %transform.1 = (f32[8,64,128]{2,1,0:T(8,128)S(1)}, f32[8,64,128]{2,1,0:T(8,128)S(1)}, f32[8,64,128]{2,1,0:T(8,128)S(1)}, f32[8,64,128]{2,1,0:T(8,128)S(1)}) custom-call(s32[16]{0:T(128)S(1)} %copy-done.2, s32[1]{0:T(128)} %bitcast.refs_1_, f32[64,64,128]{2,1,0:T(8,128)} %bitcast.27), custom_call_target="tpu_custom_call" | custom-call | tf_op jit(solution)/shard_map/transform/pallas_call | solution.py:261
  4.3 3.4 %collective-permute-start.1 = (f32[8,64,128]{2,1,0:T(8,128)S(1)}, f32[8,64,128]{2,1,0:T(8,128)S(1)}, u32[]{:S(2)}, u32[]{:S(2)}) collective-permute-start(f32[8,64,128]{2,1,0:T(8,128)S(1)} %get-tuple-element.16), channel_id=1, source_target_pairs={{0,192},{64,0},{128,64},{192,128},{1,193},{65,1},{129,65},{193,129... | collective-permute-start | bytes 786440 | tf_op jit(solution)/shard_map/ppermute | solution.py:345
  7.7 0.0 collective-permute-start
  7.7 4.3 %gram.1 = f32[32,128]{1,0:T(8,128)S(1)} custom-call(bf16[4,2,32,64,128]{4,3,2,1,0:T(8,128)(2,1)} %bitcast.24), custom_call_target="tpu_custom_call" | custom-call | flops 4000000000 | bytes 4194304 | tf_op jit(solution)/shard_map/gram/pallas_call | solution.py:274
  12.0 0.0 copy-start
  12.0 0.0 copy-start.1
  12.0 0.7 %collective-permute-done.1.b_ref = f32[8,64,128]{2,1,0:T(8,128)S(1)} collective-permute-done((f32[8,64,128]{2,1,0:T(8,128)S(1)}, f32[8,64,128]{2,1,0:T(8,128)S(1)}, u32[]{:S(2)}, u32[]{:S(2)}) %collective-permute-start.1) | collective-permute-done | bytes 262176 | tf_op jit(solution)/shard_map/ppermute | solution.py:345
  12.7 3.1 %collective-permute-done.a_ref = f32[8,64,128]{2,1,0:T(8,128)S(1)} collective-permute-done((f32[8,64,128]{2,1,0:T(8,128)S(1)}, f32[8,64,128]{2,1,0:T(8,128)S(1)}, u32[]{:S(2)}, u32[]{:S(2)}) %collective-permute-start) | collective-permute-done | bytes 262176 | tf_op jit(solution)/shard_map/ppermute | solution.py:344
  15.8 0.1 collective-permute-start.2
  15.9 2.7 %collective-permute-start.3 = (f32[4,64,128]{2,1,0:T(8,128)S(1)}, f32[4,64,128]{2,1,0:T(8,128)S(1)}, u32[]{:S(2)}, u32[]{:S(2)}) collective-permute-start(f32[4,64,128]{2,1,0:T(8,128)S(1)} %get-tuple-element.20), channel_id=1, source_target_pairs={{0,192},{64,0},{128,64},{192,128},{1,193},{65,1},{129,65},{193,129... | collective-permute-start | bytes 393224 | tf_op jit(solution)/shard_map/ppermute | solution.py:353
  18.6 19.6 %all_to_all.10 = f32[32,1,128]{2,1,0:T(1,128)S(1)} all-to-all(f32[32,1,128]{2,1,0:T(1,128)S(1)} %bitcast.23), channel_id=1, replica_groups=mesh['ta'=4,'y'=4,'z'=8,'core'=2] {'y','z'}, dimensions={0} | all-to-all | bytes 32768 | tf_op jit(solution)/shard_map/all_to_all | solution.py:354
  38.2 0.0 collective-permute-done.2.c_ref
  38.2 0.0 collective-permute-done.3.d_ref
  38.2 3.9 %project.1 = (f32[4,2,64,128]{3,2,1,0:T(8,128)S(1)}, f32[64,4,128]{2,1,0:T(4,128)}) custom-call(f32[8,64,128]{2,1,0:T(8,128)S(1)} %get-tuple-element.14.own_ref, f32[8,64,128]{2,1,0:T(8,128)S(1)} %collective-permute-done.a_ref, f32[8,64,128]{2,1,0:T(8,128)S(1)} %collective-permute-done.1.b_ref, f32[4,64,128]{2,1,0:T(8,128)S(1)} %collective-permute-done.2.c_ref, ...), custom_call_target="tpu_custom_call" | custom-call | flops 33554432 | bytes 4194304 | tf_op jit(solution)/shard_map/project/pallas_call | solution.py:292
  42.1 7.9 %all-to-all-start.1 = ((f32[64,4,128]{2,1,0:T(4,128)}), f32[64,4,128]{2,1,0:T(4,128)S(1)}, u32[]{:S(2)}, u32[]{:S(2)}) async-start(f32[64,4,128]{2,1,0:T(4,128)} %get-tuple-element.22), calls=%async_computation.1 | async-start | bytes 262144 | tf_op jit(solution)/shard_map/all_to_all | solution.py:357
  50.7 9.8 %all-to-all-done.1 = f32[64,4,128]{2,1,0:T(4,128)S(1)} async-done(((f32[64,4,128]{2,1,0:T(4,128)}), f32[64,4,128]{2,1,0:T(4,128)S(1)}, u32[]{:S(2)}, u32[]{:S(2)}) %all-to-all-start.1) | async-done | bytes 131104 | tf_op jit(solution)/shard_map/all_to_all | solution.py:357
  60.5 0.0 copy-done
  60.5 0.0 copy-done.1
  60.5 4.7 %update.1 = (bf16[4,2,32,64,128]{4,3,2,1,0:T(8,128)(2,1)}, f32[4,2,32,32]{3,2,1,0:T(8,128)}) custom-call(s32[1]{0:T(128)S(6)} %copy.15.refs_0_, f32[256,128]{1,0:T(8,128)S(1)} %bitcast.21, bf16[40,256]{1,0:T(8,128)(2,1)S(1)} %copy-done, f32[4,32]{1,0:T(4,128)S(1)} %copy-done.1, f32[4,2,64,128]{3,2,1,0:T(8,128)S(1)} %get-tuple-element.23.refs_4_, ...), custom_call_target="tpu_custom_call" | custom-call | tf_op jit(solution)/shard_map/update/pallas_call | solution.py:313
  (1 shorter events, 0.0 us)
Async XLA Ops:
  0.6 0.7 %copy-start.2 = (s32[16]{0:T(128)S(1)}, s32[16]{0:T(128)}, u32[]{:S(2)}) copy-start(s32[16]{0:T(128)} %refs_0_.2) | copy-start | bytes 196
  4.3 8.4 %collective-permute-start.1 = (f32[8,64,128]{2,1,0:T(8,128)S(1)}, f32[8,64,128]{2,1,0:T(8,128)S(1)}, u32[]{:S(2)}, u32[]{:S(2)}) collective-permute-start(f32[8,64,128]{2,1,0:T(8,128)S(1)} %get-tuple-element.16), channel_id=1, source_target_pairs={{0,192},{64,0},{128,64},{192,128},{1,193},{65,1},{129,65},{193,129... | collective-permute-start | bytes 786440 | tf_op jit(solution)/shard_map/ppermute | solution.py:345
  7.7 8.1 %collective-permute-start = (f32[8,64,128]{2,1,0:T(8,128)S(1)}, f32[8,64,128]{2,1,0:T(8,128)S(1)}, u32[]{:S(2)}, u32[]{:S(2)}) collective-permute-start(f32[8,64,128]{2,1,0:T(8,128)S(1)} %get-tuple-element.15), channel_id=1, source_target_pairs={{0,64},{64,128},{128,192},{192,0},{1,65},{65,129},{129,193},{193,1... | collective-permute-start | bytes 786440 | tf_op jit(solution)/shard_map/ppermute | solution.py:344
  12.0 48.5 %copy-start = (bf16[40,256]{1,0:T(8,128)(2,1)S(1)}, bf16[40,256]{1,0:T(8,128)(2,1)}, u32[]{:S(2)}) copy-start(bf16[40,256]{1,0:T(8,128)(2,1)} %constant.8.clone.refs_2_) | copy-start | bytes 61444
  12.0 48.5 %copy-start.1 = (f32[4,32]{1,0:T(4,128)S(1)}, f32[4,32]{1,0:T(4,128)}, u32[]{:S(2)}) copy-start(f32[4,32]{1,0:T(4,128)} %refs_3_.1) | copy-start | bytes 1540
  15.8 22.4 %collective-permute-start.2 = (f32[4,64,128]{2,1,0:T(8,128)S(1)}, f32[4,64,128]{2,1,0:T(8,128)S(1)}, u32[]{:S(2)}, u32[]{:S(2)}) collective-permute-start(f32[4,64,128]{2,1,0:T(8,128)S(1)} %get-tuple-element.19), channel_id=1, source_target_pairs={{0,64},{64,128},{128,192},{192,0},{1,65},{65,129},{129,193},{193,1... | collective-permute-start | bytes 393224 | tf_op jit(solution)/shard_map/ppermute | solution.py:352
  15.9 22.3 %collective-permute-start.3 = (f32[4,64,128]{2,1,0:T(8,128)S(1)}, f32[4,64,128]{2,1,0:T(8,128)S(1)}, u32[]{:S(2)}, u32[]{:S(2)}) collective-permute-start(f32[4,64,128]{2,1,0:T(8,128)S(1)} %get-tuple-element.20), channel_id=1, source_target_pairs={{0,192},{64,0},{128,64},{192,128},{1,193},{65,1},{129,65},{193,129... | collective-permute-start | bytes 393224 | tf_op jit(solution)/shard_map/ppermute | solution.py:353
  42.1 18.4 %all-to-all-start.1 = ((f32[64,4,128]{2,1,0:T(4,128)}), f32[64,4,128]{2,1,0:T(4,128)S(1)}, u32[]{:S(2)}, u32[]{:S(2)}) async-start(f32[64,4,128]{2,1,0:T(4,128)} %get-tuple-element.22), calls=%async_computation.1 | async-start | bytes 262144 | tf_op jit(solution)/shard_map/all_to_all | solution.py:357

commit v5 on v3

--- a/solution.py
+++ b/solution.py
@@ -116,7 +116,7 @@
     keep_ref[...] = jnp.where(first, low, high)
 
 
-def project_kernel(own_ref, a_ref, b_ref, c_ref, d_ref, u_hbm, h_ref, s_ref, blk_ref, acc_ref, u_ref, sems):
+def project_kernel(own_ref, a_ref, b_ref, c_ref, d_ref, u_hbm, h0_ref, h1_ref, h2_ref, h3_ref, s_ref, blk_ref, acc_ref, u_ref, sems):
     nb, _, rank, rows, _ = u_ref.shape
     loads = [pltpu.make_async_copy(u_hbm.at[b], u_ref.at[b], sems.at[b]) for b in range(nb)]
     for load in loads:
@@ -163,7 +163,7 @@
     )
     blk = jnp.concatenate(
         [sums[0:1, k * LANES:(k + 1) * LANES] for k in range(3)]
-        + [h_ref[...], jnp.zeros((1, LANES), jnp.float32)],
+        + [h0_ref[...] + h1_ref[...] + h2_ref[...] + h3_ref[...], jnp.zeros((1, LANES), jnp.float32)],
         axis=0,
     )
     blk_ref[...] = jnp.broadcast_to(blk[None], blk_ref.shape)
@@ -306,7 +306,7 @@
             jax.ShapeDtypeStruct((nb, 2, rows, LANES), jnp.float32),
             jax.ShapeDtypeStruct((n_space, BLK, LANES), jnp.float32),
         ),
-        in_specs=[VMEM] * 5 + [HBM, VMEM],
+        in_specs=[VMEM] * 5 + [HBM] + [VMEM] * 4,
         out_specs=(VMEM, VMEM),
         scratch_shapes=[
             pltpu.VMEM((3 * LANES * 8, LANES), jnp.float32),
@@ -316,7 +316,7 @@
         compiler_params=room(52000),
         cost_estimate=pl.CostEstimate(flops=16 * u.size, bytes_accessed=u.size * 2, transcendentals=0),
         name="project",
-    )(own, a, b, c, d, u, h)
+    )(own, a, b, c, d, u, *h)
 
 
 def call_update(block_count, g, eigenvalues, spec, u, parts=2):
@@ -370,9 +370,8 @@
 
     n = h.shape[0] // 4
     h = h.reshape(4, n, h.shape[1])
-    quarter = [lax.dynamic_index_in_dim(h, y ^ k, 0, keepdims=False) for k in range(4)]
-    h = quarter[0] + trade(quarter[1], "y", 1) + trade(quarter[2], "y", 2) + trade(quarter[3], "y", 3)
-
+    h = [lax.dynamic_index_in_dim(h, y ^ k, 0, keepdims=False) for k in range(4)]
+    h = [h[0]] + [trade(h[k], "y", k) for k in (1, 2, 3)]
     spec, blk = call_project(own, a, b, c, d, u, h, n_space)
     g = lax.all_to_all(blk, SPACE, 0, 0, tiled=True).reshape(n_space * BLK, LANES)
     fresh, coherence = call_update(block_count, g, eigenvalues, spec, u)

time: 60.6 us -> 60.5 us (level)
  starting transfers between devices: 27 us -> 25.9 us
  waiting for transfers between devices: 15.4 us -> 16.3 us
    ppermute x4, waiting for transfers between devices: 1.37 us -> 4.11 us  [trade(): return lax.ppermute(v, axis, [(i, i ^ mask) for i in range(n)])]
    ppermute x1, waiting for transfers between devices: 1.8 us -> 0.01 us  [local(): c = lax.ppermute(c, 'ta', ring_up)]
    ppermute x4, starting transfers between devices: 6.04 us -> 5.43 us  [trade(): return lax.ppermute(v, axis, [(i, i ^ mask) for i in range(n)])]
where the time goes in v5:
time: 60.5 us; the launch traced here: 60.3 us
  starting transfers between devices  25.9 us (43%)
  waiting for transfers between devices  16.3 us (27%)
  Pallas kernels  16 us (26%)
  between operations  1.36 us (2%)
  local copies, waits for them, and re-layouts  0.67 us (1%)
    all_to_all x1, starting transfers between devices, local(): lax.all_to_all(blk, SPACE, 0, 0, tiled=True).reshape(n_space * BLK, LANES)  14.3 us
    all_to_all x1, waiting for transfers between devices, local(): lax.all_to_all(blk, SPACE, 0, 0, tiled=True).reshape(n_space * BLK, LANES)  11.4 us
    ppermute x4, starting transfers between devices, trade(): return lax.ppermute(v, axis, [(i, i ^ mask) for i in range(n)])  5.43 us
    pallas_call x1, Pallas kernels, call_update(): pl.pallas_call(lambda *refs: update_kernel(parts, *refs), out_shape=(jax....  4.73 us
    pallas_call x1, Pallas kernels, call_gram(): pl.pallas_call(gram_kernel, out_shape=[jax.ShapeDtypeStruct((rank // 2, n...  4.27 us
    ppermute x4, waiting for transfers between devices, trade(): return lax.ppermute(v, axis, [(i, i ^ mask) for i in range(n)])  4.11 us
    pallas_call x1, Pallas kernels, call_project(): pl.pallas_call(project_kernel, out_shape=(jax.ShapeDtypeStruct((nb, 2, ro...  3.95 us
    ppermute x1, starting transfers between devices, local(): b = lax.ppermute(down, 'ta', ring_down)  3.39 us
  transfers between devices with their start and end apart: 9, of which 5 were waited for; matrix products, arithmetic and copies ran while one was open for 0% of the time, Pallas kernels for 7%

profile of v5, /device:TPU:1, one launch (start us, length us, event | category | flops | bytes accessed | tf_op | source)
XLA Modules:
  0.0 60.3 jit_solution(2000485275907835240)
XLA Ops:
  0.6 0.0 copy-start.2
  0.6 0.6 %copy-done.2 = s32[16]{0:T(128)S(1)} copy-done((s32[16]{0:T(128)S(1)}, s32[16]{0:T(128)}, u32[]{:S(2)}) %copy-start.2) | copy-done | bytes 88
  1.3 3.0 %transform.1 = (f32[8,64,128]{2,1,0:T(8,128)S(1)}, f32[8,64,128]{2,1,0:T(8,128)S(1)}, f32[8,64,128]{2,1,0:T(8,128)S(1)}, f32[8,64,128]{2,1,0:T(8,128)S(1)}) custom-call(s32[16]{0:T(128)S(1)} %copy-done.2, s32[1]{0:T(128)} %bitcast.refs_1_, f32[64,64,128]{2,1,0:T(8,128)} %bitcast.31), custom_call_target="tpu_custom_call" | custom-call | tf_op jit(solution)/shard_map/transform/pallas_call | solution.py:272
  4.3 3.4 %collective-permute-start.1 = (f32[8,64,128]{2,1,0:T(8,128)S(1)}, f32[8,64,128]{2,1,0:T(8,128)S(1)}, u32[]{:S(2)}, u32[]{:S(2)}) collective-permute-start(f32[8,64,128]{2,1,0:T(8,128)S(1)} %get-tuple-element.18), channel_id=1, source_target_pairs={{0,192},{64,0},{128,64},{192,128},{1,193},{65,1},{129,65},{193,129... | collective-permute-start | bytes 786440 | tf_op jit(solution)/shard_map/ppermute | solution.py:358
  7.7 0.0 collective-permute-start
  7.7 4.3 %gram.1 = (f32[16,128]{1,0:T(8,128)S(1)}, f32[16,128]{1,0:T(8,128)S(1)}) custom-call(s32[1]{0:T(128)} %bitcast.4.core_ref, bf16[4,2,32,64,128]{4,3,2,1,0:T(8,128)(2,1)} %bitcast.28), custom_call_target="tpu_custom_call" | custom-call | flops 4000000000 | bytes 4194304 | tf_op jit(solution)/shard_map/gram/pallas_call | solution.py:285
  12.0 0.0 copy-start
  12.0 0.0 copy-start.1
  12.0 2.0 %collective-permute-start.2 = (f32[16,128]{1,0:T(8,128)S(1)}, f32[16,128]{1,0:T(8,128)S(1)}, u32[]{:S(2)}, u32[]{:S(2)}) collective-permute-start(f32[16,128]{1,0:T(8,128)S(1)} %get-tuple-element.22), channel_id=1, source_target_pairs={{0,1},{1,0},{2,3},{3,2},{4,5},{5,4},{6,7},{7,6},{8,9},{9,8},{10,11... | collective-permute-start | bytes 24584 | tf_op jit(solution)/shard_map/ppermute | solution.py:257
  14.1 0.8 %collective-permute-done.2 = f32[16,128]{1,0:T(8,128)S(1)} collective-permute-done((f32[16,128]{1,0:T(8,128)S(1)}, f32[16,128]{1,0:T(8,128)S(1)}, u32[]{:S(2)}, u32[]{:S(2)}) %collective-permute-start.2) | collective-permute-done | bytes 8224 | tf_op jit(solution)/shard_map/ppermute | solution.py:257
  14.9 0.0 collective-permute-done.1.b_ref
  14.9 0.9 %collective-permute-done.a_ref = f32[8,64,128]{2,1,0:T(8,128)S(1)} collective-permute-done((f32[8,64,128]{2,1,0:T(8,128)S(1)}, f32[8,64,128]{2,1,0:T(8,128)S(1)}, u32[]{:S(2)}, u32[]{:S(2)}) %collective-permute-start) | collective-permute-done | bytes 262176 | tf_op jit(solution)/shard_map/ppermute | solution.py:357
  15.8 0.1 collective-permute-start.3
  15.9 2.7 %collective-permute-start.4 = (f32[4,64,128]{2,1,0:T(8,128)S(1)}, f32[4,64,128]{2,1,0:T(8,128)S(1)}, u32[]{:S(2)}, u32[]{:S(2)}) collective-permute-start(f32[4,64,128]{2,1,0:T(8,128)S(1)} %get-tuple-element.24), channel_id=1, source_target_pairs={{0,192},{64,0},{128,64},{192,128},{1,193},{65,1},{129,65},{193,129... | collective-permute-start | bytes 393224 | tf_op jit(solution)/shard_map/ppermute | solution.py:369
  18.6 2.7 %collective-permute-start.7 = (f32[4,128]{1,0:T(4,128)S(1)}, f32[4,128]{1,0:T(4,128)S(1)}, u32[]{:S(2)}, u32[]{:S(2)}) collective-permute-start(f32[4,128]{1,0:T(4,128)S(1)} %get-tuple-element.32), channel_id=1, source_target_pairs={{0,48},{16,32},{32,16},{48,0},{1,49},{17,33},{33,17},{49,1},{2,50}... | collective-permute-start | bytes 6152 | tf_op jit(solution)/shard_map/ppermute | solution.py:257
  21.3 0.4 collective-permute-start.6
  21.7 0.3 collective-permute-start.5
  22.0 0.6 %collective-permute-done.7.h3_ref = f32[4,128]{1,0:T(4,128)S(1)} collective-permute-done((f32[4,128]{1,0:T(4,128)S(1)}, f32[4,128]{1,0:T(4,128)S(1)}, u32[]{:S(2)}, u32[]{:S(2)}) %collective-permute-start.7) | collective-permute-done | bytes 2080 | tf_op jit(solution)/shard_map/ppermute | solution.py:257
  22.6 2.7 %collective-permute-done.6.h2_ref = f32[4,128]{1,0:T(4,128)S(1)} collective-permute-done((f32[4,128]{1,0:T(4,128)S(1)}, f32[4,128]{1,0:T(4,128)S(1)}, u32[]{:S(2)}, u32[]{:S(2)}) %collective-permute-start.6) | collective-permute-done | bytes 2080 | tf_op jit(solution)/shard_map/ppermute | solution.py:257
  25.2 0.0 collective-permute-done.5.h1_ref
  25.2 0.0 collective-permute-done.3.c_ref
  25.2 0.0 collective-permute-done.4.d_ref
  25.2 3.9 %project.1 = (f32[4,2,64,128]{3,2,1,0:T(8,128)S(1)}, f32[64,8,128]{2,1,0:T(8,128)}) custom-call(f32[8,64,128]{2,1,0:T(8,128)S(1)} %get-tuple-element.16.own_ref, f32[8,64,128]{2,1,0:T(8,128)S(1)} %collective-permute-done.a_ref, f32[8,64,128]{2,1,0:T(8,128)S(1)} %collective-permute-done.1.b_ref, f32[4,64,128]{2,1,0:T(8,128)S(1)} %collective-permute-done.3.c_ref, ...), custom_call_target="tpu_custom_call" | custom-call | flops 33554432 | bytes 4194304 | tf_op jit(solution)/shard_map/project/pallas_call | solution.py:303
  29.2 14.3 %all-to-all-start = ((f32[64,8,128]{2,1,0:T(8,128)}), f32[64,8,128]{2,1,0:T(8,128)S(1)}, u32[]{:S(2)}, u32[]{:S(2)}) async-start(f32[64,8,128]{2,1,0:T(8,128)} %get-tuple-element.26), calls=%async_computation | async-start | bytes 524288 | tf_op jit(solution)/shard_map/all_to_all | solution.py:376
  44.2 11.4 %all-to-all-done = f32[64,8,128]{2,1,0:T(8,128)S(1)} async-done(((f32[64,8,128]{2,1,0:T(8,128)}), f32[64,8,128]{2,1,0:T(8,128)S(1)}, u32[]{:S(2)}, u32[]{:S(2)}) %all-to-all-start) | async-done | bytes 262176 | tf_op jit(solution)/shard_map/all_to_all | solution.py:376
  55.6 0.0 copy-done
  55.6 0.0 copy-done.1
  55.6 4.7 %update.1 = (bf16[4,2,32,64,128]{4,3,2,1,0:T(8,128)(2,1)}, f32[4,2,32,32]{3,2,1,0:T(8,128)}) custom-call(s32[1]{0:T(128)S(6)} %copy.11.refs_0_, f32[512,128]{1,0:T(8,128)S(1)} %bitcast.27, bf16[40,512]{1,0:T(8,128)(2,1)S(1)} %copy-done, f32[4,32]{1,0:T(4,128)S(1)} %copy-done.1, f32[4,2,64,128]{3,2,1,0:T(8,128)S(1)} %get-tuple-element.27.refs_4_, ...), custom_call_target="tpu_custom_call" | custom-call | tf_op jit(solution)/shard_map/update/pallas_call | solution.py:324
  (3 shorter events, 0.0 us)
Async XLA Ops:
  0.6 0.7 %copy-start.2 = (s32[16]{0:T(128)S(1)}, s32[16]{0:T(128)}, u32[]{:S(2)}) copy-start(s32[16]{0:T(128)} %refs_0_.2) | copy-start | bytes 196
  4.3 10.6 %collective-permute-start.1 = (f32[8,64,128]{2,1,0:T(8,128)S(1)}, f32[8,64,128]{2,1,0:T(8,128)S(1)}, u32[]{:S(2)}, u32[]{:S(2)}) collective-permute-start(f32[8,64,128]{2,1,0:T(8,128)S(1)} %get-tuple-element.18), channel_id=1, source_target_pairs={{0,192},{64,0},{128,64},{192,128},{1,193},{65,1},{129,65},{193,129... | collective-permute-start | bytes 786440 | tf_op jit(solution)/shard_map/ppermute | solution.py:358
  7.7 8.1 %collective-permute-start = (f32[8,64,128]{2,1,0:T(8,128)S(1)}, f32[8,64,128]{2,1,0:T(8,128)S(1)}, u32[]{:S(2)}, u32[]{:S(2)}) collective-permute-start(f32[8,64,128]{2,1,0:T(8,128)S(1)} %get-tuple-element.17), channel_id=1, source_target_pairs={{0,64},{64,128},{128,192},{192,0},{1,65},{65,129},{129,193},{193,1... | collective-permute-start | bytes 786440 | tf_op jit(solution)/shard_map/ppermute | solution.py:357
  12.0 43.6 %copy-start = (bf16[40,512]{1,0:T(8,128)(2,1)S(1)}, bf16[40,512]{1,0:T(8,128)(2,1)}, u32[]{:S(2)}) copy-start(bf16[40,512]{1,0:T(8,128)(2,1)} %constant.34.clone.refs_2_) | copy-start | bytes 122884
  12.0 43.6 %copy-start.1 = (f32[4,32]{1,0:T(4,128)S(1)}, f32[4,32]{1,0:T(4,128)}, u32[]{:S(2)}) copy-start(f32[4,32]{1,0:T(4,128)} %refs_3_.1) | copy-start | bytes 1540
  12.0 2.9 %collective-permute-start.2 = (f32[16,128]{1,0:T(8,128)S(1)}, f32[16,128]{1,0:T(8,128)S(1)}, u32[]{:S(2)}, u32[]{:S(2)}) collective-permute-start(f32[16,128]{1,0:T(8,128)S(1)} %get-tuple-element.22), channel_id=1, source_target_pairs={{0,1},{1,0},{2,3},{3,2},{4,5},{5,4},{6,7},{7,6},{8,9},{9,8},{10,11... | collective-permute-start | bytes 24584 | tf_op jit(solution)/shard_map/ppermute | solution.py:257
  15.8 9.4 %collective-permute-start.3 = (f32[4,64,128]{2,1,0:T(8,128)S(1)}, f32[4,64,128]{2,1,0:T(8,128)S(1)}, u32[]{:S(2)}, u32[]{:S(2)}) collective-permute-start(f32[4,64,128]{2,1,0:T(8,128)S(1)} %get-tuple-element.23), channel_id=1, source_target_pairs={{0,64},{64,128},{128,192},{192,0},{1,65},{65,129},{129,193},{193,1... | collective-permute-start | bytes 393224 | tf_op jit(solution)/shard_map/ppermute | solution.py:368
  15.9 9.3 %collective-permute-start.4 = (f32[4,64,128]{2,1,0:T(8,128)S(1)}, f32[4,64,128]{2,1,0:T(8,128)S(1)}, u32[]{:S(2)}, u32[]{:S(2)}) collective-permute-start(f32[4,64,128]{2,1,0:T(8,128)S(1)} %get-tuple-element.24), channel_id=1, source_target_pairs={{0,192},{64,0},{128,64},{192,128},{1,193},{65,1},{129,65},{193,129... | collective-permute-start | bytes 393224 | tf_op jit(solution)/shard_map/ppermute | solution.py:369
  18.6 4.0 %collective-permute-start.7 = (f32[4,128]{1,0:T(4,128)S(1)}, f32[4,128]{1,0:T(4,128)S(1)}, u32[]{:S(2)}, u32[]{:S(2)}) collective-permute-start(f32[4,128]{1,0:T(4,128)S(1)} %get-tuple-element.32), channel_id=1, source_target_pairs={{0,48},{16,32},{32,16},{48,0},{1,49},{17,33},{33,17},{49,1},{2,50}... | collective-permute-start | bytes 6152 | tf_op jit(solution)/shard_map/ppermute | solution.py:257
  21.3 3.9 %collective-permute-start.6 = (f32[4,128]{1,0:T(4,128)S(1)}, f32[4,128]{1,0:T(4,128)S(1)}, u32[]{:S(2)}, u32[]{:S(2)}) collective-permute-start(f32[4,128]{1,0:T(4,128)S(1)} %get-tuple-element.33), channel_id=1, source_target_pairs={{0,32},{16,48},{32,0},{48,16},{1,33},{17,49},{33,1},{49,17},{2,34}... | collective-permute-start | bytes 6152 | tf_op jit(solution)/shard_map/ppermute | solution.py:257
  21.7 3.6 %collective-permute-start.5 = (f32[4,128]{1,0:T(4,128)S(1)}, f32[4,128]{1,0:T(4,128)S(1)}, u32[]{:S(2)}, u32[]{:S(2)}) collective-permute-start(f32[4,128]{1,0:T(4,128)S(1)} %get-tuple-element.34), channel_id=1, source_target_pairs={{0,16},{16,0},{32,48},{48,32},{1,17},{17,1},{33,49},{49,33},{2,18}... | collective-permute-start | bytes 6152 | tf_op jit(solution)/shard_map/ppermute | solution.py:257
  29.2 26.4 %all-to-all-start = ((f32[64,8,128]{2,1,0:T(8,128)}), f32[64,8,128]{2,1,0:T(8,128)S(1)}, u32[]{:S(2)}, u32[]{:S(2)}) async-start(f32[64,8,128]{2,1,0:T(8,128)} %get-tuple-element.26), calls=%async_computation | async-start | bytes 524288 | tf_op jit(solution)/shard_map/all_to_all | solution.py:376

commit v6 on v5

--- a/solution.py
+++ b/solution.py
@@ -11,12 +11,6 @@
 SPACE = ("y", "z", "core")
 LANES = 128
 BLK = 8
-UP = ((2, 0), (2, 1), (1, 2), (1, 3))
-DOWN = ((2, 2), (2, 3), (3, 0), (3, 1))
-KEEP = ((1, 0), (1, 1), (3, 2), (3, 3))
-OWN = ((0, 0), (0, 1), (0, 2), (0, 3))
-ORDER = UP + DOWN + KEEP + OWN
-
 
 def fold(v, axis):
     shape = v.shape
@@ -39,8 +33,7 @@
     return hi, mid, low
 
 
-def transform_kernel(total, chunks, bins_ref, place_ref, x_hbm, *refs):
-    *out_refs, x_ref, sems = refs
+def transform_kernel(total, chunks, bins_ref, place_ref, x_hbm, out_ref, x_ref, sems):
     slice_len, rows, _ = x_ref.shape
     piece = rows // chunks
     copies = [
@@ -49,13 +42,13 @@
     ]
     for copy in copies:
         copy.start()
-    n = 2 * len(ORDER)
+    n = 2 * bins_ref.shape[0]
     place = place_ref[0]
     row = lax.broadcasted_iota(jnp.int32, (n, slice_len), 0)
     t = lax.broadcasted_iota(jnp.int32, (n, slice_len), 1) + place * slice_len
     which = jnp.zeros((n, slice_len), jnp.int32)
-    for i, (ahead, b) in enumerate(ORDER):
-        which = jnp.where(row // 2 == i, bins_ref[((place + ahead) % 4) * 4 + b], which)
+    for i in range(n // 2):
+        which = jnp.where(row // 2 == i, bins_ref[i], which)
     phase = (which * t + (row % 2) * (total // 4)) % total
     step = 2.0 * math.pi / total
     window = 0.5 - 0.5 * jnp.cos(step * t.astype(jnp.float32))
@@ -64,7 +57,6 @@
     t_lo = (table - t_hi.astype(jnp.float32)).astype(jnp.bfloat16)
     left = jnp.concatenate([t_hi, t_lo], axis=0)
     left = jnp.concatenate([left, left], axis=1)
-    each = n // len(out_refs)
     for at in range(0, rows, 8):
         if at % piece == 0:
             copies[at // piece].wait()
@@ -78,8 +70,7 @@
             res = res[:n] + res[n:]
             got += [res[:, :LANES], res[:, LANES:]]
         got = jnp.swapaxes(jnp.stack(got, axis=0), 0, 1)
-        for i, out_ref in enumerate(out_refs):
-            out_ref[:, at:at + 8, :] = got[i * each:(i + 1) * each]
+        out_ref[:, at:at + 8, :] = got
 
 
 def gram_kernel(core_ref, u_hbm, send_ref, keep_ref, all_ref, u_ref, sems):
@@ -116,12 +107,11 @@
     keep_ref[...] = jnp.where(first, low, high)
 
 
-def project_kernel(own_ref, a_ref, b_ref, c_ref, d_ref, u_hbm, h0_ref, h1_ref, h2_ref, h3_ref, s_ref, blk_ref, acc_ref, u_ref, sems):
+def project_kernel(parts_ref, u_hbm, h0_ref, h1_ref, h2_ref, h3_ref, s_ref, blk_ref, acc_ref, u_ref, sems):
     nb, _, rank, rows, _ = u_ref.shape
     loads = [pltpu.make_async_copy(u_hbm.at[b], u_ref.at[b], sems.at[b]) for b in range(nb)]
     for load in loads:
         load.start()
-    half = nb // 2
     used = nb * (2 * rank + 1) * 8
     acc_ref[pl.ds(used, acc_ref.shape[0] - used), :] = jnp.zeros((acc_ref.shape[0] - used, LANES), jnp.float32)
 
@@ -132,10 +122,7 @@
         at = 2 * b
         s = []
         for k in (at, at + 1):
-            if b < half:
-                s.append(own_ref[k] + b_ref[k + nb] + c_ref[k])
-            else:
-                s.append(own_ref[k] + a_ref[k] + d_ref[k - nb])
+            s.append((parts_ref[0, k] + parts_ref[1, k]) + (parts_ref[2, k] + parts_ref[3, k]))
         s_re, s_im = s
         s_ref[b, 0] = s_re
         s_ref[b, 1] = s_im
@@ -268,12 +255,12 @@
 
 def call_transform(bins, place, x, total, chunks=4):
     slice_len, rows, _ = x.shape
-    n = 2 * len(ORDER)
+    n = 2 * bins.shape[0]
     return pl.pallas_call(
         lambda *refs: transform_kernel(total, chunks, *refs),
-        out_shape=[jax.ShapeDtypeStruct((n // 4, rows, LANES), jnp.float32)] * 4,
+        out_shape=jax.ShapeDtypeStruct((n, rows, LANES), jnp.float32),
         in_specs=[SMEM, SMEM, HBM],
-        out_specs=[VMEM] * 4,
+        out_specs=VMEM,
         scratch_shapes=[pltpu.VMEM(x.shape, jnp.float32), pltpu.SemaphoreType.DMA((chunks,))],
         compiler_params=room(53500),
         name="transform",
@@ -298,7 +285,7 @@
     )(core, u)
 
 
-def call_project(own, a, b, c, d, u, h, n_space):
+def call_project(parts, u, h, n_space):
     nb, _, rank, rows, _ = u.shape
     return pl.pallas_call(
         project_kernel,
@@ -306,7 +293,7 @@
             jax.ShapeDtypeStruct((nb, 2, rows, LANES), jnp.float32),
             jax.ShapeDtypeStruct((n_space, BLK, LANES), jnp.float32),
         ),
-        in_specs=[VMEM] * 5 + [HBM] + [VMEM] * 4,
+        in_specs=[VMEM, HBM] + [VMEM] * 4,
         out_specs=(VMEM, VMEM),
         scratch_shapes=[
             pltpu.VMEM((3 * LANES * 8, LANES), jnp.float32),
@@ -316,7 +303,7 @@
         compiler_params=room(52000),
         cost_estimate=pl.CostEstimate(flops=16 * u.size, bytes_accessed=u.size * 2, transcendentals=0),
         name="project",
-    )(own, a, b, c, d, u, *h)
+    )(parts, u, *h)
 
 
 def call_update(block_count, g, eigenvalues, spec, u, parts=2):
@@ -351,28 +338,20 @@
     core = lax.axis_index("core").astype(jnp.int32).reshape(1)
     y = lax.axis_index("y")
 
-    up, down, keep, own = call_transform(bins, place, fold(snapshots, 1), total)
-    ring_up = [(i, (i + 1) % groups) for i in range(groups)]
-    ring_down = [(i, (i - 1) % groups) for i in range(groups)]
-    a = lax.ppermute(up, "ta", ring_up)
-    b = lax.ppermute(down, "ta", ring_down)
+    terms = call_transform(bins, place, fold(snapshots, 1), total)
+    parts = lax.all_to_all(terms, "ta", 0, 0, tiled=True)
+    parts = parts.reshape(groups, 2 * nb, *terms.shape[1:])
 
     u = fold(old_basis, 3)
-    u, _ = lax.optimization_barrier((u, up))
+    u, _ = lax.optimization_barrier((u, terms))
     send, kept = call_gram(core, u)
-
     h = kept + trade(send, "core", 1)
-
-    c, d = keep[:nb] + a[:nb], keep[nb:] + b[:nb]
-    c, d, h = lax.optimization_barrier((c, d, h))
-    c = lax.ppermute(c, "ta", ring_up)
-    d = lax.ppermute(d, "ta", ring_down)
 
     n = h.shape[0] // 4
     h = h.reshape(4, n, h.shape[1])
     h = [lax.dynamic_index_in_dim(h, y ^ k, 0, keepdims=False) for k in range(4)]
     h = [h[0]] + [trade(h[k], "y", k) for k in (1, 2, 3)]
-    spec, blk = call_project(own, a, b, c, d, u, h, n_space)
+    spec, blk = call_project(parts, u, h, n_space)
     g = lax.all_to_all(blk, SPACE, 0, 0, tiled=True).reshape(n_space * BLK, LANES)
     fresh, coherence = call_update(block_count, g, eigenvalues, spec, u)
     return unfold(fresh, 3), coherence

time: 60.5 us -> 58.8 us (0.972)
  waiting for transfers between devices: 16.3 us -> 15 us
  starting transfers between devices: 25.9 us -> 24.6 us
  Pallas kernels: 16 us -> 16.9 us
    ppermute x4 -> x0, starting transfers between devices: 6.14 us -> none  [the longest x1 3.39 us: local(): b = lax.ppermute(down, 'ta', ring_down)]
    all_to_all x0 -> x1, starting transfers between devices: none -> 4.85 us  [local(): parts = lax.all_to_all(terms, 'ta', 0, 0, tiled=True)]
    pallas_call x1, Pallas kernels: 3.02 us -> 3.98 us  [call_transform(): pl.pallas_call(lambda *refs: transform_kernel(total, chunks, *refs), out_...]
    ppermute x4 -> x0, waiting for transfers between devices: 0.89 us -> none  [the longest x1 0.88 us: local(): a = lax.ppermute(up, 'ta', ring_up)]
  transfers between devices with their start and end apart: 9 -> 6, of which waited for: 5 -> 4; matrix products, arithmetic and copies ran while one was open for 0% -> 0% of each run, Pallas kernels for 7% -> 7%
where the time goes in v6:
time: 58.8 us; the launch traced here: 58.5 us
  starting transfers between devices  24.6 us (42%)
  Pallas kernels  16.9 us (29%)
  waiting for transfers between devices  15 us (26%)
  between operations  1.35 us (2%)
  local copies, waits for them, and re-layouts  0.67 us (1%)
    all_to_all x1, starting transfers between devices, local(): lax.all_to_all(blk, SPACE, 0, 0, tiled=True).reshape(n_space * BLK, LANES)  14.5 us
    all_to_all x1, waiting for transfers between devices, local(): lax.all_to_all(blk, SPACE, 0, 0, tiled=True).reshape(n_space * BLK, LANES)  11.4 us
    ppermute x4, starting transfers between devices, trade(): return lax.ppermute(v, axis, [(i, i ^ mask) for i in range(n)])  5.31 us
    all_to_all x1, starting transfers between devices, local(): parts = lax.all_to_all(terms, 'ta', 0, 0, tiled=True)  4.85 us
    pallas_call x1, Pallas kernels, call_update(): pl.pallas_call(lambda *refs: update_kernel(parts, *refs), out_shape=(jax....  4.73 us
    pallas_call x1, Pallas kernels, call_gram(): pl.pallas_call(gram_kernel, out_shape=[jax.ShapeDtypeStruct((rank // 2, n...  4.27 us
    pallas_call x1, Pallas kernels, call_transform(): pl.pallas_call(lambda *refs: transform_kernel(total, chunks, *refs), out_...  3.98 us
    pallas_call x1, Pallas kernels, call_project(): pl.pallas_call(project_kernel, out_shape=(jax.ShapeDtypeStruct((nb, 2, ro...  3.95 us
  transfers between devices with their start and end apart: 6, of which 4 were waited for; matrix products, arithmetic and copies ran while one was open for 0% of the time, Pallas kernels for 7%

profile of v6, /device:TPU:1, one launch (start us, length us, event | category | flops | bytes accessed | tf_op | source)
XLA Modules:
  0.0 58.5 jit_solution(6490793117623111841)
XLA Ops:
  0.6 0.0 copy-start.2
  0.6 0.6 %copy-done.2 = s32[16]{0:T(128)S(1)} copy-done((s32[16]{0:T(128)S(1)}, s32[16]{0:T(128)}, u32[]{:S(2)}) %copy-start.2) | copy-done | bytes 88
  1.3 4.0 %transform.1 = f32[32,64,128]{2,1,0:T(8,128)} custom-call(s32[16]{0:T(128)S(1)} %copy-done.2, s32[1]{0:T(128)} %bitcast.refs_1_, f32[64,64,128]{2,1,0:T(8,128)} %bitcast.33), custom_call_target="tpu_custom_call" | custom-call | tf_op jit(solution)/shard_map/transform/pallas_call | solution.py:259
  5.3 4.9 %all-to-all-start = ((f32[32,64,128]{2,1,0:T(8,128)}), f32[32,64,128]{2,1,0:T(8,128)S(1)}, u32[]{:S(2)}, u32[]{:S(2)}) async-start(f32[32,64,128]{2,1,0:T(8,128)} %transform.1), calls=%async_computation | async-start | bytes 2097152 | tf_op jit(solution)/shard_map/all_to_all | solution.py:342
  10.1 4.3 %gram.1 = (f32[16,128]{1,0:T(8,128)S(1)}, f32[16,128]{1,0:T(8,128)S(1)}) custom-call(s32[1]{0:T(128)} %bitcast.8.core_ref, bf16[4,2,32,64,128]{4,3,2,1,0:T(8,128)(2,1)} %bitcast.30), custom_call_target="tpu_custom_call" | custom-call | flops 4000000000 | bytes 4194304 | tf_op jit(solution)/shard_map/gram/pallas_call | solution.py:272
  14.4 0.0 copy-start
  14.4 0.0 copy-start.1
  14.4 2.0 %collective-permute-start = (f32[16,128]{1,0:T(8,128)S(1)}, f32[16,128]{1,0:T(8,128)S(1)}, u32[]{:S(2)}, u32[]{:S(2)}) collective-permute-start(f32[16,128]{1,0:T(8,128)S(1)} %get-tuple-element.11), channel_id=1, source_target_pairs={{0,1},{1,0},{2,3},{3,2},{4,5},{5,4},{6,7},{7,6},{8,9},{9,8},{10,11... | collective-permute-start | bytes 24584 | tf_op jit(solution)/shard_map/ppermute | solution.py:244
  16.5 0.8 %collective-permute-done = f32[16,128]{1,0:T(8,128)S(1)} collective-permute-done((f32[16,128]{1,0:T(8,128)S(1)}, f32[16,128]{1,0:T(8,128)S(1)}, u32[]{:S(2)}, u32[]{:S(2)}) %collective-permute-start) | collective-permute-done | bytes 8224 | tf_op jit(solution)/shard_map/ppermute | solution.py:244
  17.3 1.8 %collective-permute-start.3 = (f32[4,128]{1,0:T(4,128)S(1)}, f32[4,128]{1,0:T(4,128)S(1)}, u32[]{:S(2)}, u32[]{:S(2)}) collective-permute-start(f32[4,128]{1,0:T(4,128)S(1)} %get-tuple-element.16), channel_id=1, source_target_pairs={{0,48},{16,32},{32,16},{48,0},{1,49},{17,33},{33,17},{49,1},{2,50}... | collective-permute-start | bytes 6152 | tf_op jit(solution)/shard_map/ppermute | solution.py:244
  19.1 0.4 collective-permute-start.2
  19.4 1.1 %collective-permute-start.1 = (f32[4,128]{1,0:T(4,128)S(1)}, f32[4,128]{1,0:T(4,128)S(1)}, u32[]{:S(2)}, u32[]{:S(2)}) collective-permute-start(f32[4,128]{1,0:T(4,128)S(1)} %get-tuple-element.18), channel_id=1, source_target_pairs={{0,16},{16,0},{32,48},{48,32},{1,17},{17,1},{33,49},{49,33},{2,18}... | collective-permute-start | bytes 6152 | tf_op jit(solution)/shard_map/ppermute | solution.py:244
  20.6 0.7 %collective-permute-done.3.h3_ref = f32[4,128]{1,0:T(4,128)S(1)} collective-permute-done((f32[4,128]{1,0:T(4,128)S(1)}, f32[4,128]{1,0:T(4,128)S(1)}, u32[]{:S(2)}, u32[]{:S(2)}) %collective-permute-start.3) | collective-permute-done | bytes 2080 | tf_op jit(solution)/shard_map/ppermute | solution.py:244
  21.3 2.0 %collective-permute-done.2.h2_ref = f32[4,128]{1,0:T(4,128)S(1)} collective-permute-done((f32[4,128]{1,0:T(4,128)S(1)}, f32[4,128]{1,0:T(4,128)S(1)}, u32[]{:S(2)}, u32[]{:S(2)}) %collective-permute-start.2) | collective-permute-done | bytes 2080 | tf_op jit(solution)/shard_map/ppermute | solution.py:244
  23.3 0.0 collective-permute-done.1.h1_ref
  23.3 0.0 all-to-all-done
  23.4 3.9 %project.1 = (f32[4,2,64,128]{3,2,1,0:T(8,128)S(1)}, f32[64,8,128]{2,1,0:T(8,128)}) custom-call(f32[4,8,64,128]{3,2,1,0:T(8,128)S(1)} %bitcast.28, bf16[4,2,32,64,128]{4,3,2,1,0:T(8,128)(2,1)} %bitcast.31, f32[4,128]{1,0:T(4,128)S(1)} %get-tuple-element.19.h0_ref, f32[4,128]{1,0:T(4,128)S(1)} %collective-permute-done.1.h1_ref, ...), custom_call_target="tpu_custom_call" | custom-call | flops 33554432 | bytes 4194304 | tf_op jit(solution)/shard_map/project/pallas_call | solution.py:290
  27.3 14.5 %all-to-all-start.1 = ((f32[64,8,128]{2,1,0:T(8,128)}), f32[64,8,128]{2,1,0:T(8,128)S(1)}, u32[]{:S(2)}, u32[]{:S(2)}) async-start(f32[64,8,128]{2,1,0:T(8,128)} %get-tuple-element.12), calls=%async_computation.1 | async-start | bytes 524288 | tf_op jit(solution)/shard_map/all_to_all | solution.py:355
  42.5 11.4 %all-to-all-done.1 = f32[64,8,128]{2,1,0:T(8,128)S(1)} async-done(((f32[64,8,128]{2,1,0:T(8,128)}), f32[64,8,128]{2,1,0:T(8,128)S(1)}, u32[]{:S(2)}, u32[]{:S(2)}) %all-to-all-start.1) | async-done | bytes 262176 | tf_op jit(solution)/shard_map/all_to_all | solution.py:355
  53.8 0.0 copy-done
  53.8 0.0 copy-done.1
  53.8 4.7 %update.1 = (bf16[4,2,32,64,128]{4,3,2,1,0:T(8,128)(2,1)}, f32[4,2,32,32]{3,2,1,0:T(8,128)}) custom-call(s32[1]{0:T(128)S(6)} %copy.11.refs_0_, f32[512,128]{1,0:T(8,128)S(1)} %bitcast.29, bf16[40,512]{1,0:T(8,128)(2,1)S(1)} %copy-done, f32[4,32]{1,0:T(4,128)S(1)} %copy-done.1, f32[4,2,64,128]{3,2,1,0:T(8,128)S(1)} %get-tuple-element.13.refs_4_, ...), custom_call_target="tpu_custom_call" | custom-call | tf_op jit(solution)/shard_map/update/pallas_call | solution.py:311
  (2 shorter events, 0.0 us)
Async XLA Ops:
  0.6 0.7 %copy-start.2 = (s32[16]{0:T(128)S(1)}, s32[16]{0:T(128)}, u32[]{:S(2)}) copy-start(s32[16]{0:T(128)} %refs_0_.2) | copy-start | bytes 196
  5.3 18.1 %all-to-all-start = ((f32[32,64,128]{2,1,0:T(8,128)}), f32[32,64,128]{2,1,0:T(8,128)S(1)}, u32[]{:S(2)}, u32[]{:S(2)}) async-start(f32[32,64,128]{2,1,0:T(8,128)} %transform.1), calls=%async_computation | async-start | bytes 2097152 | tf_op jit(solution)/shard_map/all_to_all | solution.py:342
  14.4 39.4 %copy-start = (bf16[40,512]{1,0:T(8,128)(2,1)S(1)}, bf16[40,512]{1,0:T(8,128)(2,1)}, u32[]{:S(2)}) copy-start(bf16[40,512]{1,0:T(8,128)(2,1)} %constant.34.clone.refs_2_) | copy-start | bytes 122884
  14.4 39.4 %copy-start.1 = (f32[4,32]{1,0:T(4,128)S(1)}, f32[4,32]{1,0:T(4,128)}, u32[]{:S(2)}) copy-start(f32[4,32]{1,0:T(4,128)} %refs_3_.1) | copy-start | bytes 1540
  14.4 2.9 %collective-permute-start = (f32[16,128]{1,0:T(8,128)S(1)}, f32[16,128]{1,0:T(8,128)S(1)}, u32[]{:S(2)}, u32[]{:S(2)}) collective-permute-start(f32[16,128]{1,0:T(8,128)S(1)} %get-tuple-element.11), channel_id=1, source_target_pairs={{0,1},{1,0},{2,3},{3,2},{4,5},{5,4},{6,7},{7,6},{8,9},{9,8},{10,11... | collective-permute-start | bytes 24584 | tf_op jit(solution)/shard_map/ppermute | solution.py:244
  17.3 4.0 %collective-permute-start.3 = (f32[4,128]{1,0:T(4,128)S(1)}, f32[4,128]{1,0:T(4,128)S(1)}, u32[]{:S(2)}, u32[]{:S(2)}) collective-permute-start(f32[4,128]{1,0:T(4,128)S(1)} %get-tuple-element.16), channel_id=1, source_target_pairs={{0,48},{16,32},{32,16},{48,0},{1,49},{17,33},{33,17},{49,1},{2,50}... | collective-permute-start | bytes 6152 | tf_op jit(solution)/shard_map/ppermute | solution.py:244
  19.1 4.2 %collective-permute-start.2 = (f32[4,128]{1,0:T(4,128)S(1)}, f32[4,128]{1,0:T(4,128)S(1)}, u32[]{:S(2)}, u32[]{:S(2)}) collective-permute-start(f32[4,128]{1,0:T(4,128)S(1)} %get-tuple-element.17), channel_id=1, source_target_pairs={{0,32},{16,48},{32,0},{48,16},{1,33},{17,49},{33,1},{49,17},{2,34}... | collective-permute-start | bytes 6152 | tf_op jit(solution)/shard_map/ppermute | solution.py:244
  19.4 3.9 %collective-permute-start.1 = (f32[4,128]{1,0:T(4,128)S(1)}, f32[4,128]{1,0:T(4,128)S(1)}, u32[]{:S(2)}, u32[]{:S(2)}) collective-permute-start(f32[4,128]{1,0:T(4,128)S(1)} %get-tuple-element.18), channel_id=1, source_target_pairs={{0,16},{16,0},{32,48},{48,32},{1,17},{17,1},{33,49},{49,33},{2,18}... | collective-permute-start | bytes 6152 | tf_op jit(solution)/shard_map/ppermute | solution.py:244
  27.3 26.5 %all-to-all-start.1 = ((f32[64,8,128]{2,1,0:T(8,128)}), f32[64,8,128]{2,1,0:T(8,128)S(1)}, u32[]{:S(2)}, u32[]{:S(2)}) async-start(f32[64,8,128]{2,1,0:T(8,128)} %get-tuple-element.12), calls=%async_computation.1 | async-start | bytes 524288 | tf_op jit(solution)/shard_map/all_to_all | solution.py:355

commit v7 on v4

--- a/solution.py
+++ b/solution.py
@@ -10,7 +10,10 @@
 
 SPACE = ("y", "z", "core")
 LANES = 128
-BLK = 4
+MEETINGS = ((1, 2), (16, 32), (4, 8))
+PARTS = 2
+UNROLL = 8
+
 UP = ((2, 0), (2, 1), (1, 2), (1, 3))
 DOWN = ((2, 2), (2, 3), (3, 0), (3, 1))
 KEEP = ((1, 0), (1, 1), (3, 2), (3, 3))
@@ -112,12 +115,14 @@
     h_ref[...] = jnp.concatenate([all_ref[i] for i in range(nb)], axis=1)
 
 
-def project_kernel(own_ref, a_ref, b_ref, c_ref, d_ref, u_hbm, h_ref, s_ref, blk_ref, acc_ref, u_ref, sems):
+def project_kernel(own_ref, a_ref, b_ref, c_ref, d_ref, u_hbm, h_ref, s_ref, all_ref, acc_ref, u_ref, sems):
     nb, _, rank, rows, _ = u_ref.shape
-    loads = [pltpu.make_async_copy(u_hbm.at[b], u_ref.at[b], sems.at[b]) for b in range(nb)]
-    for load in loads:
-        load.start()
-    half = nb // 2
+    part = rank // PARTS
+    loads = []
+    for i in range(nb * PARTS):
+        at = pl.ds(i % PARTS * part, part)
+        loads.append(pltpu.make_async_copy(u_hbm.at[i // PARTS, :, at], u_ref.at[i // PARTS, :, at], sems.at[i]))
+        loads[i].start()
     used = nb * (2 * rank + 1) * 8
     acc_ref[pl.ds(used, acc_ref.shape[0] - used), :] = jnp.zeros((acc_ref.shape[0] - used, LANES), jnp.float32)
 
@@ -128,7 +133,7 @@
         at = 2 * b
         s = []
         for k in (at, at + 1):
-            if b < half:
+            if b < nb // 2:
                 s.append(own_ref[k] + b_ref[k + nb] + c_ref[k])
             else:
                 s.append(own_ref[k] + a_ref[k] + d_ref[k - nb])
@@ -136,7 +141,6 @@
         s_ref[b, 0] = s_re
         s_ref[b, 1] = s_im
         acc_ref[pl.ds((2 * nb * rank + b) * 8, 8), :] = eight(s_re * s_re + s_im * s_im)
-        loads[b].wait()
 
         def body(j, carry, b=b, s_re=s_re, s_im=s_im):
             u_re = u_ref[b, 0, j].astype(jnp.float32)
@@ -146,7 +150,9 @@
             acc_ref[pl.ds(pl.multiple_of(at + rank * 8, 8), 8), :] = eight(u_re * s_im - u_im * s_re)
             return carry
 
-        lax.fori_loop(0, rank, body, 0, unroll=4)
+        for i in range(PARTS):
+            loads[b * PARTS + i].wait()
+            lax.fori_loop(i * part, (i + 1) * part, body, 0, unroll=UNROLL)
 
     n = acc_ref.shape[0] // 8
     x = acc_ref[pl.ds(0, n, stride=8), :]
@@ -157,58 +163,42 @@
         lax.dot_general(ones, v, (((1,), (1,)), ((), ())), preferred_element_type=jnp.float32)
         for v in split3(x)
     )
-    blk = jnp.concatenate(
-        [sums[0:1, k * LANES:(k + 1) * LANES] for k in range(3)]
-        + [h_ref[...].sum(axis=0, keepdims=True)],
-        axis=0,
-    )
-    blk_ref[...] = jnp.broadcast_to(blk[None], blk_ref.shape)
-
-
-def update_kernel(parts, count_ref, g_ref, pick_ref, eig_ref, s_ref, u_hbm, out_hbm, coh_ref, coef_ref, u_ref, out_ref, in_sems, sems):
+    rows8 = [sums[0:1, k * LANES:(k + 1) * LANES] for k in range(3)] + [jnp.zeros((5, LANES), jnp.float32)]
+    all_ref[...] = jnp.concatenate(rows8 + [h_ref[...]], axis=0)
+
+
+def update_kernel(parts, count_ref, g_ref, eig_ref, s_ref, u_hbm, out_hbm, coh_ref, coef_ref, u_ref, out_ref, in_sems, sems):
     nb, _, rank, rows, _ = u_ref.shape
     loads = [pltpu.make_async_copy(u_hbm.at[b], u_ref.at[b], in_sems.at[b]) for b in range(nb)]
     for load in loads:
         load.start()
 
-    def coefficients():
-        count = jnp.full((1, 1), count_ref[0], jnp.int32).astype(jnp.float32)
-        w_old = count / (count + 1.0)
-        w_new = 1.0 / (count + 1.0)
-        pick = pick_ref[...]
-        sums = sum(jnp.dot(pick, v, preferred_element_type=jnp.float32) for v in split3(g_ref[...]))
-        g = sums[8:]
-        g_t = g.T
-        j = lax.broadcasted_iota(jnp.int32, (rank, rank), 0)
-        k = lax.broadcasted_iota(jnp.int32, (rank, rank), 1)
-        eye = j == k
-
-        def col(v):
-            return jnp.where(eye, v, 0.0).sum(axis=1, keepdims=True)
-
-        for i in range(nb):
-            at = (i % 2) * 2 * rank
-            cr = sums[i // 2:i // 2 + 1, at:at + rank]
-            ci = sums[i // 2:i // 2 + 1, at + rank:at + 2 * rank]
-            power = sums[2:3, i:i + 1]
-            a = w_old * eig_ref[i:i + 1, :]
-            cr_c, ci_c, a_c = col(cr), col(ci), col(a)
-            p = g[:, i * rank:(i + 1) * rank]
-            p_t = g_t[i * rank:(i + 1) * rank, :]
-            h_re = jnp.where(j <= k, p, p_t)
-            h_im = jnp.where(j > k, p, jnp.where(eye, 0.0, -p_t))
-            both = w_new * (a_c + a + w_new * power)
-            gram_re = a_c * a * h_re + (cr_c * cr + ci_c * ci) * both
-            gram_im = a_c * a * h_im + (ci_c * cr - cr_c * ci) * both
-            diag = jnp.where(eye, gram_re, 0.0)
-            inv_c = 1.0 / jnp.sqrt(diag.sum(axis=1, keepdims=True) + 1e-06)
-            inv_r = 1.0 / jnp.sqrt(diag.sum(axis=0, keepdims=True) + 1e-06)
-            coh_ref[i, 0] = gram_re * inv_c * inv_r
-            coh_ref[i, 1] = gram_im * inv_c * inv_r
-            for m, v in enumerate((a_c * inv_c, w_new * cr_c * inv_c, w_new * ci_c * inv_c)):
-                coef_ref[pl.ds((m * nb + i) * rank, rank), :] = jnp.broadcast_to(v, (rank, LANES))
-
-    coefficients()
+    count = jnp.full((1, 1), count_ref[0], jnp.int32).astype(jnp.float32)
+    w_old = count / (count + 1.0)
+    w_new = 1.0 / (count + 1.0)
+    sums = g_ref[...]
+    g = sums[8:]
+    j = lax.broadcasted_iota(jnp.int32, (rank, rank), 0)
+    k = lax.broadcasted_iota(jnp.int32, (rank, rank), 1)
+    eye = j == k
+
+    def col(v):
+        return jnp.where(eye, v, 0.0).sum(axis=1, keepdims=True)
+
+    kept = []
+    for i in range(nb):
+        at = (i % 2) * 2 * rank
+        cr = sums[i // 2:i // 2 + 1, at:at + rank]
+        ci = sums[i // 2:i // 2 + 1, at + rank:at + 2 * rank]
+        power = w_new * sums[2:3, i:i + 1]
+        a = w_old * eig_ref[i:i + 1, :]
+        cr_c, ci_c, a_c = col(cr), col(ci), col(a)
+        diag = a_c * a_c * col(g[:, i * rank:(i + 1) * rank]) + (cr_c * cr_c + ci_c * ci_c) * (w_new * (a_c + a_c + power))
+        inv_c = 1.0 / jnp.sqrt(diag + 1e-06)
+        for m, v in enumerate((a_c * inv_c, w_new * cr_c * inv_c, w_new * ci_c * inv_c)):
+            coef_ref[pl.ds((m * nb + i) * rank, rank), :] = jnp.broadcast_to(v, (rank, LANES))
+        kept.append((cr, ci, a, cr_c, ci_c, a_c, inv_c, power))
+
     block = rank // parts
     copies = []
     for b in range(nb):
@@ -228,22 +218,30 @@
             return carry
 
         for part in range(parts):
-            lax.fori_loop(part * block, (part + 1) * block, body, 0, unroll=4)
+            lax.fori_loop(part * block, (part + 1) * block, body, 0, unroll=UNROLL)
             at = pl.ds(part * block, block)
             copy = pltpu.make_async_copy(out_ref.at[b, :, at], out_hbm.at[b, :, at], sems.at[b * parts + part])
             copy.start()
             copies.append(copy)
+
+    g_t = g.T
+    for i, (cr, ci, a, cr_c, ci_c, a_c, inv_c, power) in enumerate(kept):
+        p = g[:, i * rank:(i + 1) * rank]
+        p_t = g_t[i * rank:(i + 1) * rank, :]
+        h_re = jnp.where(j <= k, p, p_t)
+        h_im = jnp.where(j > k, p, jnp.where(eye, 0.0, -p_t))
+        both = w_new * (a_c + a + power)
+        inv = inv_c * jnp.where(eye, inv_c, 0.0).sum(axis=0, keepdims=True)
+        coh_ref[i, 0] = (a_c * a * h_re + (cr_c * cr + ci_c * ci) * both) * inv
+        coh_ref[i, 1] = (a_c * a * h_im + (ci_c * cr - cr_c * ci) * both) * inv
     for copy in copies:
         copy.wait()
 
 
-def pick_table(rank, n_space):
-    m = np.zeros((8 + rank, n_space * BLK), np.float32)
-    for s in range(n_space):
-        for k in range(3):
-            m[k, s * BLK + k] = 1.0
-        m[8 + s * rank // n_space, s * BLK + 3] = 1.0
-    return jnp.asarray(m, jnp.bfloat16)
+def meet(v, low, high):
+    n = lax.axis_size(SPACE)
+    one, two, three = [lax.ppermute(v, SPACE, [(i, i ^ k) for i in range(n)]) for k in (low, high, low | high)]
+    return (v + one) + (two + three)
 
 
 SMEM = pl.BlockSpec(memory_space=pltpu.SMEM)
@@ -287,20 +285,20 @@
     )(u)
 
 
-def call_project(own, a, b, c, d, u, h, n_space):
+def call_project(own, a, b, c, d, u, h):
     nb, _, rank, rows, _ = u.shape
     return pl.pallas_call(
         project_kernel,
         out_shape=(
             jax.ShapeDtypeStruct((nb, 2, rows, LANES), jnp.float32),
-            jax.ShapeDtypeStruct((n_space, BLK, LANES), jnp.float32),
+            jax.ShapeDtypeStruct((8 + rank, LANES), jnp.float32),
         ),
         in_specs=[VMEM] * 5 + [HBM, VMEM],
         out_specs=(VMEM, VMEM),
         scratch_shapes=[
             pltpu.VMEM((3 * LANES * 8, LANES), jnp.float32),
             pltpu.VMEM(u.shape, u.dtype),
-            pltpu.SemaphoreType.DMA((nb,)),
+            pltpu.SemaphoreType.DMA((nb * PARTS,)),
         ],
         compiler_params=room(52000),
         cost_estimate=pl.CostEstimate(flops=16 * u.size, bytes_accessed=u.size * 2, transcendentals=0),
@@ -316,7 +314,7 @@
             jax.ShapeDtypeStruct(u.shape, jnp.bfloat16),
             jax.ShapeDtypeStruct((nb, 2, rank, rank), jnp.float32),
         ),
-        in_specs=[SMEM] + [VMEM] * 4 + [HBM],
+        in_specs=[SMEM] + [VMEM] * 3 + [HBM],
         out_specs=(HBM, VMEM),
         scratch_shapes=[
             pltpu.VMEM((3 * nb * rank, LANES), jnp.float32),
@@ -327,7 +325,7 @@
         ],
         compiler_params=room(52000),
         name="update",
-    )(block_count, g, pick_table(rank, g.shape[0] // BLK), eigenvalues, spec, u)
+    )(block_count, g, eigenvalues, spec, u)
 
 
 def local(snapshots, bins, eigenvalues, old_basis, block_count):
@@ -335,7 +333,6 @@
     groups = lax.axis_size("ta")
     total = slice_len * groups
     nb = old_basis.shape[0]
-    n_space = lax.axis_size(SPACE)
     place = lax.axis_index("ta").astype(jnp.int32).reshape(1)
 
     up, down, keep, own = call_transform(bins, place, fold(snapshots, 1), total)
@@ -347,14 +344,14 @@
     u = fold(old_basis, 3)
     u, _ = lax.optimization_barrier((u, up))
     h = call_gram(u)
+
     c, d = keep[:nb] + a[:nb], keep[nb:] + b[:nb]
     c, d, h = lax.optimization_barrier((c, d, h))
     c = lax.ppermute(c, "ta", ring_up)
     d = lax.ppermute(d, "ta", ring_down)
-    h = lax.all_to_all(h[:, None], ("y", "z"), 0, 0, tiled=True)[:, 0]
-
-    spec, blk = call_project(own, a, b, c, d, u, h, n_space)
-    g = lax.all_to_all(blk, SPACE, 0, 0, tiled=True).reshape(n_space * BLK, LANES)
+    spec, g = call_project(own, a, b, c, d, u, h)
+    for low, high in MEETINGS:
+        g = meet(g, low, high)
     fresh, coherence = call_update(block_count, g, eigenvalues, spec, u)
     return unfold(fresh, 3), coherence
 

time: 65.5 us -> 57.3 us (0.87)
  the two profiles are of different devices: /device:TPU:1 before, /device:TPU:6 now
where the time goes in v7:
time: 57.3 us; the launch traced here: 57.2 us
  starting transfers between devices  21.4 us (37%)
  waiting for transfers between devices  18.7 us (33%)
  Pallas kernels  14.9 us (26%)
  between operations  1.37 us (2%)
  local copies, waits for them, and re-layouts  0.65 us (1%)
    ppermute x9, starting transfers between devices, meet(): lax.ppermute(v, SPACE, [(i, i ^ k) for i in range(n)])  15.1 us
    ppermute x9, waiting for transfers between devices, meet(): lax.ppermute(v, SPACE, [(i, i ^ k) for i in range(n)])  10.8 us
    pallas_call x1, Pallas kernels, call_update(): pl.pallas_call(lambda *refs: update_kernel(parts, *refs), out_shape=(jax....  4.64 us
    pallas_call x1, Pallas kernels, call_gram(): pl.pallas_call(gram_kernel, out_shape=jax.ShapeDtypeStruct((rank, nb * ra...  4.27 us
    ppermute x1, waiting for transfers between devices, local(): d = lax.ppermute(d, 'ta', ring_down)  3.66 us
    ppermute x1, starting transfers between devices, local(): c = lax.ppermute(c, 'ta', ring_up)  3.03 us
    pallas_call x1, Pallas kernels, call_transform(): pl.pallas_call(lambda *refs: transform_kernel(total, chunks, *refs), out_...  3.03 us
    pallas_call x1, Pallas kernels, call_project(): pl.pallas_call(project_kernel, out_shape=(jax.ShapeDtypeStruct((nb, 2, ro...  2.98 us
  transfers between devices with their start and end apart: 13, of which 8 were waited for; matrix products, arithmetic and copies ran while one was open for 0% of the time, Pallas kernels for 7%

profile of v7, /device:TPU:6, one launch (start us, length us, event | category | flops | bytes accessed | tf_op | source)
XLA Modules:
  0.0 57.2 jit_solution(7918520182575181916)
XLA Ops:
  0.6 0.0 copy-start.1
  0.6 0.6 %copy-done.1 = s32[16]{0:T(128)S(1)} copy-done((s32[16]{0:T(128)S(1)}, s32[16]{0:T(128)}, u32[]{:S(2)}) %copy-start.1) | copy-done | bytes 88
  1.3 3.0 %transform.1 = (f32[8,64,128]{2,1,0:T(8,128)S(1)}, f32[8,64,128]{2,1,0:T(8,128)S(1)}, f32[8,64,128]{2,1,0:T(8,128)S(1)}, f32[8,64,128]{2,1,0:T(8,128)S(1)}) custom-call(s32[16]{0:T(128)S(1)} %copy-done.1, s32[1]{0:T(128)} %bitcast.refs_1_, f32[64,64,128]{2,1,0:T(8,128)} %bitcast.19), custom_call_target="tpu_custom_call" | custom-call | tf_op jit(solution)/shard_map/transform/pallas_call | solution.py:259
  4.3 0.9 %collective-permute-start.1 = (f32[8,64,128]{2,1,0:T(8,128)S(1)}, f32[8,64,128]{2,1,0:T(8,128)S(1)}, u32[]{:S(2)}, u32[]{:S(2)}) collective-permute-start(f32[8,64,128]{2,1,0:T(8,128)S(1)} %get-tuple-element.16), channel_id=1, source_target_pairs={{0,192},{64,0},{128,64},{192,128},{1,193},{65,1},{129,65},{193,129... | collective-permute-start | bytes 786440 | tf_op jit(solution)/shard_map/ppermute | solution.py:342
  5.2 2.4 %collective-permute-start = (f32[8,64,128]{2,1,0:T(8,128)S(1)}, f32[8,64,128]{2,1,0:T(8,128)S(1)}, u32[]{:S(2)}, u32[]{:S(2)}) collective-permute-start(f32[8,64,128]{2,1,0:T(8,128)S(1)} %get-tuple-element.15), channel_id=1, source_target_pairs={{0,64},{64,128},{128,192},{192,0},{1,65},{65,129},{129,193},{193,1... | collective-permute-start | bytes 786440 | tf_op jit(solution)/shard_map/ppermute | solution.py:341
  7.6 4.3 %gram.1.h_ref = f32[32,128]{1,0:T(8,128)S(1)} custom-call(bf16[4,2,32,64,128]{4,3,2,1,0:T(8,128)(2,1)} %bitcast.16), custom_call_target="tpu_custom_call" | custom-call | flops 4000000000 | bytes 4194304 | tf_op jit(solution)/shard_map/gram/pallas_call | solution.py:272
  11.9 0.0 copy-start
  11.9 1.7 %collective-permute-done.1.b_ref = f32[8,64,128]{2,1,0:T(8,128)S(1)} collective-permute-done((f32[8,64,128]{2,1,0:T(8,128)S(1)}, f32[8,64,128]{2,1,0:T(8,128)S(1)}, u32[]{:S(2)}, u32[]{:S(2)}) %collective-permute-start.1) | collective-permute-done | bytes 262176 | tf_op jit(solution)/shard_map/ppermute | solution.py:342
  13.7 0.0 collective-permute-done.a_ref
  13.7 3.0 %collective-permute-start.2 = (f32[4,64,128]{2,1,0:T(8,128)S(1)}, f32[4,64,128]{2,1,0:T(8,128)S(1)}, u32[]{:S(2)}, u32[]{:S(2)}) collective-permute-start(f32[4,64,128]{2,1,0:T(8,128)S(1)} %get-tuple-element.19), channel_id=1, source_target_pairs={{0,64},{64,128},{128,192},{192,0},{1,65},{65,129},{129,193},{193,1... | collective-permute-start | bytes 393224 | tf_op jit(solution)/shard_map/ppermute | solution.py:350
  16.7 0.0 collective-permute-start.3
  16.7 2.5 %collective-permute-done.2.c_ref = f32[4,64,128]{2,1,0:T(8,128)S(1)} collective-permute-done((f32[4,64,128]{2,1,0:T(8,128)S(1)}, f32[4,64,128]{2,1,0:T(8,128)S(1)}, u32[]{:S(2)}, u32[]{:S(2)}) %collective-permute-start.2) | collective-permute-done | bytes 131104 | tf_op jit(solution)/shard_map/ppermute | solution.py:350
  19.3 3.7 %collective-permute-done.3.d_ref = f32[4,64,128]{2,1,0:T(8,128)S(1)} collective-permute-done((f32[4,64,128]{2,1,0:T(8,128)S(1)}, f32[4,64,128]{2,1,0:T(8,128)S(1)}, u32[]{:S(2)}, u32[]{:S(2)}) %collective-permute-start.3) | collective-permute-done | bytes 131104 | tf_op jit(solution)/shard_map/ppermute | solution.py:351
  22.9 3.0 %project.1 = (f32[4,2,64,128]{3,2,1,0:T(8,128)S(1)}, f32[40,128]{1,0:T(8,128)S(1)}) custom-call(f32[8,64,128]{2,1,0:T(8,128)S(1)} %get-tuple-element.14.own_ref, f32[8,64,128]{2,1,0:T(8,128)S(1)} %collective-permute-done.a_ref, f32[8,64,128]{2,1,0:T(8,128)S(1)} %collective-permute-done.1.b_ref, f32[4,64,128]{2,1,0:T(8,128)S(1)} %collective-permute-done.2.c_ref, ...), custom_call_target="tpu_custom_call" | custom-call | flops 33554432 | bytes 4194304 | tf_op jit(solution)/shard_map/project/pallas_call | solution.py:290
  25.9 0.1 collective-permute-start.6
  26.0 2.0 %collective-permute-start.5 = (f32[40,128]{1,0:T(8,128)S(1)}, f32[40,128]{1,0:T(8,128)S(1)}, u32[]{:S(2)}, u32[]{:S(2)}) collective-permute-start(f32[40,128]{1,0:T(8,128)S(1)} %get-tuple-element.22), channel_id=1, source_target_pairs={{0,2},{1,3},{2,0},{3,1},{4,6},{5,7},{6,4},{7,5},{8,10},{9,11},{10,... | collective-permute-start | bytes 61448 | tf_op jit(solution)/shard_map/ppermute | solution.py:243
  28.0 0.0 collective-permute-start.4
  28.0 1.2 %collective-permute-done.6 = f32[40,128]{1,0:T(8,128)S(1)} collective-permute-done((f32[40,128]{1,0:T(8,128)S(1)}, f32[40,128]{1,0:T(8,128)S(1)}, u32[]{:S(2)}, u32[]{:S(2)}) %collective-permute-start.6) | collective-permute-done | bytes 20512 | tf_op jit(solution)/shard_map/ppermute | solution.py:243
  29.2 0.7 %collective-permute-done.5 = f32[40,128]{1,0:T(8,128)S(1)} collective-permute-done((f32[40,128]{1,0:T(8,128)S(1)}, f32[40,128]{1,0:T(8,128)S(1)}, u32[]{:S(2)}, u32[]{:S(2)}) %collective-permute-start.5) | collective-permute-done | bytes 20512 | tf_op jit(solution)/shard_map/ppermute | solution.py:243
  29.9 0.0 collective-permute-done.4
  29.9 3.1 %collective-permute-start.9 = (f32[40,128]{1,0:T(8,128)S(1)}, f32[40,128]{1,0:T(8,128)S(1)}, u32[]{:S(2)}, u32[]{:S(2)}) collective-permute-start(f32[40,128]{1,0:T(8,128)S(1)} %add_add_fusion.2), channel_id=1, source_target_pairs={{0,48},{1,49},{2,50},{3,51},{4,52},{5,53},{6,54},{7,55},{8,56},{9,... | collective-permute-start | bytes 61448 | tf_op jit(solution)/shard_map/ppermute | solution.py:243
  33.0 0.6 %collective-permute-start.8 = (f32[40,128]{1,0:T(8,128)S(1)}, f32[40,128]{1,0:T(8,128)S(1)}, u32[]{:S(2)}, u32[]{:S(2)}) collective-permute-start(f32[40,128]{1,0:T(8,128)S(1)} %add_add_fusion.2), channel_id=1, source_target_pairs={{0,32},{1,33},{2,34},{3,35},{4,36},{5,37},{6,38},{7,39},{8,40},{9,... | collective-permute-start | bytes 61448 | tf_op jit(solution)/shard_map/ppermute | solution.py:243
  33.6 0.5 collective-permute-start.7
  34.1 1.0 %collective-permute-done.9 = f32[40,128]{1,0:T(8,128)S(1)} collective-permute-done((f32[40,128]{1,0:T(8,128)S(1)}, f32[40,128]{1,0:T(8,128)S(1)}, u32[]{:S(2)}, u32[]{:S(2)}) %collective-permute-start.9) | collective-permute-done | bytes 20512 | tf_op jit(solution)/shard_map/ppermute | solution.py:243
  35.1 3.4 %collective-permute-done.8 = f32[40,128]{1,0:T(8,128)S(1)} collective-permute-done((f32[40,128]{1,0:T(8,128)S(1)}, f32[40,128]{1,0:T(8,128)S(1)}, u32[]{:S(2)}, u32[]{:S(2)}) %collective-permute-start.8) | collective-permute-done | bytes 20512 | tf_op jit(solution)/shard_map/ppermute | solution.py:243
  38.5 0.0 collective-permute-done.7
  38.5 6.3 %collective-permute-start.12 = (f32[40,128]{1,0:T(8,128)S(1)}, f32[40,128]{1,0:T(8,128)S(1)}, u32[]{:S(2)}, u32[]{:S(2)}) collective-permute-start(f32[40,128]{1,0:T(8,128)S(1)} %add_add_fusion.1), channel_id=1, source_target_pairs={{0,12},{1,13},{2,14},{3,15},{4,8},{5,9},{6,10},{7,11},{8,4},{9,5},... | collective-permute-start | bytes 61448 | tf_op jit(solution)/shard_map/ppermute | solution.py:243
  44.8 1.0 %collective-permute-start.11 = (f32[40,128]{1,0:T(8,128)S(1)}, f32[40,128]{1,0:T(8,128)S(1)}, u32[]{:S(2)}, u32[]{:S(2)}) collective-permute-start(f32[40,128]{1,0:T(8,128)S(1)} %add_add_fusion.1), channel_id=1, source_target_pairs={{0,8},{1,9},{2,10},{3,11},{4,12},{5,13},{6,14},{7,15},{8,0},{9,1},... | collective-permute-start | bytes 61448 | tf_op jit(solution)/shard_map/ppermute | solution.py:243
  45.8 1.5 %collective-permute-start.10 = (f32[40,128]{1,0:T(8,128)S(1)}, f32[40,128]{1,0:T(8,128)S(1)}, u32[]{:S(2)}, u32[]{:S(2)}) collective-permute-start(f32[40,128]{1,0:T(8,128)S(1)} %add_add_fusion.1), channel_id=1, source_target_pairs={{0,4},{1,5},{2,6},{3,7},{4,0},{5,1},{6,2},{7,3},{8,12},{9,13},{10,... | collective-permute-start | bytes 61448 | tf_op jit(solution)/shard_map/ppermute | solution.py:243
  47.9 0.0 collective-permute-done.12
  47.9 4.6 %collective-permute-done.11 = f32[40,128]{1,0:T(8,128)S(1)} collective-permute-done((f32[40,128]{1,0:T(8,128)S(1)}, f32[40,128]{1,0:T(8,128)S(1)}, u32[]{:S(2)}, u32[]{:S(2)}) %collective-permute-start.11) | collective-permute-done | bytes 20512 | tf_op jit(solution)/shard_map/ppermute | solution.py:243
  52.5 0.0 collective-permute-done.10
  52.5 0.0 copy-done
  52.5 4.6 %update.1 = (bf16[4,2,32,64,128]{4,3,2,1,0:T(8,128)(2,1)}, f32[4,2,32,32]{3,2,1,0:T(8,128)}) custom-call(s32[1]{0:T(128)S(6)} %copy.10.refs_0_, f32[40,128]{1,0:T(8,128)S(1)} %add_add_fusion.refs_1_, f32[4,32]{1,0:T(4,128)S(1)} %copy-done, f32[4,2,64,128]{3,2,1,0:T(8,128)S(1)} %get-tuple-element.23.refs_3_, bf16[4,2,32,64,128]{4,3,2,1,0:T(8,128)(2,1)} %bitcast.18), custom_call_target="tpu_custom_call" | custom-call | tf_op jit(solution)/shard_map/update/pallas_call | solution.py:311
  (4 shorter events, 0.1 us)
Async XLA Ops:
  0.6 0.7 %copy-start.1 = (s32[16]{0:T(128)S(1)}, s32[16]{0:T(128)}, u32[]{:S(2)}) copy-start(s32[16]{0:T(128)} %refs_0_.2) | copy-start | bytes 196
  4.3 9.3 %collective-permute-start.1 = (f32[8,64,128]{2,1,0:T(8,128)S(1)}, f32[8,64,128]{2,1,0:T(8,128)S(1)}, u32[]{:S(2)}, u32[]{:S(2)}) collective-permute-start(f32[8,64,128]{2,1,0:T(8,128)S(1)} %get-tuple-element.16), channel_id=1, source_target_pairs={{0,192},{64,0},{128,64},{192,128},{1,193},{65,1},{129,65},{193,129... | collective-permute-start | bytes 786440 | tf_op jit(solution)/shard_map/ppermute | solution.py:342
  5.2 8.4 %collective-permute-start = (f32[8,64,128]{2,1,0:T(8,128)S(1)}, f32[8,64,128]{2,1,0:T(8,128)S(1)}, u32[]{:S(2)}, u32[]{:S(2)}) collective-permute-start(f32[8,64,128]{2,1,0:T(8,128)S(1)} %get-tuple-element.15), channel_id=1, source_target_pairs={{0,64},{64,128},{128,192},{192,0},{1,65},{65,129},{129,193},{193,1... | collective-permute-start | bytes 786440 | tf_op jit(solution)/shard_map/ppermute | solution.py:341
  11.9 40.6 %copy-start = (f32[4,32]{1,0:T(4,128)S(1)}, f32[4,32]{1,0:T(4,128)}, u32[]{:S(2)}) copy-start(f32[4,32]{1,0:T(4,128)} %refs_2_.1) | copy-start | bytes 1540
  13.7 5.6 %collective-permute-start.2 = (f32[4,64,128]{2,1,0:T(8,128)S(1)}, f32[4,64,128]{2,1,0:T(8,128)S(1)}, u32[]{:S(2)}, u32[]{:S(2)}) collective-permute-start(f32[4,64,128]{2,1,0:T(8,128)S(1)} %get-tuple-element.19), channel_id=1, source_target_pairs={{0,64},{64,128},{128,192},{192,0},{1,65},{65,129},{129,193},{193,1... | collective-permute-start | bytes 393224 | tf_op jit(solution)/shard_map/ppermute | solution.py:350
  16.7 6.2 %collective-permute-start.3 = (f32[4,64,128]{2,1,0:T(8,128)S(1)}, f32[4,64,128]{2,1,0:T(8,128)S(1)}, u32[]{:S(2)}, u32[]{:S(2)}) collective-permute-start(f32[4,64,128]{2,1,0:T(8,128)S(1)} %get-tuple-element.20), channel_id=1, source_target_pairs={{0,192},{64,0},{128,64},{192,128},{1,193},{65,1},{129,65},{193,129... | collective-permute-start | bytes 393224 | tf_op jit(solution)/shard_map/ppermute | solution.py:351
  25.9 3.3 %collective-permute-start.6 = (f32[40,128]{1,0:T(8,128)S(1)}, f32[40,128]{1,0:T(8,128)S(1)}, u32[]{:S(2)}, u32[]{:S(2)}) collective-permute-start(f32[40,128]{1,0:T(8,128)S(1)} %get-tuple-element.22), channel_id=1, source_target_pairs={{0,3},{1,2},{2,1},{3,0},{4,7},{5,6},{6,5},{7,4},{8,11},{9,10},{10,... | collective-permute-start | bytes 61448 | tf_op jit(solution)/shard_map/ppermute | solution.py:243
  26.0 3.9 %collective-permute-start.5 = (f32[40,128]{1,0:T(8,128)S(1)}, f32[40,128]{1,0:T(8,128)S(1)}, u32[]{:S(2)}, u32[]{:S(2)}) collective-permute-start(f32[40,128]{1,0:T(8,128)S(1)} %get-tuple-element.22), channel_id=1, source_target_pairs={{0,2},{1,3},{2,0},{3,1},{4,6},{5,7},{6,4},{7,5},{8,10},{9,11},{10,... | collective-permute-start | bytes 61448 | tf_op jit(solution)/shard_map/ppermute | solution.py:243
  28.0 1.9 %collective-permute-start.4 = (f32[40,128]{1,0:T(8,128)S(1)}, f32[40,128]{1,0:T(8,128)S(1)}, u32[]{:S(2)}, u32[]{:S(2)}) collective-permute-start(f32[40,128]{1,0:T(8,128)S(1)} %get-tuple-element.22), channel_id=1, source_target_pairs={{0,1},{1,0},{2,3},{3,2},{4,5},{5,4},{6,7},{7,6},{8,9},{9,8},{10,11... | collective-permute-start | bytes 61448 | tf_op jit(solution)/shard_map/ppermute | solution.py:243
  29.9 5.2 %collective-permute-start.9 = (f32[40,128]{1,0:T(8,128)S(1)}, f32[40,128]{1,0:T(8,128)S(1)}, u32[]{:S(2)}, u32[]{:S(2)}) collective-permute-start(f32[40,128]{1,0:T(8,128)S(1)} %add_add_fusion.2), channel_id=1, source_target_pairs={{0,48},{1,49},{2,50},{3,51},{4,52},{5,53},{6,54},{7,55},{8,56},{9,... | collective-permute-start | bytes 61448 | tf_op jit(solution)/shard_map/ppermute | solution.py:243
  33.0 5.5 %collective-permute-start.8 = (f32[40,128]{1,0:T(8,128)S(1)}, f32[40,128]{1,0:T(8,128)S(1)}, u32[]{:S(2)}, u32[]{:S(2)}) collective-permute-start(f32[40,128]{1,0:T(8,128)S(1)} %add_add_fusion.2), channel_id=1, source_target_pairs={{0,32},{1,33},{2,34},{3,35},{4,36},{5,37},{6,38},{7,39},{8,40},{9,... | collective-permute-start | bytes 61448 | tf_op jit(solution)/shard_map/ppermute | solution.py:243
  33.6 4.9 %collective-permute-start.7 = (f32[40,128]{1,0:T(8,128)S(1)}, f32[40,128]{1,0:T(8,128)S(1)}, u32[]{:S(2)}, u32[]{:S(2)}) collective-permute-start(f32[40,128]{1,0:T(8,128)S(1)} %add_add_fusion.2), channel_id=1, source_target_pairs={{0,16},{1,17},{2,18},{3,19},{4,20},{5,21},{6,22},{7,23},{8,24},{9,... | collective-permute-start | bytes 61448 | tf_op jit(solution)/shard_map/ppermute | solution.py:243
  38.5 9.4 %collective-permute-start.12 = (f32[40,128]{1,0:T(8,128)S(1)}, f32[40,128]{1,0:T(8,128)S(1)}, u32[]{:S(2)}, u32[]{:S(2)}) collective-permute-start(f32[40,128]{1,0:T(8,128)S(1)} %add_add_fusion.1), channel_id=1, source_target_pairs={{0,12},{1,13},{2,14},{3,15},{4,8},{5,9},{6,10},{7,11},{8,4},{9,5},... | collective-permute-start | bytes 61448 | tf_op jit(solution)/shard_map/ppermute | solution.py:243
  44.8 7.7 %collective-permute-start.11 = (f32[40,128]{1,0:T(8,128)S(1)}, f32[40,128]{1,0:T(8,128)S(1)}, u32[]{:S(2)}, u32[]{:S(2)}) collective-permute-start(f32[40,128]{1,0:T(8,128)S(1)} %add_add_fusion.1), channel_id=1, source_target_pairs={{0,8},{1,9},{2,10},{3,11},{4,12},{5,13},{6,14},{7,15},{8,0},{9,1},... | collective-permute-start | bytes 61448 | tf_op jit(solution)/shard_map/ppermute | solution.py:243
  45.8 6.7 %collective-permute-start.10 = (f32[40,128]{1,0:T(8,128)S(1)}, f32[40,128]{1,0:T(8,128)S(1)}, u32[]{:S(2)}, u32[]{:S(2)}) collective-permute-start(f32[40,128]{1,0:T(8,128)S(1)} %add_add_fusion.1), channel_id=1, source_target_pairs={{0,4},{1,5},{2,6},{3,7},{4,0},{5,1},{6,2},{7,3},{8,12},{9,13},{10,... | collective-permute-start | bytes 61448 | tf_op jit(solution)/shard_map/ppermute | solution.py:243
